TPU v7x, 32 devices: a whole 2x2x4 slice. The times are simulated.
32 devices in a mesh: dom: 16 (over z, x, core), col: 2 (over y).
Axes of the slice: x: 2, y: 2, z: 4, core: 2. Of those that a mesh axis runs over, the one named last changes fastest.
Arguments:
- snapshots: bfloat16 [128, 3, 32768], P('col', None, 'dom'), may hold values from -30 to 30
- mass_tiles: bfloat16 [16, 3, 3, 32768], P(None, None, None, 'dom'), may hold values from -2 to 2
- tile_slot: int32 [15, 32768], P(None, 'dom'), may hold values from 0 to 3071
- send_up: int32 [8192], P('dom'), may hold values from 0 to 2047
- send_down: int32 [8192], P('dom'), may hold values from 0 to 2047
Outputs:
- mass_snap: bfloat16 [128, 3, 32768], P('col', None, 'dom')
- gram: float32 [128, 128], P(None, 'col')
Inputs may be any that keep to these rules, and one draw needn't show every extreme that they name: `tile_slot`: slots below 2048 are the partition's own nodes, the next 512 those received from the previous partition, the last 512 those from the next partition.
All inputs are finite; a program needn't handle non-finite values.
Results may differ from a plain program's by a relative error of at most 0.001.
Values may be sent and summed in bfloat16 or wider, within the bound.
No kernel may reach another device: no remote copies, remote signals or barrier semaphores. Data moves between devices by JAX's collectives and lax.ppermute only.
A program may use at most 64 MiB of HBM per device.

v0:
```python
import jax
import jax.numpy as jnp
from jax import lax
from jax.sharding import PartitionSpec as P


def shifted(value, axis, steps):
    count = lax.axis_size(axis)
    leading, last = (max(0, -steps), min(count, count - steps))
    return lax.ppermute(value, axis, [(source, source + steps) for source in range(leading, last)])


def couple(tiles, values):
    total_sum = tiles[None, :, 0, :].astype(jnp.float32) * values[:, None, 0, :].astype(jnp.float32)
    for in_comp in (1, 2):
        total_sum = total_sum + tiles[None, :, in_comp, :].astype(jnp.float32) * values[
            :, None, in_comp, :
        ].astype(jnp.float32)
    return total_sum


def apply_mass(local_snap, flat_ext, mass_tiles, tile_slot):
    snap_count = local_snap.shape[0]
    node_count = local_snap.shape[2]
    others = tile_slot.shape[0]
    total_sum = couple(mass_tiles[0], local_snap)
    gathered = jnp.take(flat_ext, tile_slot.reshape(-1), axis=1)
    gathered = gathered.reshape(snap_count, 3, others, node_count)
    for in_comp in (0, 1, 2):
        tile_part = jnp.transpose(mass_tiles[1:, :, in_comp, :], (1, 0, 2)).astype(jnp.float32)
        values = gathered[:, in_comp].astype(jnp.float32)
        total_sum = total_sum + jnp.sum(tile_part[None] * values[:, None], axis=2)
    return total_sum.astype(jnp.bfloat16)


def inner_products(left_rows, right_rows):
    left_flat = left_rows.reshape(left_rows.shape[0], -1)
    right_flat = right_rows.reshape(right_rows.shape[0], -1)
    return lax.dot_general(
        left_flat, right_flat, (((1,), (1,)), ((), ())), preferred_element_type=jnp.float32
    )


def body(snapshots, mass_tiles, tile_slot, send_up, send_down):
    snap_count = snapshots.shape[0]
    flat_local = snapshots.reshape(snap_count * 3, -1)
    to_upper = jnp.take(flat_local, send_up, axis=1)
    to_lower = jnp.take(flat_local, send_down, axis=1)
    from_lower = shifted(to_upper, "dom", 1)
    from_upper = shifted(to_lower, "dom", -1)
    flat_ext = jnp.concatenate([flat_local, from_lower, from_upper], axis=1)
    mass_snap = apply_mass(snapshots, flat_ext, mass_tiles, tile_slot)
    block_terms = inner_products(lax.all_gather(snapshots, "col", axis=0, tiled=True), mass_snap)
    summed_gram = lax.psum(block_terms, "dom")
    node_total = 3.0 * snapshots.shape[2] * lax.axis_size("dom")
    gram = summed_gram / node_total
    return (mass_snap, gram)


def solution(mesh):
    placed = (P("col", None, "dom"), P(None, None, None, "dom"), P(None, "dom"), P("dom"), P("dom"))
    return jax.shard_map(
        body,
        mesh=mesh,
        in_specs=placed,
        out_specs=(P("col", None, "dom"), P(None, "col")),
        check_vma=False,
    )
```

profile of v0, /device:TPU:0, one launch (start us, length us, event | category | flops | bytes accessed | tf_op | source)
XLA Modules:
  0.0 300.8 jit_solution(1382220188660814233)
XLA Ops:
  7.2 0.0 all-gather.2.cloned.1.call-start
  7.2 0.7 all-gather.2.cloned.1.call-update
  7.9 1.8 copy.30
  9.7 0.7 compare_select_fusion.3
  10.4 0.7 compare_and_fusion.2
  11.1 0.7 reshape.93
  11.8 0.5 copy.33
  12.3 2.0 gather_fusion.1
  14.3 0.8 select_bitcast_fusion.1
  15.2 2.4 collective-permute-start
  17.6 2.0 gather_fusion.2
  19.6 0.1 select_bitcast_fusion
  19.7 1.5 collective-permute-start.1
  21.2 1.1 convert_bitcast_fusion.2
  22.3 1.2 bitcast_convert_fusion.2
  23.6 0.1 copy.40
  23.8 0.1 compare_select_fusion
  24.0 0.1 slice_convert_fusion.2
  24.1 0.7 copy-done.10
  24.8 0.4 collective-permute-done.1
  25.2 1.2 pad_maximum_fusion
  26.5 120.6 %gather_fusion = bf16[30720,192]{1,0:T(8,128)(2,1)} fusion(bf16[192,3072]{0,1:T(8,128)(2,1)S(1)} %pad_maximum_fusion, s32[30720]{0:T(1024)S(1)} %broadcast_clamp_fusion), kind=kCustom, calls=%fused_computation.2 | custom fusion | bytes 23715840 | tf_op jit(solution)/shard_map/jit(_take)/gather | solution.py:27
  147.1 18.1 %copy.34 = bf16[192,30720]{1,0:T(8,128)(2,1)} copy(bf16[192,30720]{0,1:T(8,128)(2,1)} %bitcast.65) | data formatting | bytes 23592960 | tf_op jit(solution)/shard_map/jit(_take)/gather | solution.py:27
  165.1 17.4 %gather.10 = bf16[64,3,15,2048]{3,2,1,0:T(8,128)(2,1)} reshape(bf16[192,30720]{1,0:T(8,128)(2,1)} %copy.34) | data formatting | bytes 23592960 | tf_op jit(solution)/shard_map/jit(_take)/gather | solution.py:27
  182.6 21.2 %copy_select_fusion = bf16[64,3,15,2048]{3,0,2,1:T(8,128)(2,1)S(1)} fusion(bf16[64,3,15,2048]{3,2,1,0:T(8,128)(2,1)} %gather.10, pred[15,2048]{1,0:T(8,128)(4,1)S(1)} %compare_and_fusion), kind=kLoop, calls=%fused_computation.6 | loop fusion | flops 5898240 | bytes 23623680 | tf_op jit(solution)/shard_map/jit(_take)/select_n | solution.py:27
  203.8 9.2 %fusion.2 = (f32[64,15,2048]{2,0,1:T(8,128)}, f32[64,15,2048]{2,0,1:T(8,128)}, f32[64,15,2048]{2,0,1:T(8,128)}) fusion(bf16[64,3,15,2048]{3,0,2,1:T(8,128)(2,1)S(1)} %copy_select_fusion), kind=kLoop, calls=%fused_computation.12 | loop fusion | flops 5898240 | bytes 35389440 | tf_op jit(solution)/shard_map/mul | solution.py:32
  213.0 5.1 %multiply_reduce_fusion.2 = f32[64,3,2048]{2,0,1:T(8,128)S(1)} fusion(f32[64,15,2048]{2,0,1:T(8,128)} %get-tuple-element.3, f32[3,15,2048]{2,1,0:T(8,128)S(1)} %copy-done.5), kind=kLoop, calls=%fused_computation.5 | loop fusion | flops 11403264 | bytes 9805824 | tf_op jit(solution)/shard_map/reduce_sum | solution.py:32
  218.2 8.7 %multiply_reduce_fusion = (f32[64,3,2048]{2,0,1:T(8,128)S(1)}, f32[64,3,2048]{2,0,1:T(8,128)S(1)}) fusion(f32[64,15,2048]{2,0,1:T(8,128)} %get-tuple-element.4, f32[3,15,2048]{2,1,0:T(8,128)S(1)} %copy-done.6, f32[64,15,2048]{2,0,1:T(8,128)} %get-tuple-element.5, f32[3,15,2048]{2,1,0:T(8,128)S(1)} %copy-done.7), kind=kLoop, calls=%fused_computation.3 | loop fusion | flops 22806528 | bytes 19611648 | tf_op jit(solution)/shard_map/reduce_sum | solution.py:32
  226.9 0.7 add_convert_fusion
  227.6 2.3 convolution_bitcast_fusion
  230.0 63.3 %psum.7 = f32[128,64]{0,1:T(8,128)S(1)} all-reduce(f32[128,64]{0,1:T(8,128)S(1)} %convolution_bitcast_fusion), channel_id=1, replica_groups=mesh['dom'=16,'col'=2] {'dom'}, use_global_device_ids=true, to_apply=%region_3.5 | all-reduce | flops 8192 | bytes 65536 | tf_op jit(solution)/shard_map/psum | solution.py:54
  293.3 0.6 broadcast_multiply_fusion
  (35 shorter events, 0.3 us)
Async XLA Ops:
  7.2 220.5 %all-gather.2.cloned.1.call-start = ((), (), s32[]{:S(2)}) async-start(), calls=%async_computation | async-start | bytes 2359296 | tf_op jit(solution)/shard_map/all_gather | solution.py:53
  9.7 7.9 %copy-start.11 = (s32[512]{0:T(512)S(1)}, s32[512]{0:T(512)}, u32[]{:S(2)}) copy-start(s32[512]{0:T(512)} %param.11) | copy-start | bytes 6148
  11.8 9.4 %copy-start.8 = (bf16[16,3,3,2048]{3,0,2,1:T(8,128)(2,1)S(1)}, bf16[16,3,3,2048]{3,0,2,1:T(8,128)(2,1)}, u32[]{:S(2)}) copy-start(bf16[16,3,3,2048]{3,0,2,1:T(8,128)(2,1)} %param.8) | copy-start | bytes 1769476
  12.3 10.0 %copy-start = (bf16[64,3,2048]{2,0,1:T(8,128)(2,1)S(1)}, bf16[64,3,2048]{2,0,1:T(8,128)(2,1)}, u32[]{:S(2)}) copy-start(bf16[64,3,2048]{2,0,1:T(8,128)(2,1)} %param.7) | copy-start | bytes 2359300
  15.2 8.9 %collective-permute-start = (bf16[192,512]{0,1:T(8,128)(2,1)}, bf16[192,512]{0,1:T(8,128)(2,1)S(1)}, u32[]{:S(2)}, u32[]{:S(2)}) collective-permute-start(bf16[192,512]{0,1:T(8,128)(2,1)} %select_bitcast_fusion.1), channel_id=1, source_target_pairs={{0,2},{2,4},{4,6},{6,8},{8,10},{10,12},{12,14},{14,16},{16,18},{18... | collective-permute-start | bytes 589832 | tf_op jit(solution)/shard_map/ppermute | solution.py:10
  17.6 6.0 %copy-start.9 = (s32[15,2048]{1,0:T(8,128)S(1)}, s32[15,2048]{1,0:T(8,128)}, u32[]{:S(2)}) copy-start(s32[15,2048]{1,0:T(8,128)} %param.9) | copy-start | bytes 368644
  19.7 5.5 %collective-permute-start.1 = (bf16[192,512]{0,1:T(8,128)(2,1)S(1)}, bf16[192,512]{0,1:T(8,128)(2,1)S(1)}, u32[]{:S(2)}, u32[]{:S(2)}) collective-permute-start(bf16[192,512]{0,1:T(8,128)(2,1)S(1)} %select_bitcast_fusion), channel_id=1, source_target_pairs={{2,0},{4,2},{6,4},{8,6},{10,8},{12,10},{14,12},{16,14},{18,16},{20... | collective-permute-start | bytes 589832 | tf_op jit(solution)/shard_map/ppermute | solution.py:10
  24.1 0.7 copy-start.10
  203.8 9.2 %copy-start.5 = (f32[3,15,2048]{2,1,0:T(8,128)S(1)}, f32[3,15,2048]{2,1,0:T(8,128)}, u32[]{:S(2)}) copy-start(f32[3,15,2048]{2,1,0:T(8,128)} %get-tuple-element.9) | copy-start | bytes 1105924
  213.0 5.1 %copy-start.6 = (f32[3,15,2048]{2,1,0:T(8,128)S(1)}, f32[3,15,2048]{2,1,0:T(8,128)}, u32[]{:S(2)}) copy-start(f32[3,15,2048]{2,1,0:T(8,128)} %get-tuple-element.10) | copy-start | bytes 1105924
  213.0 5.1 %copy-start.7 = (f32[3,15,2048]{2,1,0:T(8,128)S(1)}, f32[3,15,2048]{2,1,0:T(8,128)}, u32[]{:S(2)}) copy-start(f32[3,15,2048]{2,1,0:T(8,128)} %get-tuple-element.11) | copy-start | bytes 1105924
  218.1 8.7 %copy-start.2 = (f32[64,2048]{1,0:T(8,128)S(1)}, f32[64,2048]{1,0:T(8,128)}, u32[]{:S(2)}) copy-start(f32[64,2048]{1,0:T(8,128)} %get-tuple-element.6) | copy-start | bytes 1572868
  218.1 8.7 %copy-start.3 = (f32[64,2048]{1,0:T(8,128)S(1)}, f32[64,2048]{1,0:T(8,128)}, u32[]{:S(2)}) copy-start(f32[64,2048]{1,0:T(8,128)} %get-tuple-element.7) | copy-start | bytes 1572868
  218.1 8.7 %copy-start.4 = (f32[64,2048]{1,0:T(8,128)S(1)}, f32[64,2048]{1,0:T(8,128)}, u32[]{:S(2)}) copy-start(f32[64,2048]{1,0:T(8,128)} %get-tuple-element.8) | copy-start | bytes 1572868
  227.6 66.3 %copy-start.1 = (bf16[64,3,2048]{2,0,1:T(8,128)(2,1)}, bf16[64,3,2048]{2,0,1:T(8,128)(2,1)S(1)}, u32[]{:S(2)}) copy-start(bf16[64,3,2048]{2,0,1:T(8,128)(2,1)S(1)} %add_convert_fusion) | copy-start | bytes 2359300
Sparse Core Ops, SparseCore 0:
  9.5 29.8 all-gather.1
where the time goes:
time: 302 us; the launch traced here: 301 us
  local copies, waits for them, and re-layouts  164 us (54%)
  blocking collectives  63.3 us (21%)
  other arithmetic  51.7 us (17%)
  between operations  14.4 us (5%)
  starting transfers between devices  3.91 us (1%)
    gather x3, local copies, waits for them, and re-layouts, apply_mass(): gathered = jnp.take(flat_ext, tile_slot.reshape(-1), axis=1)  156 us
    psum x1, blocking collectives, body(): summed_gram = lax.psum(block_terms, 'dom')  63.3 us
    select_n x2, other arithmetic, apply_mass(): gathered = jnp.take(flat_ext, tile_slot.reshape(-1), axis=1)  21.3 us
    reduce_sum x2, other arithmetic, apply_mass(): total_sum = total_sum + jnp.sum(tile_part[None] * values[:, None], axis=2)  13.8 us
    mul x1, other arithmetic, apply_mass(): total_sum = total_sum + jnp.sum(tile_part[None] * values[:, None], axis=2)  9.23 us
  transfers between devices with their start and end apart: 3, of which 1 were waited for; matrix products, arithmetic and copies ran while one was open for 71% of the time, Pallas kernels for 0%

commit v1 on v0

v1 whole, which is shorter than its diff:
```python
import functools

import jax
import jax.numpy as jnp
import numpy as np
from jax import lax
from jax.experimental import pallas as pl
from jax.experimental.pallas import tpu as pltpu
from jax.sharding import PartitionSpec as P

LANES = 128
HALF = LANES // 2
GROUP = 8
BF16 = jnp.bfloat16
F32 = jnp.float32


def shifted(value, axis, steps):
    count = lax.axis_size(axis)
    leading, last = (max(0, -steps), min(count, count - steps))
    return lax.ppermute(value, axis, [(source, source + steps) for source in range(leading, last)])


def nt_dot(left, right):
    return lax.dot_general(left, right, (((1,), (1,)), ((), ())), preferred_element_type=F32)


def table_kernel(snap_ref, up_ref, down_ref, table_ref, to_upper_ref, to_lower_ref):
    node_count = snap_ref.shape[2]
    row = lax.broadcasted_iota(jnp.int32, (2 * LANES, 2 * LANES), 0)
    col = lax.broadcasted_iota(jnp.int32, (2 * LANES, 2 * LANES), 1)
    pick = jnp.where(col == (row // 2) + LANES * (row % 2), 1.0, 0.0).astype(BF16)
    empty = jnp.zeros((HALF, LANES), BF16)
    for start in range(0, node_count, LANES):
        comps = [snap_ref[:, comp, start : start + LANES] for comp in range(3)]
        first = jnp.concatenate([comps[0], comps[2]], axis=0)
        second = jnp.concatenate([comps[1], empty], axis=0)
        rows = nt_dot(pick, jnp.concatenate([first, second], axis=1)).astype(BF16)
        table_ref[start : start + LANES] = rows.reshape(LANES, 2, LANES)
    for out_ref, list_ref in ((to_upper_ref, up_ref), (to_lower_ref, down_ref)):
        for entry in range(out_ref.shape[0]):
            out_ref[entry] = table_ref[list_ref[entry]]


def node_table(snap, send_up, send_down):
    node_count = snap.shape[2]
    halo = send_up.shape[0]
    smem = pl.BlockSpec(memory_space=pltpu.SMEM)
    vmem = pl.BlockSpec(memory_space=pltpu.VMEM)
    return pl.pallas_call(
        table_kernel,
        in_specs=[vmem, smem, smem],
        out_specs=[vmem] * 3,
        out_shape=[
            jax.ShapeDtypeStruct((node_count, 2, LANES), BF16),
            jax.ShapeDtypeStruct((halo, 2, LANES), BF16),
            jax.ShapeDtypeStruct((halo, 2, LANES), BF16),
        ],
        name="node_table",
    )(snap, send_up, send_down)


def spread_matrix(tiles):
    spread = np.zeros((tiles, 3, 3, 2, 3, tiles, GROUP, 2), np.float32)
    for tile in range(tiles):
        for comp in range(3):
            for half, pair, in_comp in ((0, 0, 0), (0, 1, 1), (1, 0, 2)):
                spread[tile, comp, in_comp, half, comp, tile, :, pair] = 1.0
    return jnp.asarray(spread.reshape(tiles * 9, 6 * tiles * GROUP * 2), BF16)


def spread_kernel(tile_ref, spread_ref, out_ref):
    depth = out_ref.shape[2]
    turned = tile_ref[...].astype(F32).T.astype(BF16)
    node = lax.broadcasted_iota(jnp.int32, (GROUP, depth), 0)
    slot = (lax.broadcasted_iota(jnp.int32, (GROUP, depth), 1) // 2) % GROUP
    own = node == slot
    for pair in range(3):
        both = [
            jnp.dot(turned, spread_ref[:, (2 * pair + one) * depth : (2 * pair + one + 1) * depth], preferred_element_type=F32)
            for one in range(2)
        ]
        for group in range(out_ref.shape[0]):
            kept = [jnp.where(own, part[group * GROUP : (group + 1) * GROUP], 0.0) for part in both]
            out_ref[group, 16 * pair : 16 * (pair + 1), :] = jnp.concatenate(kept, axis=0).astype(BF16)


def spread_tiles(mass_tiles):
    tiles, _, _, node_count = mass_tiles.shape
    depth = tiles * GROUP * 2
    step = LANES
    spread = spread_matrix(tiles)
    return pl.pallas_call(
        spread_kernel,
        grid=(node_count // step,),
        in_specs=[
            pl.BlockSpec((tiles * 9, step), lambda i: (0, i)),
            pl.BlockSpec(spread.shape, lambda i: (0, 0)),
        ],
        out_specs=pl.BlockSpec((step // GROUP, 48, depth), lambda i: (i, 0, 0)),
        out_shape=jax.ShapeDtypeStruct((node_count // GROUP, 48, depth), BF16),
        cost_estimate=pl.CostEstimate(flops=2 * node_count * tiles * 9 * 6 * depth, bytes_accessed=node_count * 6 * depth * 2, transcendentals=0),
        name="spread_tiles",
    )(mass_tiles.reshape(tiles * 9, node_count), spread)


def mass_kernel(slot_hbm, table_hbm, lower_hbm, upper_hbm, left_ref, out_ref, slots0, slots1, table_ref, turn_ref, sem, fill_sem):
    step, steps = pl.program_id(0), pl.num_programs(0)
    others = slot_hbm.shape[0]
    nodes, halo = table_hbm.shape[0], lower_hbm.shape[0]
    low_half = lax.broadcasted_iota(jnp.int32, (GROUP, LANES), 1) < HALF
    slot_refs = (slots0, slots1)

    def fetch(block, part):
        source = slot_hbm.at[:, pl.ds(pl.multiple_of(block * LANES, LANES), LANES)]
        return pltpu.make_async_copy(source, slot_refs[part], sem.at[part])

    @pl.when(step == 0)
    def _():
        fetch(0, 0).start()
        fetch(1, 1).start()
        fills = [
            pltpu.make_async_copy(table_hbm, table_ref.at[pl.ds(0, nodes)], fill_sem.at[0]),
            pltpu.make_async_copy(lower_hbm, table_ref.at[pl.ds(nodes, halo)], fill_sem.at[1]),
            pltpu.make_async_copy(upper_hbm, table_ref.at[pl.ds(nodes + halo, halo)], fill_sem.at[2]),
        ]
        for fill in fills:
            fill.start()
        for fill in fills:
            fill.wait()

    for part in range(2):
        block = 2 * step + part
        fetch(block, part).wait()
        for group in range(LANES // GROUP):
            first = block * LANES + group * GROUP
            rows = [table_ref[pl.ds(first, GROUP)].reshape(2 * GROUP, LANES)]
            for tile in range(others):
                found = [table_ref[slot_refs[part][tile, group * GROUP + node]] for node in range(GROUP)]
                rows.append(jnp.stack(found).reshape(2 * GROUP, LANES))
            sums = jnp.dot(left_ref[part * (LANES // GROUP) + group], jnp.concatenate(rows, axis=0), preferred_element_type=F32)
            for comp in range(3):
                low = sums[comp * GROUP : (comp + 1) * GROUP]
                high = sums[(3 + comp) * GROUP : (4 + comp) * GROUP]
                turn_ref[comp, group * GROUP : (group + 1) * GROUP, :] = jnp.where(low_half, low, high)

        @pl.when(step < steps - 1)
        def _():
            fetch(block + 2, part).start()

        for comp in range(3):
            turned = turn_ref[comp].T
            out_ref[:, comp, part * LANES : (part + 1) * LANES] = (turned[:HALF] + turned[HALF:]).astype(BF16)


def apply_mass(table, from_lower, from_upper, left, tile_slot):
    nodes, halo = table.shape[0], from_lower.shape[0]
    others = tile_slot.shape[0]
    any_space = pl.BlockSpec(memory_space=pl.ANY)
    groups = 2 * LANES // GROUP
    return pl.pallas_call(
        mass_kernel,
        grid=(nodes // (2 * LANES),),
        in_specs=[any_space] * 4 + [pl.BlockSpec((groups, 48, left.shape[2]), lambda i: (i, 0, 0))],
        out_specs=pl.BlockSpec((HALF, 3, 2 * LANES), lambda i: (0, 0, i)),
        out_shape=jax.ShapeDtypeStruct((HALF, 3, nodes), BF16),
        scratch_shapes=[
            pltpu.SMEM((others, LANES), jnp.int32),
            pltpu.SMEM((others, LANES), jnp.int32),
            pltpu.VMEM((nodes + 2 * halo, 2, LANES), BF16),
            pltpu.VMEM((3, LANES, LANES), F32),
            pltpu.SemaphoreType.DMA((2,)),
            pltpu.SemaphoreType.DMA((3,)),
        ],
        cost_estimate=pl.CostEstimate(flops=2 * nodes * 6 * left.shape[2] * LANES, bytes_accessed=left.size * 2, transcendentals=0),
        name="mass_rows",
    )(tile_slot, table, from_lower, from_upper, left)


def summed(value, axis):
    count = lax.axis_size(axis)
    if count & (count - 1):
        return lax.psum(value, axis)
    step = 1
    while step < count:
        value = value + lax.ppermute(value, axis, [(source, source ^ step) for source in range(count)])
        step *= 2
    return value


def body(snapshots, mass_tiles, tile_slot, send_up, send_down):
    snap_count, _, node_count = snapshots.shape
    cols = lax.axis_size("col")
    others = [
        lax.ppermute(snapshots, "col", [(source, (source + shift) % cols) for source in range(cols)])
        for shift in range(1, cols)
    ]
    left = spread_tiles(mass_tiles)
    pieces = []
    for start in range(0, snap_count, HALF):
        piece = snapshots[start : start + HALF]
        size = piece.shape[0]
        if size < HALF:
            piece = jnp.pad(piece, ((0, HALF - size), (0, 0), (0, 0)))
        table, to_upper, to_lower = node_table(piece, send_up, send_down)
        from_lower = shifted(to_upper, "dom", 1)
        from_upper = shifted(to_lower, "dom", -1)
        pieces.append(apply_mass(table, from_lower, from_upper, left, tile_slot)[:size])
    mass_snap = pieces[0] if len(pieces) == 1 else jnp.concatenate(pieces, axis=0)
    flat_mass = mass_snap.reshape(snap_count, -1)
    terms = jnp.concatenate([nt_dot(part.reshape(snap_count, -1), flat_mass) for part in [snapshots] + others], axis=0)
    total = summed(terms, "dom") / (3.0 * node_count * lax.axis_size("dom"))
    gram = jnp.roll(total.reshape(cols, snap_count, snap_count)[::-1], lax.axis_index("col") + 1, axis=0)
    return mass_snap, gram.reshape(cols * snap_count, snap_count)


def solution(mesh):
    placed = (P("col", None, "dom"), P(None, None, None, "dom"), P(None, "dom"), P("dom"), P("dom"))
    return jax.shard_map(
        body,
        mesh=mesh,
        in_specs=placed,
        out_specs=(P("col", None, "dom"), P(None, "col")),
        check_vma=False,
    )
```

time: 302 us -> 78.4 us (0.26)
  local copies, waits for them, and re-layouts: 164 us -> 9.19 us
  blocking collectives: 63.3 us -> 0 us
  other arithmetic: 51.7 us -> 0.31 us
  Pallas kernels: 0 us -> 43.1 us
  between operations: 14.4 us -> 0.75 us
  starting transfers between devices: 3.91 us -> 16.5 us
  waiting for transfers between devices: 1.14 us -> 6.58 us
    gather x5 -> x0, local copies, waits for them, and re-layouts: 160 us -> none  [the longest x3 156 us: apply_mass(): gathered = jnp.take(flat_ext, tile_slot.reshape(-1), axis=1)]
    psum x1 -> x0, blocking collectives: 63.3 us -> none  [body(): summed_gram = lax.psum(block_terms, 'dom')]
    pallas_call x0 -> x3, Pallas kernels: none -> 43.1 us  [the longest x1 26.6 us: apply_mass(): pl.pallas_call(mass_kernel, grid=(nodes // (2 * LANES),), in_specs=[any_s...]
    select_n x6 -> x0, other arithmetic: 23 us -> none  [the longest x2 21.3 us: apply_mass(): gathered = jnp.take(flat_ext, tile_slot.reshape(-1), axis=1)]
    reduce_sum x2 -> x0, other arithmetic: 13.8 us -> none  [apply_mass(): total_sum = total_sum + jnp.sum(tile_part[None] * values[:, None], axis=2)]
    ppermute x0 -> x5, starting transfers between devices: none -> 13.7 us  [the longest x4 10.7 us: summed(): lax.ppermute(value, axis, [(source, source ^ step) for source in range(co...]
    mul x2 -> x0, other arithmetic: 10.5 us -> none  [the longest x1 9.23 us: apply_mass(): total_sum = total_sum + jnp.sum(tile_part[None] * values[:, None], axis=2)]
    ppermute x0 -> x5, waiting for transfers between devices: none -> 6.57 us  [the longest x4 6.57 us: summed(): lax.ppermute(value, axis, [(source, source ^ step) for source in range(co...]
  transfers between devices with their start and end apart: 3 -> 7, of which waited for: 1 -> 4; matrix products, arithmetic and copies ran while one was open for 71% -> 10% of each run, Pallas kernels for 0% -> 56%
where the time goes in v1:
time: 78.4 us; the launch traced here: 77.1 us
  Pallas kernels  43.1 us (55%)
  starting transfers between devices  16.5 us (21%)
  local copies, waits for them, and re-layouts  9.19 us (12%)
  waiting for transfers between devices  6.58 us (8%)
    pallas_call x1, Pallas kernels, apply_mass(): pl.pallas_call(mass_kernel, grid=(nodes // (2 * LANES),), in_specs=[any_s...  26.6 us
    pallas_call x1, Pallas kernels, spread_tiles(): pl.pallas_call(spread_kernel, grid=(node_count // step,), in_specs=[pl.Bl...  11.2 us
    ppermute x4, starting transfers between devices, summed(): lax.ppermute(value, axis, [(source, source ^ step) for source in range(co...  10.7 us
    unnamed x11, local copies, waits for them, and re-layouts  6.98 us
    ppermute x4, waiting for transfers between devices, summed(): lax.ppermute(value, axis, [(source, source ^ step) for source in range(co...  6.57 us
    pallas_call x1, Pallas kernels, node_table(): pl.pallas_call(table_kernel, in_specs=[vmem, smem, smem], out_specs=[vmem...  5.25 us
    ppermute x1, starting transfers between devices, body(): lax.ppermute(snapshots, 'col', [(source, (source + shift) % cols) for sou...  3.06 us
    ppermute x2, starting transfers between devices, shifted(): lax.ppermute(value, axis, [(source, source + steps) for source in range(l...  2.75 us
  transfers between devices with their start and end apart: 7, of which 4 were waited for; matrix products, arithmetic and copies ran while one was open for 10% of the time, Pallas kernels for 56%

profile of v1, /device:TPU:0, one launch (start us, length us, event | category | flops | bytes accessed | tf_op | source)
XLA Modules:
  0.0 77.1 jit_solution(16828306609367233929)
XLA Ops:
  0.6 3.1 %collective-permute-start.2 = (bf16[64,3,2048]{2,0,1:T(8,128)(2,1)}, bf16[64,3,2048]{2,0,1:T(8,128)(2,1)S(1)}, u32[]{:S(2)}, u32[]{:S(2)}) collective-permute-start(bf16[64,3,2048]{2,0,1:T(8,128)(2,1)} %param.6), channel_id=1, source_target_pairs={{0,1},{1,0},{2,3},{3,2},{4,5},{5,4},{6,7},{7,6},{8,9},{9,8},{10,11... | collective-permute-start | bytes 2359304 | tf_op jit(solution)/shard_map/ppermute | solution.py:195
  3.7 2.8 %copy.13.snap_ref = bf16[64,3,2048]{2,1,0:T(4,128)(2,1)} copy(bf16[64,3,2048]{2,0,1:T(8,128)(2,1)} %param.6) | data formatting | bytes 1572864 | tf_op args[0]
  6.5 5.2 %node_table.1 = (bf16[2048,2,128]{2,1,0:T(2,128)(2,1)}, bf16[512,2,128]{2,1,0:T(2,128)(2,1)}, bf16[512,2,128]{2,1,0:T(2,128)(2,1)}) custom-call(bf16[64,3,2048]{2,1,0:T(4,128)(2,1)} %copy.13.snap_ref, s32[512]{0:T(512)} %up_ref.1, s32[512]{0:T(512)} %down_ref.1), custom_call_target="tpu_custom_call" | custom-call | tf_op jit(solution)/shard_map/node_table/pallas_call | solution.py:50
  11.8 1.5 %collective-permute-start = (bf16[512,2,128]{2,1,0:T(2,128)(2,1)}, bf16[512,2,128]{2,1,0:T(2,128)(2,1)S(1)}, u32[]{:S(2)}, u32[]{:S(2)}) collective-permute-start(bf16[512,2,128]{2,1,0:T(2,128)(2,1)} %get-tuple-element.6), channel_id=1, source_target_pairs={{0,2},{2,4},{4,6},{6,8},{8,10},{10,12},{12,14},{14,16},{16,18},{18... | collective-permute-start | bytes 786440 | tf_op jit(solution)/shard_map/ppermute | solution.py:21
  13.2 1.3 %collective-permute-start.1 = (bf16[512,2,128]{2,1,0:T(2,128)(2,1)}, bf16[512,2,128]{2,1,0:T(2,128)(2,1)S(1)}, u32[]{:S(2)}, u32[]{:S(2)}) collective-permute-start(bf16[512,2,128]{2,1,0:T(2,128)(2,1)} %get-tuple-element.7), channel_id=1, source_target_pairs={{2,0},{4,2},{6,4},{8,6},{10,8},{12,10},{14,12},{16,14},{18,16},{20... | collective-permute-start | bytes 786440 | tf_op jit(solution)/shard_map/ppermute | solution.py:21
  14.5 1.6 %copy.14 = bf16[16,3,3,2048]{3,2,1,0:T(4,128)(2,1)S(1)} copy(bf16[16,3,3,2048]{3,0,2,1:T(8,128)(2,1)} %param.7) | data formatting | bytes 1179648 | tf_op args[1]
  16.1 1.2 %reshape.16.tile_ref = bf16[144,2048]{1,0:T(8,128)(2,1)} reshape(bf16[16,3,3,2048]{3,2,1,0:T(4,128)(2,1)S(1)} %copy.14) | data formatting | bytes 1179648 | tf_op jit(solution)/shard_map/reshape | solution.py:104
  17.3 11.2 %spread_tiles.1.left_ref = bf16[256,48,256]{2,1,0:T(8,128)(2,1)} custom-call(bf16[144,2048]{1,0:T(8,128)(2,1)} %reshape.16.tile_ref, bf16[144,1536]{1,0:T(8,128)(2,1)} %constant.32.clone.spread_ref), custom_call_target="tpu_custom_call" | custom-call | flops 905969664 | bytes 6291456 | tf_op jit(solution)/shard_map/spread_tiles/pallas_call | solution.py:93
  28.6 0.0 collective-permute-done.lower_hbm
  28.6 0.0 collective-permute-done.1.upper_hbm
  28.6 0.7 copy-done.2
  29.3 0.1 copy-done.3
  29.4 26.6 %mass_rows.1 = bf16[64,3,2048]{2,1,0:T(4,128)(2,1)} custom-call(s32[15,2048]{1,0:T(8,128)} %slot_hbm.1, bf16[2048,2,128]{2,1,0:T(2,128)(2,1)} %get-tuple-element.5.table_hbm, bf16[512,2,128]{2,1,0:T(2,128)(2,1)} %copy-done.2, bf16[512,2,128]{2,1,0:T(2,128)(2,1)} %copy-done.3, bf16[256,48,256]{2,1,0:T(8,128)(2,1)} %spread_tiles.1.left_ref), custom_call_target="tpu_custom_call" | custom-call | flops 805306368 | bytes 6291456 | tf_op jit(solution)/shard_map/mass_rows/pallas_call | solution.py:161
  56.0 1.8 %copy.17 = bf16[64,3,2048]{2,0,1:T(8,128)(2,1)S(1)} copy(bf16[64,3,2048]{2,1,0:T(4,128)(2,1)} %mass_rows.1) | data formatting | bytes 1572864
  57.8 0.0 copy-start
  57.8 0.4 convolution_bitcast_fusion.1
  58.2 0.0 collective-permute-done.2
  58.2 0.4 convolution_bitcast_fusion
  58.5 0.1 pad_maximum_fusion
  58.6 2.7 %collective-permute-start.3 = (f32[128,64]{0,1:T(8,128)S(1)}, f32[128,64]{0,1:T(8,128)S(1)}, u32[]{:S(2)}, u32[]{:S(2)}) collective-permute-start(f32[128,64]{0,1:T(8,128)S(1)} %pad_maximum_fusion), channel_id=1, source_target_pairs={{0,2},{2,0},{4,6},{6,4},{8,10},{10,8},{12,14},{14,12},{16,18},{18,... | collective-permute-start | bytes 98312 | tf_op jit(solution)/shard_map/ppermute | solution.py:186
  61.3 0.9 %collective-permute-done.3 = f32[128,64]{0,1:T(8,128)S(1)} collective-permute-done((f32[128,64]{0,1:T(8,128)S(1)}, f32[128,64]{0,1:T(8,128)S(1)}, u32[]{:S(2)}, u32[]{:S(2)}) %collective-permute-start.3) | collective-permute-done | bytes 32800 | tf_op jit(solution)/shard_map/ppermute | solution.py:186
  62.1 0.1 fusion.5
  62.2 2.0 %collective-permute-start.4 = (f32[128,64]{0,1:T(8,128)S(1)}, f32[128,64]{0,1:T(8,128)S(1)}, u32[]{:S(2)}, u32[]{:S(2)}) collective-permute-start(f32[128,64]{0,1:T(8,128)S(1)} %fusion.5), channel_id=1, source_target_pairs={{0,4},{2,6},{4,0},{6,2},{8,12},{10,14},{12,8},{14,10},{16,20},{18,... | collective-permute-start | bytes 98312 | tf_op jit(solution)/shard_map/ppermute | solution.py:186
  64.2 1.9 %collective-permute-done.4 = f32[128,64]{0,1:T(8,128)S(1)} collective-permute-done((f32[128,64]{0,1:T(8,128)S(1)}, f32[128,64]{0,1:T(8,128)S(1)}, u32[]{:S(2)}, u32[]{:S(2)}) %collective-permute-start.4) | collective-permute-done | bytes 32800 | tf_op jit(solution)/shard_map/ppermute | solution.py:186
  66.1 3.0 %collective-permute-start.5 = (f32[128,64]{0,1:T(8,128)S(1)}, f32[128,64]{0,1:T(8,128)S(1)}, u32[]{:S(2)}, u32[]{:S(2)}) collective-permute-start(f32[128,64]{0,1:T(8,128)S(1)} %add.26), channel_id=1, source_target_pairs={{0,8},{2,10},{4,12},{6,14},{8,0},{10,2},{12,4},{14,6},{16,24},{18,... | collective-permute-start | bytes 98312 | tf_op jit(solution)/shard_map/ppermute | solution.py:186
  69.1 1.9 %collective-permute-done.5 = f32[128,64]{0,1:T(8,128)S(1)} collective-permute-done((f32[128,64]{0,1:T(8,128)S(1)}, f32[128,64]{0,1:T(8,128)S(1)}, u32[]{:S(2)}, u32[]{:S(2)}) %collective-permute-start.5) | collective-permute-done | bytes 32800 | tf_op jit(solution)/shard_map/ppermute | solution.py:186
  71.0 3.1 %collective-permute-start.6 = (f32[128,64]{0,1:T(8,128)S(1)}, f32[128,64]{0,1:T(8,128)S(1)}, u32[]{:S(2)}, u32[]{:S(2)}) collective-permute-start(f32[128,64]{0,1:T(8,128)S(1)} %add.27), channel_id=1, source_target_pairs={{0,16},{2,18},{4,20},{6,22},{8,24},{10,26},{12,28},{14,30},{16,0},... | collective-permute-start | bytes 98312 | tf_op jit(solution)/shard_map/ppermute | solution.py:186
  74.0 1.9 %collective-permute-done.6 = f32[128,64]{0,1:T(8,128)S(1)} collective-permute-done((f32[128,64]{0,1:T(8,128)S(1)}, f32[128,64]{0,1:T(8,128)S(1)}, u32[]{:S(2)}, u32[]{:S(2)}) %collective-permute-start.6) | collective-permute-done | bytes 32800 | tf_op jit(solution)/shard_map/ppermute | solution.py:186
  75.9 0.1 reshape.17
  76.0 0.2 rev.3
  76.2 0.1 fusion
  76.3 0.7 reshape.18
  (8 shorter events, 0.0 us)
Async XLA Ops:
  0.6 57.5 %collective-permute-start.2 = (bf16[64,3,2048]{2,0,1:T(8,128)(2,1)}, bf16[64,3,2048]{2,0,1:T(8,128)(2,1)S(1)}, u32[]{:S(2)}, u32[]{:S(2)}) collective-permute-start(bf16[64,3,2048]{2,0,1:T(8,128)(2,1)} %param.6), channel_id=1, source_target_pairs={{0,1},{1,0},{2,3},{3,2},{4,5},{5,4},{6,7},{7,6},{8,9},{9,8},{10,11... | collective-permute-start | bytes 2359304 | tf_op jit(solution)/shard_map/ppermute | solution.py:195
  11.8 16.8 %collective-permute-start = (bf16[512,2,128]{2,1,0:T(2,128)(2,1)}, bf16[512,2,128]{2,1,0:T(2,128)(2,1)S(1)}, u32[]{:S(2)}, u32[]{:S(2)}) collective-permute-start(bf16[512,2,128]{2,1,0:T(2,128)(2,1)} %get-tuple-element.6), channel_id=1, source_target_pairs={{0,2},{2,4},{4,6},{6,8},{8,10},{10,12},{12,14},{14,16},{16,18},{18... | collective-permute-start | bytes 786440 | tf_op jit(solution)/shard_map/ppermute | solution.py:21
  13.2 15.4 %collective-permute-start.1 = (bf16[512,2,128]{2,1,0:T(2,128)(2,1)}, bf16[512,2,128]{2,1,0:T(2,128)(2,1)S(1)}, u32[]{:S(2)}, u32[]{:S(2)}) collective-permute-start(bf16[512,2,128]{2,1,0:T(2,128)(2,1)} %get-tuple-element.7), channel_id=1, source_target_pairs={{2,0},{4,2},{6,4},{8,6},{10,8},{12,10},{14,12},{16,14},{18,16},{20... | collective-permute-start | bytes 786440 | tf_op jit(solution)/shard_map/ppermute | solution.py:21
  28.6 29.2 %copy-start.1 = (bf16[64,3,2048]{2,0,1:T(8,128)(2,1)S(1)}, bf16[64,3,2048]{2,0,1:T(8,128)(2,1)}, u32[]{:S(2)}) copy-start(bf16[64,3,2048]{2,0,1:T(8,128)(2,1)} %param.6) | copy-start | bytes 2359300
  28.6 0.7 copy-start.2
  28.6 0.8 %copy-start.3 = (bf16[512,2,128]{2,1,0:T(2,128)(2,1)}, bf16[512,2,128]{2,1,0:T(2,128)(2,1)S(1)}, u32[]{:S(2)}) copy-start(bf16[512,2,128]{2,1,0:T(2,128)(2,1)S(1)} %collective-permute-done.1.upper_hbm) | copy-start | bytes 786436
  57.8 19.3 %copy-start = (bf16[64,3,2048]{2,0,1:T(8,128)(2,1)}, bf16[64,3,2048]{2,0,1:T(8,128)(2,1)S(1)}, u32[]{:S(2)}) copy-start(bf16[64,3,2048]{2,0,1:T(8,128)(2,1)S(1)} %copy.17) | copy-start | bytes 2359300
  58.6 3.5 %collective-permute-start.3 = (f32[128,64]{0,1:T(8,128)S(1)}, f32[128,64]{0,1:T(8,128)S(1)}, u32[]{:S(2)}, u32[]{:S(2)}) collective-permute-start(f32[128,64]{0,1:T(8,128)S(1)} %pad_maximum_fusion), channel_id=1, source_target_pairs={{0,2},{2,0},{4,6},{6,4},{8,10},{10,8},{12,14},{14,12},{16,18},{18,... | collective-permute-start | bytes 98312 | tf_op jit(solution)/shard_map/ppermute | solution.py:186
  62.2 3.9 %collective-permute-start.4 = (f32[128,64]{0,1:T(8,128)S(1)}, f32[128,64]{0,1:T(8,128)S(1)}, u32[]{:S(2)}, u32[]{:S(2)}) collective-permute-start(f32[128,64]{0,1:T(8,128)S(1)} %fusion.5), channel_id=1, source_target_pairs={{0,4},{2,6},{4,0},{6,2},{8,12},{10,14},{12,8},{14,10},{16,20},{18,... | collective-permute-start | bytes 98312 | tf_op jit(solution)/shard_map/ppermute | solution.py:186
  66.1 4.8 %collective-permute-start.5 = (f32[128,64]{0,1:T(8,128)S(1)}, f32[128,64]{0,1:T(8,128)S(1)}, u32[]{:S(2)}, u32[]{:S(2)}) collective-permute-start(f32[128,64]{0,1:T(8,128)S(1)} %add.26), channel_id=1, source_target_pairs={{0,8},{2,10},{4,12},{6,14},{8,0},{10,2},{12,4},{14,6},{16,24},{18,... | collective-permute-start | bytes 98312 | tf_op jit(solution)/shard_map/ppermute | solution.py:186
  71.0 4.9 %collective-permute-start.6 = (f32[128,64]{0,1:T(8,128)S(1)}, f32[128,64]{0,1:T(8,128)S(1)}, u32[]{:S(2)}, u32[]{:S(2)}) collective-permute-start(f32[128,64]{0,1:T(8,128)S(1)} %add.27), channel_id=1, source_target_pairs={{0,16},{2,18},{4,20},{6,22},{8,24},{10,26},{12,28},{14,30},{16,0},... | collective-permute-start | bytes 98312 | tf_op jit(solution)/shard_map/ppermute | solution.py:186

commit v2 on v1

--- a/solution.py
+++ b/solution.py
@@ -32,7 +32,7 @@
     pick = jnp.where(col == (row // 2) + LANES * (row % 2), 1.0, 0.0).astype(BF16)
     empty = jnp.zeros((HALF, LANES), BF16)
     for start in range(0, node_count, LANES):
-        comps = [snap_ref[:, comp, start : start + LANES] for comp in range(3)]
+        comps = [snap_ref[comp, :, start : start + LANES] for comp in range(3)]
         first = jnp.concatenate([comps[0], comps[2]], axis=0)
         second = jnp.concatenate([comps[1], empty], axis=0)
         rows = nt_dot(pick, jnp.concatenate([first, second], axis=1)).astype(BF16)
@@ -61,11 +61,11 @@
 
 
 def spread_matrix(tiles):
-    spread = np.zeros((tiles, 3, 3, 2, 3, tiles, GROUP, 2), np.float32)
+    spread = np.zeros((3, 3, tiles, 2, 3, tiles, GROUP, 2), np.float32)
     for tile in range(tiles):
         for comp in range(3):
             for half, pair, in_comp in ((0, 0, 0), (0, 1, 1), (1, 0, 2)):
-                spread[tile, comp, in_comp, half, comp, tile, :, pair] = 1.0
+                spread[comp, in_comp, tile, half, comp, tile, :, pair] = 1.0
     return jnp.asarray(spread.reshape(tiles * 9, 6 * tiles * GROUP * 2), BF16)
 
 
@@ -101,7 +101,7 @@
         out_shape=jax.ShapeDtypeStruct((node_count // GROUP, 48, depth), BF16),
         cost_estimate=pl.CostEstimate(flops=2 * node_count * tiles * 9 * 6 * depth, bytes_accessed=node_count * 6 * depth * 2, transcendentals=0),
         name="spread_tiles",
-    )(mass_tiles.reshape(tiles * 9, node_count), spread)
+    )(jnp.transpose(mass_tiles, (1, 2, 0, 3)).reshape(tiles * 9, node_count), spread)
 
 
 def mass_kernel(slot_hbm, table_hbm, lower_hbm, upper_hbm, left_ref, out_ref, slots0, slots1, table_ref, turn_ref, sem, fill_sem):
@@ -150,7 +150,7 @@
 
         for comp in range(3):
             turned = turn_ref[comp].T
-            out_ref[:, comp, part * LANES : (part + 1) * LANES] = (turned[:HALF] + turned[HALF:]).astype(BF16)
+            out_ref[comp, :, part * LANES : (part + 1) * LANES] = (turned[:HALF] + turned[HALF:]).astype(BF16)
 
 
 def apply_mass(table, from_lower, from_upper, left, tile_slot):
@@ -162,8 +162,8 @@
         mass_kernel,
         grid=(nodes // (2 * LANES),),
         in_specs=[any_space] * 4 + [pl.BlockSpec((groups, 48, left.shape[2]), lambda i: (i, 0, 0))],
-        out_specs=pl.BlockSpec((HALF, 3, 2 * LANES), lambda i: (0, 0, i)),
-        out_shape=jax.ShapeDtypeStruct((HALF, 3, nodes), BF16),
+        out_specs=pl.BlockSpec((3, HALF, 2 * LANES), lambda i: (0, 0, i)),
+        out_shape=jax.ShapeDtypeStruct((3, HALF, nodes), BF16),
         scratch_shapes=[
             pltpu.SMEM((others, LANES), jnp.int32),
             pltpu.SMEM((others, LANES), jnp.int32),
@@ -188,30 +188,37 @@
     return value
 
 
+def in_order(blocks):
+    cols, here = len(blocks), lax.axis_index("col")
+    if cols == 2:
+        first = here == 0
+        return jnp.concatenate([jnp.where(first, *blocks), jnp.where(first, *blocks[::-1])], axis=1)
+    return jnp.concatenate([lax.dynamic_index_in_dim(jnp.stack(blocks), lax.rem(here - col + cols, cols), 0, False) for col in range(cols)], axis=1)
+
+
 def body(snapshots, mass_tiles, tile_slot, send_up, send_down):
     snap_count, _, node_count = snapshots.shape
     cols = lax.axis_size("col")
-    others = [
-        lax.ppermute(snapshots, "col", [(source, (source + shift) % cols) for source in range(cols)])
+    by_comp = jnp.transpose(snapshots, (1, 0, 2))
+    parts = [by_comp] + [
+        lax.ppermute(by_comp, "col", [(source, (source + shift) % cols) for source in range(cols)])
         for shift in range(1, cols)
     ]
     left = spread_tiles(mass_tiles)
     pieces = []
     for start in range(0, snap_count, HALF):
-        piece = snapshots[start : start + HALF]
-        size = piece.shape[0]
+        piece = by_comp[:, start : start + HALF]
+        size = piece.shape[1]
         if size < HALF:
-            piece = jnp.pad(piece, ((0, HALF - size), (0, 0), (0, 0)))
+            piece = jnp.pad(piece, ((0, 0), (0, HALF - size), (0, 0)))
         table, to_upper, to_lower = node_table(piece, send_up, send_down)
         from_lower = shifted(to_upper, "dom", 1)
         from_upper = shifted(to_lower, "dom", -1)
-        pieces.append(apply_mass(table, from_lower, from_upper, left, tile_slot)[:size])
-    mass_snap = pieces[0] if len(pieces) == 1 else jnp.concatenate(pieces, axis=0)
-    flat_mass = mass_snap.reshape(snap_count, -1)
-    terms = jnp.concatenate([nt_dot(part.reshape(snap_count, -1), flat_mass) for part in [snapshots] + others], axis=0)
-    total = summed(terms, "dom") / (3.0 * node_count * lax.axis_size("dom"))
-    gram = jnp.roll(total.reshape(cols, snap_count, snap_count)[::-1], lax.axis_index("col") + 1, axis=0)
-    return mass_snap, gram.reshape(cols * snap_count, snap_count)
+        pieces.append(apply_mass(table, from_lower, from_upper, left, tile_slot)[:, :size])
+    mass_rows = pieces[0] if len(pieces) == 1 else jnp.concatenate(pieces, axis=1)
+    blocks = [lax.dot_general(mass_rows, part, (((0, 2), (0, 2)), ((), ())), preferred_element_type=F32) for part in parts]
+    total = summed(in_order(blocks), "dom") / (3.0 * node_count * lax.axis_size("dom"))
+    return jnp.transpose(mass_rows, (1, 0, 2)), total.T
 
 
 def solution(mesh):

time: 78.4 us -> 69.5 us (0.89)
  local copies, waits for them, and re-layouts: 9.19 us -> 0.78 us
  Pallas kernels: 43.1 us -> 39.9 us
  matrix products: 0.7 us -> 2.97 us
    unnamed x11 -> x6, local copies, waits for them, and re-layouts: 6.98 us -> 0.78 us
    dot_general x2, matrix products: 0.7 us -> 2.97 us  [body(): lax.dot_general(mass_rows, part, (((0, 2), (0, 2)), ((), ())), preferred_...]
    reshape x3 -> x0, local copies, waits for them, and re-layouts: 2.05 us -> none  [the longest x1 1.24 us: spread_tiles(): mass_tiles.reshape(tiles * 9, node_count)]
    pallas_call x1, Pallas kernels: 5.25 us -> 3.47 us  [node_table(): pl.pallas_call(table_kernel, in_specs=[vmem, smem, smem], out_specs=[vmem...]
    pallas_call x1, Pallas kernels: 26.6 us -> 25.2 us  [apply_mass(): pl.pallas_call(mass_kernel, grid=(nodes // (2 * LANES),), in_specs=[any_s...]
  transfers between devices with their start and end apart: 7 -> 7, of which waited for: 4 -> 4; matrix products, arithmetic and copies ran while one was open for 10% -> 0% of each run, Pallas kernels for 56% -> 59%
where the time goes in v2:
time: 69.5 us; the launch traced here: 68.2 us
  Pallas kernels  39.9 us (57%)
  starting transfers between devices  16.5 us (24%)
  waiting for transfers between devices  6.61 us (10%)
  matrix products  2.97 us (4%)
  other arithmetic  0.79 us (1%)
  local copies, waits for them, and re-layouts  0.78 us (1%)
  between operations  0.72 us (1%)
    pallas_call x1, Pallas kernels, apply_mass(): pl.pallas_call(mass_kernel, grid=(nodes // (2 * LANES),), in_specs=[any_s...  25.2 us
    pallas_call x1, Pallas kernels, spread_tiles(): pl.pallas_call(spread_kernel, grid=(node_count // step,), in_specs=[pl.Bl...  11.2 us
    ppermute x4, starting transfers between devices, summed(): lax.ppermute(value, axis, [(source, source ^ step) for source in range(co...  10.6 us
    ppermute x4, waiting for transfers between devices, summed(): lax.ppermute(value, axis, [(source, source ^ step) for source in range(co...  6.6 us
    pallas_call x1, Pallas kernels, node_table(): pl.pallas_call(table_kernel, in_specs=[vmem, smem, smem], out_specs=[vmem...  3.47 us
    ppermute x1, starting transfers between devices, body(): lax.ppermute(by_comp, 'col', [(source, (source + shift) % cols) for sourc...  3.06 us
    dot_general x2, matrix products, body(): lax.dot_general(mass_rows, part, (((0, 2), (0, 2)), ((), ())), preferred_...  2.97 us
    ppermute x2, starting transfers between devices, shifted(): lax.ppermute(value, axis, [(source, source + steps) for source in range(l...  2.76 us
  transfers between devices with their start and end apart: 7, of which 4 were waited for; matrix products, arithmetic and copies ran while one was open for 0% of the time, Pallas kernels for 59%

profile of v2, /device:TPU:0, one launch (start us, length us, event | category | flops | bytes accessed | tf_op | source)
XLA Modules:
  0.0 68.2 jit_solution(4822657184703336111)
XLA Ops:
  0.6 3.1 %collective-permute-start.2 = (bf16[3,64,2048]{2,1,0:T(8,128)(2,1)}, bf16[3,64,2048]{2,1,0:T(8,128)(2,1)S(1)}, u32[]{:S(2)}, u32[]{:S(2)}) collective-permute-start(bf16[3,64,2048]{2,1,0:T(8,128)(2,1)} %bitcast.19), channel_id=1, source_target_pairs={{0,1},{1,0},{2,3},{3,2},{4,5},{5,4},{6,7},{7,6},{8,9},{9,8},{10,11... | collective-permute-start | bytes 2359304 | tf_op jit(solution)/shard_map/ppermute | solution.py:204
  3.7 3.5 %node_table.1 = (bf16[2048,2,128]{2,1,0:T(2,128)(2,1)}, bf16[512,2,128]{2,1,0:T(2,128)(2,1)}, bf16[512,2,128]{2,1,0:T(2,128)(2,1)}) custom-call(bf16[3,64,2048]{2,1,0:T(8,128)(2,1)} %bitcast.20, s32[512]{0:T(512)} %up_ref.1, s32[512]{0:T(512)} %down_ref.1), custom_call_target="tpu_custom_call" | custom-call | tf_op jit(solution)/shard_map/node_table/pallas_call | solution.py:50
  7.2 1.5 %collective-permute-start = (bf16[512,2,128]{2,1,0:T(2,128)(2,1)}, bf16[512,2,128]{2,1,0:T(2,128)(2,1)S(1)}, u32[]{:S(2)}, u32[]{:S(2)}) collective-permute-start(bf16[512,2,128]{2,1,0:T(2,128)(2,1)} %get-tuple-element.6), channel_id=1, source_target_pairs={{0,2},{2,4},{4,6},{6,8},{8,10},{10,12},{12,14},{14,16},{16,18},{18... | collective-permute-start | bytes 786440 | tf_op jit(solution)/shard_map/ppermute | solution.py:21
  8.6 1.3 %collective-permute-start.1 = (bf16[512,2,128]{2,1,0:T(2,128)(2,1)}, bf16[512,2,128]{2,1,0:T(2,128)(2,1)S(1)}, u32[]{:S(2)}, u32[]{:S(2)}) collective-permute-start(bf16[512,2,128]{2,1,0:T(2,128)(2,1)} %get-tuple-element.7), channel_id=1, source_target_pairs={{2,0},{4,2},{6,4},{8,6},{10,8},{12,10},{14,12},{16,14},{18,16},{20... | collective-permute-start | bytes 786440 | tf_op jit(solution)/shard_map/ppermute | solution.py:21
  9.9 11.2 %spread_tiles.1.left_ref = bf16[256,48,256]{2,1,0:T(8,128)(2,1)} custom-call(bf16[144,2048]{1,0:T(8,128)(2,1)} %bitcast.21, bf16[144,1536]{1,0:T(8,128)(2,1)} %constant.11.clone.spread_ref), custom_call_target="tpu_custom_call" | custom-call | flops 905969664 | bytes 6291456 | tf_op jit(solution)/shard_map/spread_tiles/pallas_call | solution.py:93
  21.2 0.0 copy-start
  21.2 0.0 collective-permute-done.lower_hbm
  21.2 0.0 copy-start.1
  21.2 0.0 collective-permute-done.1.upper_hbm
  21.2 0.0 copy-start.2
  21.2 0.7 copy-done.1
  21.9 0.1 copy-done.2
  22.0 25.2 %mass_rows.1 = bf16[3,64,2048]{2,1,0:T(8,128)(2,1)} custom-call(s32[15,2048]{1,0:T(8,128)} %slot_hbm.1, bf16[2048,2,128]{2,1,0:T(2,128)(2,1)} %get-tuple-element.5.table_hbm, bf16[512,2,128]{2,1,0:T(2,128)(2,1)} %copy-done.1, bf16[512,2,128]{2,1,0:T(2,128)(2,1)} %copy-done.2, bf16[256,48,256]{2,1,0:T(8,128)(2,1)} %spread_tiles.1.left_ref), custom_call_target="tpu_custom_call" | custom-call | flops 805306368 | bytes 6291456 | tf_op jit(solution)/shard_map/mass_rows/pallas_call | solution.py:161
  47.2 0.0 collective-permute-done.2
  47.2 1.5 %convolution_bitcast_fusion = f32[64,64]{1,0:T(8,128)S(1)} fusion(bf16[3,64,2048]{2,1,0:T(8,128)(2,1)} %mass_rows.1, bf16[3,64,2048]{2,1,0:T(8,128)(2,1)S(1)} %collective-permute-done.2), kind=kOutput, calls=%fused_computation | convolution fusion | flops 50331648 | bytes 1589248 | tf_op jit(solution)/shard_map/dot_general | solution.py:219
  48.7 0.0 copy-done
  48.7 1.5 %broadcast_select_fusion.1 = (f32[64,64]{1,0:T(8,128)S(1)}, f32[64,64]{1,0:T(8,128)S(1)}) fusion(f32[64,64]{1,0:T(8,128)S(1)} %convolution_bitcast_fusion, pred[]{:T(512)S(6)} %eq.3, bf16[3,64,2048]{2,1,0:T(8,128)(2,1)} %mass_rows.1, bf16[64,3,2048]{2,0,1:T(8,128)(2,1)S(1)} %copy-done), kind=kOutput, calls=%fused_computation.5 | convolution fusion | flops 50339840 | bytes 1622017 | tf_op jit(solution)/shard_map/dot_general | solution.py:219
  50.2 0.1 pad_maximum_fusion
  50.3 2.7 %collective-permute-start.3 = (f32[64,128]{1,0:T(8,128)S(1)}, f32[64,128]{1,0:T(8,128)S(1)}, u32[]{:S(2)}, u32[]{:S(2)}) collective-permute-start(f32[64,128]{1,0:T(8,128)S(1)} %pad_maximum_fusion), channel_id=1, source_target_pairs={{0,2},{2,0},{4,6},{6,4},{8,10},{10,8},{12,14},{14,12},{16,18},{18,... | collective-permute-start | bytes 98312 | tf_op jit(solution)/shard_map/ppermute | solution.py:186
  53.0 0.9 %collective-permute-done.3 = f32[64,128]{1,0:T(8,128)S(1)} collective-permute-done((f32[64,128]{1,0:T(8,128)S(1)}, f32[64,128]{1,0:T(8,128)S(1)}, u32[]{:S(2)}, u32[]{:S(2)}) %collective-permute-start.3) | collective-permute-done | bytes 32800 | tf_op jit(solution)/shard_map/ppermute | solution.py:186
  53.8 0.1 fusion.4
  53.9 2.0 %collective-permute-start.4 = (f32[64,128]{1,0:T(8,128)S(1)}, f32[64,128]{1,0:T(8,128)S(1)}, u32[]{:S(2)}, u32[]{:S(2)}) collective-permute-start(f32[64,128]{1,0:T(8,128)S(1)} %fusion.4), channel_id=1, source_target_pairs={{0,4},{2,6},{4,0},{6,2},{8,12},{10,14},{12,8},{14,10},{16,20},{18,... | collective-permute-start | bytes 98312 | tf_op jit(solution)/shard_map/ppermute | solution.py:186
  55.9 2.0 %collective-permute-done.4 = f32[64,128]{1,0:T(8,128)S(1)} collective-permute-done((f32[64,128]{1,0:T(8,128)S(1)}, f32[64,128]{1,0:T(8,128)S(1)}, u32[]{:S(2)}, u32[]{:S(2)}) %collective-permute-start.4) | collective-permute-done | bytes 32800 | tf_op jit(solution)/shard_map/ppermute | solution.py:186
  57.8 2.9 %collective-permute-start.5 = (f32[64,128]{1,0:T(8,128)S(1)}, f32[64,128]{1,0:T(8,128)S(1)}, u32[]{:S(2)}, u32[]{:S(2)}) collective-permute-start(f32[64,128]{1,0:T(8,128)S(1)} %add.13), channel_id=1, source_target_pairs={{0,8},{2,10},{4,12},{6,14},{8,0},{10,2},{12,4},{14,6},{16,24},{18,... | collective-permute-start | bytes 98312 | tf_op jit(solution)/shard_map/ppermute | solution.py:186
  60.8 1.9 %collective-permute-done.5 = f32[64,128]{1,0:T(8,128)S(1)} collective-permute-done((f32[64,128]{1,0:T(8,128)S(1)}, f32[64,128]{1,0:T(8,128)S(1)}, u32[]{:S(2)}, u32[]{:S(2)}) %collective-permute-start.5) | collective-permute-done | bytes 32800 | tf_op jit(solution)/shard_map/ppermute | solution.py:186
  62.7 3.1 %collective-permute-start.6 = (f32[64,128]{1,0:T(8,128)S(1)}, f32[64,128]{1,0:T(8,128)S(1)}, u32[]{:S(2)}, u32[]{:S(2)}) collective-permute-start(f32[64,128]{1,0:T(8,128)S(1)} %add.14), channel_id=1, source_target_pairs={{0,16},{2,18},{4,20},{6,22},{8,24},{10,26},{12,28},{14,30},{16,0},... | collective-permute-start | bytes 98312 | tf_op jit(solution)/shard_map/ppermute | solution.py:186
  65.7 1.9 %collective-permute-done.6 = f32[64,128]{1,0:T(8,128)S(1)} collective-permute-done((f32[64,128]{1,0:T(8,128)S(1)}, f32[64,128]{1,0:T(8,128)S(1)}, u32[]{:S(2)}, u32[]{:S(2)}) %collective-permute-start.6) | collective-permute-done | bytes 32800 | tf_op jit(solution)/shard_map/ppermute | solution.py:186
  67.6 0.6 multiply_bitcast_fusion
  (2 shorter events, 0.0 us)
Async XLA Ops:
  0.6 46.6 %collective-permute-start.2 = (bf16[3,64,2048]{2,1,0:T(8,128)(2,1)}, bf16[3,64,2048]{2,1,0:T(8,128)(2,1)S(1)}, u32[]{:S(2)}, u32[]{:S(2)}) collective-permute-start(bf16[3,64,2048]{2,1,0:T(8,128)(2,1)} %bitcast.19), channel_id=1, source_target_pairs={{0,1},{1,0},{2,3},{3,2},{4,5},{5,4},{6,7},{7,6},{8,9},{9,8},{10,11... | collective-permute-start | bytes 2359304 | tf_op jit(solution)/shard_map/ppermute | solution.py:204
  7.2 14.0 %collective-permute-start = (bf16[512,2,128]{2,1,0:T(2,128)(2,1)}, bf16[512,2,128]{2,1,0:T(2,128)(2,1)S(1)}, u32[]{:S(2)}, u32[]{:S(2)}) collective-permute-start(bf16[512,2,128]{2,1,0:T(2,128)(2,1)} %get-tuple-element.6), channel_id=1, source_target_pairs={{0,2},{2,4},{4,6},{6,8},{8,10},{10,12},{12,14},{14,16},{16,18},{18... | collective-permute-start | bytes 786440 | tf_op jit(solution)/shard_map/ppermute | solution.py:21
  8.6 12.6 %collective-permute-start.1 = (bf16[512,2,128]{2,1,0:T(2,128)(2,1)}, bf16[512,2,128]{2,1,0:T(2,128)(2,1)S(1)}, u32[]{:S(2)}, u32[]{:S(2)}) collective-permute-start(bf16[512,2,128]{2,1,0:T(2,128)(2,1)} %get-tuple-element.7), channel_id=1, source_target_pairs={{2,0},{4,2},{6,4},{8,6},{10,8},{12,10},{14,12},{16,14},{18,16},{20... | collective-permute-start | bytes 786440 | tf_op jit(solution)/shard_map/ppermute | solution.py:21
  21.2 27.5 %copy-start = (bf16[64,3,2048]{2,0,1:T(8,128)(2,1)S(1)}, bf16[64,3,2048]{2,0,1:T(8,128)(2,1)}, u32[]{:S(2)}) copy-start(bf16[64,3,2048]{2,0,1:T(8,128)(2,1)} %param.6) | copy-start | bytes 2359300
  21.2 0.7 %copy-start.1 = (bf16[512,2,128]{2,1,0:T(2,128)(2,1)}, bf16[512,2,128]{2,1,0:T(2,128)(2,1)S(1)}, u32[]{:S(2)}) copy-start(bf16[512,2,128]{2,1,0:T(2,128)(2,1)S(1)} %collective-permute-done.lower_hbm) | copy-start | bytes 786436
  21.2 0.8 %copy-start.2 = (bf16[512,2,128]{2,1,0:T(2,128)(2,1)}, bf16[512,2,128]{2,1,0:T(2,128)(2,1)S(1)}, u32[]{:S(2)}) copy-start(bf16[512,2,128]{2,1,0:T(2,128)(2,1)S(1)} %collective-permute-done.1.upper_hbm) | copy-start | bytes 786436
  50.3 3.5 %collective-permute-start.3 = (f32[64,128]{1,0:T(8,128)S(1)}, f32[64,128]{1,0:T(8,128)S(1)}, u32[]{:S(2)}, u32[]{:S(2)}) collective-permute-start(f32[64,128]{1,0:T(8,128)S(1)} %pad_maximum_fusion), channel_id=1, source_target_pairs={{0,2},{2,0},{4,6},{6,4},{8,10},{10,8},{12,14},{14,12},{16,18},{18,... | collective-permute-start | bytes 98312 | tf_op jit(solution)/shard_map/ppermute | solution.py:186
  53.9 3.9 %collective-permute-start.4 = (f32[64,128]{1,0:T(8,128)S(1)}, f32[64,128]{1,0:T(8,128)S(1)}, u32[]{:S(2)}, u32[]{:S(2)}) collective-permute-start(f32[64,128]{1,0:T(8,128)S(1)} %fusion.4), channel_id=1, source_target_pairs={{0,4},{2,6},{4,0},{6,2},{8,12},{10,14},{12,8},{14,10},{16,20},{18,... | collective-permute-start | bytes 98312 | tf_op jit(solution)/shard_map/ppermute | solution.py:186
  57.8 4.8 %collective-permute-start.5 = (f32[64,128]{1,0:T(8,128)S(1)}, f32[64,128]{1,0:T(8,128)S(1)}, u32[]{:S(2)}, u32[]{:S(2)}) collective-permute-start(f32[64,128]{1,0:T(8,128)S(1)} %add.13), channel_id=1, source_target_pairs={{0,8},{2,10},{4,12},{6,14},{8,0},{10,2},{12,4},{14,6},{16,24},{18,... | collective-permute-start | bytes 98312 | tf_op jit(solution)/shard_map/ppermute | solution.py:186
  62.7 4.9 %collective-permute-start.6 = (f32[64,128]{1,0:T(8,128)S(1)}, f32[64,128]{1,0:T(8,128)S(1)}, u32[]{:S(2)}, u32[]{:S(2)}) collective-permute-start(f32[64,128]{1,0:T(8,128)S(1)} %add.14), channel_id=1, source_target_pairs={{0,16},{2,18},{4,20},{6,22},{8,24},{10,26},{12,28},{14,30},{16,0},... | collective-permute-start | bytes 98312 | tf_op jit(solution)/shard_map/ppermute | solution.py:186

commit v3 on v2

--- a/solution.py
+++ b/solution.py
@@ -70,25 +70,30 @@
 
 
 def spread_kernel(tile_ref, spread_ref, out_ref):
-    depth = out_ref.shape[2]
-    turned = tile_ref[...].astype(F32).T.astype(BF16)
+    sides = out_ref.shape[0]
+    depth = sides * LANES
+    groups = LANES // GROUP
     node = lax.broadcasted_iota(jnp.int32, (GROUP, depth), 0)
     slot = (lax.broadcasted_iota(jnp.int32, (GROUP, depth), 1) // 2) % GROUP
     own = node == slot
-    for pair in range(3):
-        both = [
-            jnp.dot(turned, spread_ref[:, (2 * pair + one) * depth : (2 * pair + one + 1) * depth], preferred_element_type=F32)
-            for one in range(2)
-        ]
-        for group in range(out_ref.shape[0]):
-            kept = [jnp.where(own, part[group * GROUP : (group + 1) * GROUP], 0.0) for part in both]
-            out_ref[group, 16 * pair : 16 * (pair + 1), :] = jnp.concatenate(kept, axis=0).astype(BF16)
+    for block in range(tile_ref.shape[1] // LANES):
+        turned = tile_ref[:, block * LANES : (block + 1) * LANES].T
+        for pair in range(3):
+            both = [
+                jnp.dot(turned, spread_ref[:, (2 * pair + one) * depth : (2 * pair + one + 1) * depth], preferred_element_type=F32)
+                for one in range(2)
+            ]
+            for group in range(groups):
+                kept = [jnp.where(own, part[group * GROUP : (group + 1) * GROUP], 0.0) for part in both]
+                rows = jnp.concatenate(kept, axis=0).astype(BF16)
+                for side in range(sides):
+                    out_ref[side, block * groups + group, 16 * pair : 16 * (pair + 1), :] = rows[:, side * LANES : (side + 1) * LANES]
 
 
 def spread_tiles(mass_tiles):
     tiles, _, _, node_count = mass_tiles.shape
     depth = tiles * GROUP * 2
-    step = LANES
+    step = min(node_count, 4 * LANES)
     spread = spread_matrix(tiles)
     return pl.pallas_call(
         spread_kernel,
@@ -97,48 +102,59 @@
             pl.BlockSpec((tiles * 9, step), lambda i: (0, i)),
             pl.BlockSpec(spread.shape, lambda i: (0, 0)),
         ],
-        out_specs=pl.BlockSpec((step // GROUP, 48, depth), lambda i: (i, 0, 0)),
-        out_shape=jax.ShapeDtypeStruct((node_count // GROUP, 48, depth), BF16),
+        out_specs=pl.BlockSpec((depth // LANES, step // GROUP, 48, LANES), lambda i: (0, i, 0, 0)),
+        out_shape=jax.ShapeDtypeStruct((depth // LANES, node_count // GROUP, 48, LANES), BF16),
         cost_estimate=pl.CostEstimate(flops=2 * node_count * tiles * 9 * 6 * depth, bytes_accessed=node_count * 6 * depth * 2, transcendentals=0),
         name="spread_tiles",
     )(jnp.transpose(mass_tiles, (1, 2, 0, 3)).reshape(tiles * 9, node_count), spread)
 
 
-def mass_kernel(slot_hbm, table_hbm, lower_hbm, upper_hbm, left_ref, out_ref, slots0, slots1, table_ref, turn_ref, sem, fill_sem):
+def mass_kernel(parts, slot_hbm, table_hbm, lower_hbm, upper_hbm, left_hbm, own_hbm, out_ref, *scratch):
+    slot_refs, left_refs, own_refs = (scratch[kind * parts : (kind + 1) * parts] for kind in range(3))
+    table_ref, turn_ref, sem, fill_sem = scratch[3 * parts :]
     step, steps = pl.program_id(0), pl.num_programs(0)
     others = slot_hbm.shape[0]
+    sides = left_hbm.shape[0]
     nodes, halo = table_hbm.shape[0], lower_hbm.shape[0]
+    groups = LANES // GROUP
     low_half = lax.broadcasted_iota(jnp.int32, (GROUP, LANES), 1) < HALF
-    slot_refs = (slots0, slots1)
-
-    def fetch(block, part):
-        source = slot_hbm.at[:, pl.ds(pl.multiple_of(block * LANES, LANES), LANES)]
-        return pltpu.make_async_copy(source, slot_refs[part], sem.at[part])
+
+    def fetches(block, part):
+        def window(width):
+            return pl.ds(pl.multiple_of(block * width, width), width)
+
+        return (
+            pltpu.make_async_copy(slot_hbm.at[:, window(LANES)], slot_refs[part], sem.at[part, 0]),
+            pltpu.make_async_copy(left_hbm.at[:, window(groups)], left_refs[part], sem.at[part, 1]),
+            pltpu.make_async_copy(own_hbm.at[window(2 * LANES)], own_refs[part], sem.at[part, 2]),
+        )
 
     @pl.when(step == 0)
     def _():
-        fetch(0, 0).start()
-        fetch(1, 1).start()
         fills = [
             pltpu.make_async_copy(table_hbm, table_ref.at[pl.ds(0, nodes)], fill_sem.at[0]),
             pltpu.make_async_copy(lower_hbm, table_ref.at[pl.ds(nodes, halo)], fill_sem.at[1]),
             pltpu.make_async_copy(upper_hbm, table_ref.at[pl.ds(nodes + halo, halo)], fill_sem.at[2]),
         ]
-        for fill in fills:
-            fill.start()
+        for copy in (*fetches(0, 0), *fills):
+            copy.start()
+        for part in range(1, parts):
+            for copy in fetches(part, part):
+                copy.start()
         for fill in fills:
             fill.wait()
 
-    for part in range(2):
-        block = 2 * step + part
-        fetch(block, part).wait()
-        for group in range(LANES // GROUP):
-            first = block * LANES + group * GROUP
-            rows = [table_ref[pl.ds(first, GROUP)].reshape(2 * GROUP, LANES)]
+    for part in range(parts):
+        block = parts * step + part
+        for copy in fetches(block, part):
+            copy.wait()
+        for group in range(groups):
+            rows = [own_refs[part][2 * GROUP * group : 2 * GROUP * (group + 1), :]]
             for tile in range(others):
                 found = [table_ref[slot_refs[part][tile, group * GROUP + node]] for node in range(GROUP)]
                 rows.append(jnp.stack(found).reshape(2 * GROUP, LANES))
-            sums = jnp.dot(left_ref[part * (LANES // GROUP) + group], jnp.concatenate(rows, axis=0), preferred_element_type=F32)
+            left = jnp.concatenate([left_refs[part][side, group] for side in range(sides)], axis=1)
+            sums = jnp.dot(left, jnp.concatenate(rows, axis=0), preferred_element_type=F32)
             for comp in range(3):
                 low = sums[comp * GROUP : (comp + 1) * GROUP]
                 high = sums[(3 + comp) * GROUP : (4 + comp) * GROUP]
@@ -146,7 +162,8 @@
 
         @pl.when(step < steps - 1)
         def _():
-            fetch(block + 2, part).start()
+            for copy in fetches(block + parts, part):
+                copy.start()
 
         for comp in range(3):
             turned = turn_ref[comp].T
@@ -156,25 +173,28 @@
 def apply_mass(table, from_lower, from_upper, left, tile_slot):
     nodes, halo = table.shape[0], from_lower.shape[0]
     others = tile_slot.shape[0]
+    sides = left.shape[0]
+    blocks = nodes // LANES
+    parts = next(count for count in (4, 2, 1) if blocks % count == 0)
     any_space = pl.BlockSpec(memory_space=pl.ANY)
-    groups = 2 * LANES // GROUP
     return pl.pallas_call(
-        mass_kernel,
-        grid=(nodes // (2 * LANES),),
-        in_specs=[any_space] * 4 + [pl.BlockSpec((groups, 48, left.shape[2]), lambda i: (i, 0, 0))],
-        out_specs=pl.BlockSpec((3, HALF, 2 * LANES), lambda i: (0, 0, i)),
+        functools.partial(mass_kernel, parts),
+        grid=(blocks // parts,),
+        in_specs=[any_space] * 6,
+        out_specs=pl.BlockSpec((3, HALF, parts * LANES), lambda i: (0, 0, i)),
         out_shape=jax.ShapeDtypeStruct((3, HALF, nodes), BF16),
-        scratch_shapes=[
-            pltpu.SMEM((others, LANES), jnp.int32),
-            pltpu.SMEM((others, LANES), jnp.int32),
+        scratch_shapes=[pltpu.SMEM((others, LANES), jnp.int32)] * parts
+        + [pltpu.VMEM((sides, LANES // GROUP, 48, LANES), BF16)] * parts
+        + [pltpu.VMEM((2 * LANES, LANES), BF16)] * parts
+        + [
             pltpu.VMEM((nodes + 2 * halo, 2, LANES), BF16),
             pltpu.VMEM((3, LANES, LANES), F32),
-            pltpu.SemaphoreType.DMA((2,)),
+            pltpu.SemaphoreType.DMA((parts, 3)),
             pltpu.SemaphoreType.DMA((3,)),
         ],
-        cost_estimate=pl.CostEstimate(flops=2 * nodes * 6 * left.shape[2] * LANES, bytes_accessed=left.size * 2, transcendentals=0),
+        cost_estimate=pl.CostEstimate(flops=2 * nodes * 6 * sides * LANES * LANES, bytes_accessed=left.size * 2, transcendentals=0),
         name="mass_rows",
-    )(tile_slot, table, from_lower, from_upper, left)
+    )(tile_slot, table, from_lower, from_upper, left, table.reshape(2 * nodes, LANES))
 
 
 def summed(value, axis):

time: 69.5 us -> 62.3 us (0.90); the launches traced: 68.2 us -> 62 us
  Pallas kernels: 39.9 us -> 33.7 us
    pallas_call x1, Pallas kernels: 11.2 us -> 5.61 us  [spread_tiles(): pl.pallas_call(spread_kernel, grid=(node_count // step,), in_specs=[pl.Bl...]
  transfers between devices with their start and end apart: 7 -> 7, of which waited for: 4 -> 4; matrix products, arithmetic and copies ran while one was open for 0% -> 0% of each run, Pallas kernels for 59% -> 54%
where the time goes in v3:
time: 62.3 us; the launch traced here: 62 us
  Pallas kernels  33.7 us (54%)
  starting transfers between devices  16.5 us (26%)
  waiting for transfers between devices  6.55 us (11%)
  matrix products  2.97 us (5%)
  other arithmetic  0.79 us (1%)
  local copies, waits for them, and re-layouts  0.78 us (1%)
  between operations  0.72 us (1%)
    pallas_call x1, Pallas kernels, apply_mass(): pl.pallas_call(functools.partial(mass_kernel, parts), grid=(blocks // par...  24.6 us
    ppermute x4, starting transfers between devices, summed(): lax.ppermute(value, axis, [(source, source ^ step) for source in range(co...  10.7 us
    ppermute x4, waiting for transfers between devices, summed(): lax.ppermute(value, axis, [(source, source ^ step) for source in range(co...  6.55 us
    pallas_call x1, Pallas kernels, spread_tiles(): pl.pallas_call(spread_kernel, grid=(node_count // step,), in_specs=[pl.Bl...  5.61 us
    pallas_call x1, Pallas kernels, node_table(): pl.pallas_call(table_kernel, in_specs=[vmem, smem, smem], out_specs=[vmem...  3.47 us
    ppermute x1, starting transfers between devices, body(): lax.ppermute(by_comp, 'col', [(source, (source + shift) % cols) for sourc...  3.06 us
    dot_general x2, matrix products, body(): lax.dot_general(mass_rows, part, (((0, 2), (0, 2)), ((), ())), preferred_...  2.97 us
    ppermute x2, starting transfers between devices, shifted(): lax.ppermute(value, axis, [(source, source + steps) for source in range(l...  2.76 us
  transfers between devices with their start and end apart: 7, of which 4 were waited for; matrix products, arithmetic and copies ran while one was open for 0% of the time, Pallas kernels for 54%

profile of v3, /device:TPU:0, one launch (start us, length us, event | category | flops | bytes accessed | tf_op | source)
XLA Modules:
  0.0 62.0 jit_solution(6174847236763795896)
XLA Ops:
  0.6 3.1 %collective-permute-start.2 = (bf16[3,64,2048]{2,1,0:T(8,128)(2,1)}, bf16[3,64,2048]{2,1,0:T(8,128)(2,1)S(1)}, u32[]{:S(2)}, u32[]{:S(2)}) collective-permute-start(bf16[3,64,2048]{2,1,0:T(8,128)(2,1)} %bitcast.21), channel_id=1, source_target_pairs={{0,1},{1,0},{2,3},{3,2},{4,5},{5,4},{6,7},{7,6},{8,9},{9,8},{10,11... | collective-permute-start | bytes 2359304 | tf_op jit(solution)/shard_map/ppermute | solution.py:224
  3.7 3.5 %node_table.1 = (bf16[2048,2,128]{2,1,0:T(2,128)(2,1)}, bf16[512,2,128]{2,1,0:T(2,128)(2,1)}, bf16[512,2,128]{2,1,0:T(2,128)(2,1)}) custom-call(bf16[3,64,2048]{2,1,0:T(8,128)(2,1)} %bitcast.22, s32[512]{0:T(512)} %up_ref.1, s32[512]{0:T(512)} %down_ref.1), custom_call_target="tpu_custom_call" | custom-call | tf_op jit(solution)/shard_map/node_table/pallas_call | solution.py:50
  7.2 1.5 %collective-permute-start = (bf16[512,2,128]{2,1,0:T(2,128)(2,1)}, bf16[512,2,128]{2,1,0:T(2,128)(2,1)S(1)}, u32[]{:S(2)}, u32[]{:S(2)}) collective-permute-start(bf16[512,2,128]{2,1,0:T(2,128)(2,1)} %get-tuple-element.6), channel_id=1, source_target_pairs={{0,2},{2,4},{4,6},{6,8},{8,10},{10,12},{12,14},{14,16},{16,18},{18... | collective-permute-start | bytes 786440 | tf_op jit(solution)/shard_map/ppermute | solution.py:21
  8.6 1.3 %collective-permute-start.1 = (bf16[512,2,128]{2,1,0:T(2,128)(2,1)}, bf16[512,2,128]{2,1,0:T(2,128)(2,1)S(1)}, u32[]{:S(2)}, u32[]{:S(2)}) collective-permute-start(bf16[512,2,128]{2,1,0:T(2,128)(2,1)} %get-tuple-element.7), channel_id=1, source_target_pairs={{2,0},{4,2},{6,4},{8,6},{10,8},{12,10},{14,12},{16,14},{18,16},{20... | collective-permute-start | bytes 786440 | tf_op jit(solution)/shard_map/ppermute | solution.py:21
  9.9 5.6 %spread_tiles.1.left_hbm = bf16[2,256,48,128]{3,2,1,0:T(8,128)(2,1)} custom-call(bf16[144,2048]{1,0:T(8,128)(2,1)} %bitcast.23, bf16[144,1536]{1,0:T(8,128)(2,1)} %constant.11.clone.spread_ref), custom_call_target="tpu_custom_call" | custom-call | flops 905969664 | bytes 6291456 | tf_op jit(solution)/shard_map/spread_tiles/pallas_call | solution.py:98
  15.5 0.0 copy-start
  15.5 0.0 collective-permute-done.lower_hbm
  15.6 0.0 copy-start.1
  15.6 0.0 collective-permute-done.1.upper_hbm
  15.6 0.0 copy-start.2
  15.6 0.7 %copy-done.1 = bf16[512,2,128]{2,1,0:T(2,128)(2,1)} copy-done((bf16[512,2,128]{2,1,0:T(2,128)(2,1)}, bf16[512,2,128]{2,1,0:T(2,128)(2,1)S(1)}, u32[]{:S(2)}) %copy-start.1) | copy-done | bytes 262168
  16.2 0.1 copy-done.2
  16.3 24.6 %mass_rows.1 = bf16[3,64,2048]{2,1,0:T(8,128)(2,1)} custom-call(s32[15,2048]{1,0:T(8,128)} %slot_hbm.1, bf16[2048,2,128]{2,1,0:T(2,128)(2,1)} %get-tuple-element.5.table_hbm, bf16[512,2,128]{2,1,0:T(2,128)(2,1)} %copy-done.1, bf16[512,2,128]{2,1,0:T(2,128)(2,1)} %copy-done.2, bf16[2,256,48,128]{3,2,1,0:T(8,128)(2,1)} %spread_tiles.1.left_hbm, ...), custom_call_target="tpu_custom_call" | custom-call | flops 805306368 | bytes 6291456 | tf_op jit(solution)/shard_map/mass_rows/pallas_call | solution.py:180
  41.0 0.0 collective-permute-done.2
  41.0 1.5 %convolution_bitcast_fusion = f32[64,64]{1,0:T(8,128)S(1)} fusion(bf16[3,64,2048]{2,1,0:T(8,128)(2,1)} %mass_rows.1, bf16[3,64,2048]{2,1,0:T(8,128)(2,1)S(1)} %collective-permute-done.2), kind=kOutput, calls=%fused_computation | convolution fusion | flops 50331648 | bytes 1589248 | tf_op jit(solution)/shard_map/dot_general | solution.py:239
  42.5 0.0 copy-done
  42.5 1.5 %broadcast_select_fusion.1 = (f32[64,64]{1,0:T(8,128)S(1)}, f32[64,64]{1,0:T(8,128)S(1)}) fusion(f32[64,64]{1,0:T(8,128)S(1)} %convolution_bitcast_fusion, pred[]{:T(512)S(6)} %eq.3, bf16[3,64,2048]{2,1,0:T(8,128)(2,1)} %mass_rows.1, bf16[64,3,2048]{2,0,1:T(8,128)(2,1)S(1)} %copy-done), kind=kOutput, calls=%fused_computation.5 | convolution fusion | flops 50339840 | bytes 1622017 | tf_op jit(solution)/shard_map/dot_general | solution.py:239
  44.0 0.1 pad_maximum_fusion
  44.1 3.2 %collective-permute-start.3 = (f32[64,128]{1,0:T(8,128)S(1)}, f32[64,128]{1,0:T(8,128)S(1)}, u32[]{:S(2)}, u32[]{:S(2)}) collective-permute-start(f32[64,128]{1,0:T(8,128)S(1)} %pad_maximum_fusion), channel_id=1, source_target_pairs={{0,2},{2,0},{4,6},{6,4},{8,10},{10,8},{12,14},{14,12},{16,18},{18,... | collective-permute-start | bytes 98312 | tf_op jit(solution)/shard_map/ppermute | solution.py:206
  47.3 0.9 %collective-permute-done.3 = f32[64,128]{1,0:T(8,128)S(1)} collective-permute-done((f32[64,128]{1,0:T(8,128)S(1)}, f32[64,128]{1,0:T(8,128)S(1)}, u32[]{:S(2)}, u32[]{:S(2)}) %collective-permute-start.3) | collective-permute-done | bytes 32800 | tf_op jit(solution)/shard_map/ppermute | solution.py:206
  48.1 0.1 fusion.4
  48.2 2.2 %collective-permute-start.4 = (f32[64,128]{1,0:T(8,128)S(1)}, f32[64,128]{1,0:T(8,128)S(1)}, u32[]{:S(2)}, u32[]{:S(2)}) collective-permute-start(f32[64,128]{1,0:T(8,128)S(1)} %fusion.4), channel_id=1, source_target_pairs={{0,4},{2,6},{4,0},{6,2},{8,12},{10,14},{12,8},{14,10},{16,20},{18,... | collective-permute-start | bytes 98312 | tf_op jit(solution)/shard_map/ppermute | solution.py:206
  50.4 1.9 %collective-permute-done.4 = f32[64,128]{1,0:T(8,128)S(1)} collective-permute-done((f32[64,128]{1,0:T(8,128)S(1)}, f32[64,128]{1,0:T(8,128)S(1)}, u32[]{:S(2)}, u32[]{:S(2)}) %collective-permute-start.4) | collective-permute-done | bytes 32800 | tf_op jit(solution)/shard_map/ppermute | solution.py:206
  52.3 2.3 %collective-permute-start.5 = (f32[64,128]{1,0:T(8,128)S(1)}, f32[64,128]{1,0:T(8,128)S(1)}, u32[]{:S(2)}, u32[]{:S(2)}) collective-permute-start(f32[64,128]{1,0:T(8,128)S(1)} %add.13), channel_id=1, source_target_pairs={{0,8},{2,10},{4,12},{6,14},{8,0},{10,2},{12,4},{14,6},{16,24},{18,... | collective-permute-start | bytes 98312 | tf_op jit(solution)/shard_map/ppermute | solution.py:206
  54.6 1.9 %collective-permute-done.5 = f32[64,128]{1,0:T(8,128)S(1)} collective-permute-done((f32[64,128]{1,0:T(8,128)S(1)}, f32[64,128]{1,0:T(8,128)S(1)}, u32[]{:S(2)}, u32[]{:S(2)}) %collective-permute-start.5) | collective-permute-done | bytes 32800 | tf_op jit(solution)/shard_map/ppermute | solution.py:206
  56.5 3.0 %collective-permute-start.6 = (f32[64,128]{1,0:T(8,128)S(1)}, f32[64,128]{1,0:T(8,128)S(1)}, u32[]{:S(2)}, u32[]{:S(2)}) collective-permute-start(f32[64,128]{1,0:T(8,128)S(1)} %add.14), channel_id=1, source_target_pairs={{0,16},{2,18},{4,20},{6,22},{8,24},{10,26},{12,28},{14,30},{16,0},... | collective-permute-start | bytes 98312 | tf_op jit(solution)/shard_map/ppermute | solution.py:206
  59.5 1.9 %collective-permute-done.6 = f32[64,128]{1,0:T(8,128)S(1)} collective-permute-done((f32[64,128]{1,0:T(8,128)S(1)}, f32[64,128]{1,0:T(8,128)S(1)}, u32[]{:S(2)}, u32[]{:S(2)}) %collective-permute-start.6) | collective-permute-done | bytes 32800 | tf_op jit(solution)/shard_map/ppermute | solution.py:206
  61.4 0.6 %multiply_bitcast_fusion = f32[128,64]{0,1:T(8,128)} fusion(f32[64,128]{1,0:T(8,128)S(1)} %add.14, f32[64,128]{1,0:T(8,128)S(1)} %collective-permute-done.6), kind=kLoop, calls=%fused_computation.3 | loop fusion | flops 16384 | bytes 98304 | tf_op jit(solution)/shard_map/transpose | solution.py:241
  (2 shorter events, 0.0 us)
Async XLA Ops:
  0.6 40.3 %collective-permute-start.2 = (bf16[3,64,2048]{2,1,0:T(8,128)(2,1)}, bf16[3,64,2048]{2,1,0:T(8,128)(2,1)S(1)}, u32[]{:S(2)}, u32[]{:S(2)}) collective-permute-start(bf16[3,64,2048]{2,1,0:T(8,128)(2,1)} %bitcast.21), channel_id=1, source_target_pairs={{0,1},{1,0},{2,3},{3,2},{4,5},{5,4},{6,7},{7,6},{8,9},{9,8},{10,11... | collective-permute-start | bytes 2359304 | tf_op jit(solution)/shard_map/ppermute | solution.py:224
  7.2 8.4 %collective-permute-start = (bf16[512,2,128]{2,1,0:T(2,128)(2,1)}, bf16[512,2,128]{2,1,0:T(2,128)(2,1)S(1)}, u32[]{:S(2)}, u32[]{:S(2)}) collective-permute-start(bf16[512,2,128]{2,1,0:T(2,128)(2,1)} %get-tuple-element.6), channel_id=1, source_target_pairs={{0,2},{2,4},{4,6},{6,8},{8,10},{10,12},{12,14},{14,16},{16,18},{18... | collective-permute-start | bytes 786440 | tf_op jit(solution)/shard_map/ppermute | solution.py:21
  8.6 6.9 %collective-permute-start.1 = (bf16[512,2,128]{2,1,0:T(2,128)(2,1)}, bf16[512,2,128]{2,1,0:T(2,128)(2,1)S(1)}, u32[]{:S(2)}, u32[]{:S(2)}) collective-permute-start(bf16[512,2,128]{2,1,0:T(2,128)(2,1)} %get-tuple-element.7), channel_id=1, source_target_pairs={{2,0},{4,2},{6,4},{8,6},{10,8},{12,10},{14,12},{16,14},{18,16},{20... | collective-permute-start | bytes 786440 | tf_op jit(solution)/shard_map/ppermute | solution.py:21
  15.5 26.9 %copy-start = (bf16[64,3,2048]{2,0,1:T(8,128)(2,1)S(1)}, bf16[64,3,2048]{2,0,1:T(8,128)(2,1)}, u32[]{:S(2)}) copy-start(bf16[64,3,2048]{2,0,1:T(8,128)(2,1)} %param.6) | copy-start | bytes 2359300
  15.6 0.7 %copy-start.1 = (bf16[512,2,128]{2,1,0:T(2,128)(2,1)}, bf16[512,2,128]{2,1,0:T(2,128)(2,1)S(1)}, u32[]{:S(2)}) copy-start(bf16[512,2,128]{2,1,0:T(2,128)(2,1)S(1)} %collective-permute-done.lower_hbm) | copy-start | bytes 786436
  15.6 0.8 %copy-start.2 = (bf16[512,2,128]{2,1,0:T(2,128)(2,1)}, bf16[512,2,128]{2,1,0:T(2,128)(2,1)S(1)}, u32[]{:S(2)}) copy-start(bf16[512,2,128]{2,1,0:T(2,128)(2,1)S(1)} %collective-permute-done.1.upper_hbm) | copy-start | bytes 786436
  44.1 4.1 %collective-permute-start.3 = (f32[64,128]{1,0:T(8,128)S(1)}, f32[64,128]{1,0:T(8,128)S(1)}, u32[]{:S(2)}, u32[]{:S(2)}) collective-permute-start(f32[64,128]{1,0:T(8,128)S(1)} %pad_maximum_fusion), channel_id=1, source_target_pairs={{0,2},{2,0},{4,6},{6,4},{8,10},{10,8},{12,14},{14,12},{16,18},{18,... | collective-permute-start | bytes 98312 | tf_op jit(solution)/shard_map/ppermute | solution.py:206
  48.2 4.1 %collective-permute-start.4 = (f32[64,128]{1,0:T(8,128)S(1)}, f32[64,128]{1,0:T(8,128)S(1)}, u32[]{:S(2)}, u32[]{:S(2)}) collective-permute-start(f32[64,128]{1,0:T(8,128)S(1)} %fusion.4), channel_id=1, source_target_pairs={{0,4},{2,6},{4,0},{6,2},{8,12},{10,14},{12,8},{14,10},{16,20},{18,... | collective-permute-start | bytes 98312 | tf_op jit(solution)/shard_map/ppermute | solution.py:206
  52.3 4.2 %collective-permute-start.5 = (f32[64,128]{1,0:T(8,128)S(1)}, f32[64,128]{1,0:T(8,128)S(1)}, u32[]{:S(2)}, u32[]{:S(2)}) collective-permute-start(f32[64,128]{1,0:T(8,128)S(1)} %add.13), channel_id=1, source_target_pairs={{0,8},{2,10},{4,12},{6,14},{8,0},{10,2},{12,4},{14,6},{16,24},{18,... | collective-permute-start | bytes 98312 | tf_op jit(solution)/shard_map/ppermute | solution.py:206
  56.5 4.9 %collective-permute-start.6 = (f32[64,128]{1,0:T(8,128)S(1)}, f32[64,128]{1,0:T(8,128)S(1)}, u32[]{:S(2)}, u32[]{:S(2)}) collective-permute-start(f32[64,128]{1,0:T(8,128)S(1)} %add.14), channel_id=1, source_target_pairs={{0,16},{2,18},{4,20},{6,22},{8,24},{10,26},{12,28},{14,30},{16,0},... | collective-permute-start | bytes 98312 | tf_op jit(solution)/shard_map/ppermute | solution.py:206

commit v4 on v3

--- a/solution.py
+++ b/solution.py
@@ -11,21 +11,22 @@
 LANES = 128
 HALF = LANES // 2
 GROUP = 8
+VMEM_BYTES = 20 * 2**20
 BF16 = jnp.bfloat16
 F32 = jnp.float32
 
 
-def shifted(value, axis, steps):
+def swap(value, axis, first):
     count = lax.axis_size(axis)
-    leading, last = (max(0, -steps), min(count, count - steps))
-    return lax.ppermute(value, axis, [(source, source + steps) for source in range(leading, last)])
+    pairs = [(low, low + 1) for low in range(first, count - 1, 2)]
+    return lax.ppermute(value, axis, pairs + [(high, low) for low, high in pairs])
 
 
 def nt_dot(left, right):
     return lax.dot_general(left, right, (((1,), (1,)), ((), ())), preferred_element_type=F32)
 
 
-def table_kernel(snap_ref, up_ref, down_ref, table_ref, to_upper_ref, to_lower_ref):
+def table_kernel(snap_ref, near_ref, far_ref, table_ref, to_near_ref, to_far_ref):
     node_count = snap_ref.shape[2]
     row = lax.broadcasted_iota(jnp.int32, (2 * LANES, 2 * LANES), 0)
     col = lax.broadcasted_iota(jnp.int32, (2 * LANES, 2 * LANES), 1)
@@ -37,14 +38,14 @@
         second = jnp.concatenate([comps[1], empty], axis=0)
         rows = nt_dot(pick, jnp.concatenate([first, second], axis=1)).astype(BF16)
         table_ref[start : start + LANES] = rows.reshape(LANES, 2, LANES)
-    for out_ref, list_ref in ((to_upper_ref, up_ref), (to_lower_ref, down_ref)):
+    for out_ref, list_ref in ((to_near_ref, near_ref), (to_far_ref, far_ref)):
         for entry in range(out_ref.shape[0]):
             out_ref[entry] = table_ref[list_ref[entry]]
 
 
-def node_table(snap, send_up, send_down):
+def node_table(snap, near_list, far_list):
     node_count = snap.shape[2]
-    halo = send_up.shape[0]
+    halo = near_list.shape[0]
     smem = pl.BlockSpec(memory_space=pltpu.SMEM)
     vmem = pl.BlockSpec(memory_space=pltpu.VMEM)
     return pl.pallas_call(
@@ -56,8 +57,9 @@
             jax.ShapeDtypeStruct((halo, 2, LANES), BF16),
             jax.ShapeDtypeStruct((halo, 2, LANES), BF16),
         ],
+        compiler_params=pltpu.CompilerParams(vmem_limit_bytes=VMEM_BYTES),
         name="node_table",
-    )(snap, send_up, send_down)
+    )(snap, near_list, far_list)
 
 
 def spread_matrix(tiles):
@@ -105,17 +107,18 @@
         out_specs=pl.BlockSpec((depth // LANES, step // GROUP, 48, LANES), lambda i: (0, i, 0, 0)),
         out_shape=jax.ShapeDtypeStruct((depth // LANES, node_count // GROUP, 48, LANES), BF16),
         cost_estimate=pl.CostEstimate(flops=2 * node_count * tiles * 9 * 6 * depth, bytes_accessed=node_count * 6 * depth * 2, transcendentals=0),
+        compiler_params=pltpu.CompilerParams(vmem_limit_bytes=VMEM_BYTES),
         name="spread_tiles",
     )(jnp.transpose(mass_tiles, (1, 2, 0, 3)).reshape(tiles * 9, node_count), spread)
 
 
-def mass_kernel(parts, slot_hbm, table_hbm, lower_hbm, upper_hbm, left_hbm, own_hbm, out_ref, *scratch):
+def mass_kernel(parts, slot_hbm, table_hbm, near_in, far_in, left_hbm, own_hbm, out_ref, again_ref, *scratch):
     slot_refs, left_refs, own_refs = (scratch[kind * parts : (kind + 1) * parts] for kind in range(3))
     table_ref, turn_ref, sem, fill_sem = scratch[3 * parts :]
     step, steps = pl.program_id(0), pl.num_programs(0)
     others = slot_hbm.shape[0]
     sides = left_hbm.shape[0]
-    nodes, halo = table_hbm.shape[0], lower_hbm.shape[0]
+    nodes, halo = table_hbm.shape[0], near_in.shape[0]
     groups = LANES // GROUP
     low_half = lax.broadcasted_iota(jnp.int32, (GROUP, LANES), 1) < HALF
 
@@ -131,10 +134,11 @@
 
     @pl.when(step == 0)
     def _():
+        odd = lax.rem(lax.axis_index("dom"), 2)
         fills = [
             pltpu.make_async_copy(table_hbm, table_ref.at[pl.ds(0, nodes)], fill_sem.at[0]),
-            pltpu.make_async_copy(lower_hbm, table_ref.at[pl.ds(nodes, halo)], fill_sem.at[1]),
-            pltpu.make_async_copy(upper_hbm, table_ref.at[pl.ds(nodes + halo, halo)], fill_sem.at[2]),
+            pltpu.make_async_copy(near_in, table_ref.at[pl.ds(nodes + (1 - odd) * halo, halo)], fill_sem.at[1]),
+            pltpu.make_async_copy(far_in, table_ref.at[pl.ds(nodes + odd * halo, halo)], fill_sem.at[2]),
         ]
         for copy in (*fetches(0, 0), *fills):
             copy.start()
@@ -167,11 +171,13 @@
 
         for comp in range(3):
             turned = turn_ref[comp].T
-            out_ref[comp, :, part * LANES : (part + 1) * LANES] = (turned[:HALF] + turned[HALF:]).astype(BF16)
-
-
-def apply_mass(table, from_lower, from_upper, left, tile_slot):
-    nodes, halo = table.shape[0], from_lower.shape[0]
+            rounded = (turned[:HALF] + turned[HALF:]).astype(BF16)
+            out_ref[comp, :, part * LANES : (part + 1) * LANES] = rounded
+            again_ref[comp, :, part * LANES : (part + 1) * LANES] = rounded
+
+
+def apply_mass(table, from_near, from_far, left, tile_slot):
+    nodes, halo = table.shape[0], from_near.shape[0]
     others = tile_slot.shape[0]
     sides = left.shape[0]
     blocks = nodes // LANES
@@ -180,9 +186,9 @@
     return pl.pallas_call(
         functools.partial(mass_kernel, parts),
         grid=(blocks // parts,),
-        in_specs=[any_space] * 6,
-        out_specs=pl.BlockSpec((3, HALF, parts * LANES), lambda i: (0, 0, i)),
-        out_shape=jax.ShapeDtypeStruct((3, HALF, nodes), BF16),
+        in_specs=[any_space] * 2 + [pl.BlockSpec(memory_space=pltpu.VMEM)] * 2 + [any_space] * 2,
+        out_specs=[pl.BlockSpec((3, HALF, parts * LANES), lambda i: (0, 0, i))] * 2,
+        out_shape=[jax.ShapeDtypeStruct((3, HALF, nodes), BF16)] * 2,
         scratch_shapes=[pltpu.SMEM((others, LANES), jnp.int32)] * parts
         + [pltpu.VMEM((sides, LANES // GROUP, 48, LANES), BF16)] * parts
         + [pltpu.VMEM((2 * LANES, LANES), BF16)] * parts
@@ -193,8 +199,9 @@
             pltpu.SemaphoreType.DMA((3,)),
         ],
         cost_estimate=pl.CostEstimate(flops=2 * nodes * 6 * sides * LANES * LANES, bytes_accessed=left.size * 2, transcendentals=0),
+        compiler_params=pltpu.CompilerParams(vmem_limit_bytes=VMEM_BYTES),
         name="mass_rows",
-    )(tile_slot, table, from_lower, from_upper, left, table.reshape(2 * nodes, LANES))
+    )(tile_slot, table, from_near, from_far, left, table.reshape(2 * nodes, LANES))
 
 
 def summed(value, axis):
@@ -225,18 +232,19 @@
         for shift in range(1, cols)
     ]
     left = spread_tiles(mass_tiles)
+    even = lax.rem(lax.axis_index("dom"), 2) == 0
+    near_list, far_list = jnp.where(even, send_up, send_down), jnp.where(even, send_down, send_up)
     pieces = []
     for start in range(0, snap_count, HALF):
         piece = by_comp[:, start : start + HALF]
         size = piece.shape[1]
         if size < HALF:
             piece = jnp.pad(piece, ((0, 0), (0, HALF - size), (0, 0)))
-        table, to_upper, to_lower = node_table(piece, send_up, send_down)
-        from_lower = shifted(to_upper, "dom", 1)
-        from_upper = shifted(to_lower, "dom", -1)
-        pieces.append(apply_mass(table, from_lower, from_upper, left, tile_slot)[:, :size])
-    mass_rows = pieces[0] if len(pieces) == 1 else jnp.concatenate(pieces, axis=1)
-    blocks = [lax.dot_general(mass_rows, part, (((0, 2), (0, 2)), ((), ())), preferred_element_type=F32) for part in parts]
+        table, to_near, to_far = node_table(piece, near_list, far_list)
+        both = apply_mass(table, swap(to_near, "dom", 0), swap(to_far, "dom", 1), left, tile_slot)
+        pieces.append([rows[:, :size] for rows in both])
+    mass_rows, again = pieces[0] if len(pieces) == 1 else [jnp.concatenate(rows, axis=1) for rows in zip(*pieces)]
+    blocks = [lax.dot_general(again, part, (((0, 2), (0, 2)), ((), ())), preferred_element_type=F32) for part in parts]
     total = summed(in_order(blocks), "dom") / (3.0 * node_count * lax.axis_size("dom"))
     return jnp.transpose(mass_rows, (1, 0, 2)), total.T
 

time: 62.3 us -> 60.4 us (0.970)
  local copies, waits for them, and re-layouts: 0.78 us -> 3.21 us
  Pallas kernels: 33.7 us -> 31.4 us
  matrix products: 2.97 us -> 0.71 us
  other arithmetic: 0.79 us -> 1.49 us
    pallas_call x1, Pallas kernels: 5.61 us -> 2.93 us  [spread_tiles(): pl.pallas_call(spread_kernel, grid=(node_count // step,), in_specs=[pl.Bl...]
    unnamed x6 -> x10, local copies, waits for them, and re-layouts: 0.78 us -> 3.21 us
    dot_general x2, matrix products: 2.97 us -> 0.71 us  [body(): lax.dot_general(again, part, (((0, 2), (0, 2)), ((), ())), preferred_elem...]
    ppermute x2, starting transfers between devices: 2.76 us -> 0.75 us  [swap(): lax.ppermute(value, axis, pairs + [(high, low) for low, high in pairs])]
    pallas_call x1, Pallas kernels: 24.6 us -> 26.5 us  [apply_mass(): pl.pallas_call(functools.partial(mass_kernel, parts), grid=(blocks // par...]
    ppermute x4, starting transfers between devices: 10.7 us -> 12.1 us  [summed(): lax.ppermute(value, axis, [(source, source ^ step) for source in range(co...]
    pallas_call x1, Pallas kernels: 3.47 us -> 2.02 us  [node_table(): pl.pallas_call(table_kernel, in_specs=[vmem, smem, smem], out_specs=[vmem...]
    select_n x0 -> x1, other arithmetic: none -> 0.7 us  [body(): jnp.where(even, send_down, send_up)]
  transfers between devices with their start and end apart: 7 -> 7, of which waited for: 4 -> 4; matrix products, arithmetic and copies ran while one was open for 0% -> 1% of each run, Pallas kernels for 54% -> 52%
where the time goes in v4:
time: 60.4 us; the launch traced here: 60.1 us
  Pallas kernels  31.4 us (52%)
  starting transfers between devices  15.9 us (26%)
  waiting for transfers between devices  6.55 us (11%)
  local copies, waits for them, and re-layouts  3.21 us (5%)
  other arithmetic  1.49 us (2%)
  between operations  0.76 us (1%)
  matrix products  0.71 us (1%)
    pallas_call x1, Pallas kernels, apply_mass(): pl.pallas_call(functools.partial(mass_kernel, parts), grid=(blocks // par...  26.5 us
    ppermute x4, starting transfers between devices, summed(): lax.ppermute(value, axis, [(source, source ^ step) for source in range(co...  12.1 us
    ppermute x4, waiting for transfers between devices, summed(): lax.ppermute(value, axis, [(source, source ^ step) for source in range(co...  6.54 us
    unnamed x10, local copies, waits for them, and re-layouts  3.21 us
    ppermute x1, starting transfers between devices, body(): lax.ppermute(by_comp, 'col', [(source, (source + shift) % cols) for sourc...  3.06 us
    pallas_call x1, Pallas kernels, spread_tiles(): pl.pallas_call(spread_kernel, grid=(node_count // step,), in_specs=[pl.Bl...  2.93 us
    pallas_call x1, Pallas kernels, node_table(): pl.pallas_call(table_kernel, in_specs=[vmem, smem, smem], out_specs=[vmem...  2.02 us
  transfers between devices with their start and end apart: 7, of which 4 were waited for; matrix products, arithmetic and copies ran while one was open for 1% of the time, Pallas kernels for 52%

profile of v4, /device:TPU:0, one launch (start us, length us, event | category | flops | bytes accessed | tf_op | source)
XLA Modules:
  0.0 60.1 jit_solution(10474024408514568735)
XLA Ops:
  0.6 3.1 %collective-permute-start.2 = (bf16[3,64,2048]{2,1,0:T(8,128)(2,1)}, bf16[3,64,2048]{2,1,0:T(8,128)(2,1)S(1)}, u32[]{:S(2)}, u32[]{:S(2)}) collective-permute-start(bf16[3,64,2048]{2,1,0:T(8,128)(2,1)} %bitcast.20), channel_id=1, source_target_pairs={{0,1},{1,0},{2,3},{3,2},{4,5},{5,4},{6,7},{7,6},{8,9},{9,8},{10,11... | collective-permute-start | bytes 2359304 | tf_op jit(solution)/shard_map/ppermute | solution.py:231
  3.7 0.7 %broadcast_select_fusion.2 = (s32[512]{0:T(512)S(1)}, s32[512]{0:T(512)S(1)}) fusion(s32[512]{0:T(512)} %param.10, s32[512]{0:T(512)} %param.9, pred[]{:T(512)S(6)} %eq.6), kind=kLoop, calls=%fused_computation.6 | loop fusion | flops 1024 | bytes 8193 | tf_op jit(solution)/shard_map/jit(_where)/select_n | solution.py:236
  4.4 0.0 copy-start
  4.4 1.1 %copy-done = bf16[64,3,2048]{2,0,1:T(8,128)(2,1)S(1)} copy-done((bf16[64,3,2048]{2,0,1:T(8,128)(2,1)S(1)}, bf16[64,3,2048]{2,0,1:T(8,128)(2,1)}, u32[]{:S(2)}) %copy-start) | copy-done | bytes 786456
  5.5 0.0 copy-start.4
  5.5 2.0 %node_table.1 = (bf16[2048,2,128]{2,1,0:T(2,128)(2,1)S(1)}, bf16[512,2,128]{2,1,0:T(2,128)(2,1)S(1)}, bf16[512,2,128]{2,1,0:T(2,128)(2,1)S(1)}) custom-call(bf16[3,64,2048]{2,1,0:T(8,128)(2,1)S(1)} %bitcast.21, s32[512]{0:T(512)S(1)} %get-tuple-element.15.near_ref, s32[512]{0:T(512)S(1)} %get-tuple-element.14.far_ref), custom_call_target="tpu_custom_call" | custom-call | tf_op jit(solution)/shard_map/node_table/pallas_call | solution.py:51
  7.6 0.1 collective-permute-start
  7.6 0.7 %collective-permute-start.1 = (bf16[512,2,128]{2,1,0:T(2,128)(2,1)S(1)}, bf16[512,2,128]{2,1,0:T(2,128)(2,1)S(1)}, u32[]{:S(2)}, u32[]{:S(2)}) collective-permute-start(bf16[512,2,128]{2,1,0:T(2,128)(2,1)S(1)} %get-tuple-element.9), channel_id=1, source_target_pairs={{2,4},{6,8},{10,12},{14,16},{18,20},{22,24},{26,28},{4,2},{8,6},{1... | collective-permute-start | bytes 786440 | tf_op jit(solution)/shard_map/ppermute | solution.py:22
  8.3 0.0 copy-start.2
  8.3 1.1 %copy-done.2 = bf16[16,3,3,2048]{3,0,2,1:T(8,128)(2,1)S(1)} copy-done((bf16[16,3,3,2048]{3,0,2,1:T(8,128)(2,1)S(1)}, bf16[16,3,3,2048]{3,0,2,1:T(8,128)(2,1)}, u32[]{:S(2)}) %copy-start.2) | copy-done | bytes 589848
  9.4 1.0 %copy-done.3 = bf16[144,1536]{1,0:T(8,128)(2,1)S(1)} copy-done((bf16[144,1536]{1,0:T(8,128)(2,1)S(1)}, bf16[144,1536]{1,0:T(8,128)(2,1)}, u32[]{:S(2)}) %copy-start.3) | copy-done | bytes 442392
  10.4 2.9 %spread_tiles.1.left_hbm = bf16[2,256,48,128]{3,2,1,0:T(8,128)(2,1)S(1)} custom-call(bf16[144,2048]{1,0:T(8,128)(2,1)S(1)} %bitcast.22, bf16[144,1536]{1,0:T(8,128)(2,1)S(1)} %copy-done.3), custom_call_target="tpu_custom_call" | custom-call | flops 905969664 | bytes 6291456 | tf_op jit(solution)/shard_map/spread_tiles/pallas_call | solution.py:100
  13.3 0.0 copy-start.1
  13.4 0.0 collective-permute-done.near_in
  13.4 0.0 collective-permute-done.1.far_in
  13.4 0.0 copy-done.4
  13.4 26.5 %mass_rows.1 = (bf16[3,64,2048]{2,1,0:T(8,128)(2,1)}, bf16[3,64,2048]{2,1,0:T(8,128)(2,1)S(1)}) custom-call(s32[15,2048]{1,0:T(8,128)S(1)} %copy-done.4, bf16[2048,2,128]{2,1,0:T(2,128)(2,1)S(1)} %get-tuple-element.7.table_hbm, bf16[512,2,128]{2,1,0:T(2,128)(2,1)S(1)} %collective-permute-done.near_in, ...), custom_call_target="tpu_custom_call" | custom-call | flops 805306368 | bytes 6291456 | tf_op jit(solution)/shard_map/mass_rows/pallas_call | solution.py:186
  39.9 0.0 collective-permute-done.2
  39.9 0.4 convolution_bitcast_fusion
  40.2 0.0 copy-done.1
  40.3 0.4 broadcast_select_fusion.1
  40.6 0.1 pad_maximum_fusion
  40.7 3.8 %collective-permute-start.3 = (f32[64,128]{1,0:T(8,128)S(1)}, f32[64,128]{1,0:T(8,128)S(1)}, u32[]{:S(2)}, u32[]{:S(2)}) collective-permute-start(f32[64,128]{1,0:T(8,128)S(1)} %pad_maximum_fusion), channel_id=1, source_target_pairs={{0,2},{2,0},{4,6},{6,4},{8,10},{10,8},{12,14},{14,12},{16,18},{18,... | collective-permute-start | bytes 98312 | tf_op jit(solution)/shard_map/ppermute | solution.py:213
  44.5 0.9 %collective-permute-done.3 = f32[64,128]{1,0:T(8,128)S(1)} collective-permute-done((f32[64,128]{1,0:T(8,128)S(1)}, f32[64,128]{1,0:T(8,128)S(1)}, u32[]{:S(2)}, u32[]{:S(2)}) %collective-permute-start.3) | collective-permute-done | bytes 32800 | tf_op jit(solution)/shard_map/ppermute | solution.py:213
  45.4 0.1 fusion.4
  45.5 2.7 %collective-permute-start.4 = (f32[64,128]{1,0:T(8,128)S(1)}, f32[64,128]{1,0:T(8,128)S(1)}, u32[]{:S(2)}, u32[]{:S(2)}) collective-permute-start(f32[64,128]{1,0:T(8,128)S(1)} %fusion.4), channel_id=1, source_target_pairs={{0,4},{2,6},{4,0},{6,2},{8,12},{10,14},{12,8},{14,10},{16,20},{18,... | collective-permute-start | bytes 98312 | tf_op jit(solution)/shard_map/ppermute | solution.py:213
  48.2 1.9 %collective-permute-done.4 = f32[64,128]{1,0:T(8,128)S(1)} collective-permute-done((f32[64,128]{1,0:T(8,128)S(1)}, f32[64,128]{1,0:T(8,128)S(1)}, u32[]{:S(2)}, u32[]{:S(2)}) %collective-permute-start.4) | collective-permute-done | bytes 32800 | tf_op jit(solution)/shard_map/ppermute | solution.py:213
  50.1 2.6 %collective-permute-start.5 = (f32[64,128]{1,0:T(8,128)S(1)}, f32[64,128]{1,0:T(8,128)S(1)}, u32[]{:S(2)}, u32[]{:S(2)}) collective-permute-start(f32[64,128]{1,0:T(8,128)S(1)} %add.13), channel_id=1, source_target_pairs={{0,8},{2,10},{4,12},{6,14},{8,0},{10,2},{12,4},{14,6},{16,24},{18,... | collective-permute-start | bytes 98312 | tf_op jit(solution)/shard_map/ppermute | solution.py:213
  52.7 1.9 %collective-permute-done.5 = f32[64,128]{1,0:T(8,128)S(1)} collective-permute-done((f32[64,128]{1,0:T(8,128)S(1)}, f32[64,128]{1,0:T(8,128)S(1)}, u32[]{:S(2)}, u32[]{:S(2)}) %collective-permute-start.5) | collective-permute-done | bytes 32800 | tf_op jit(solution)/shard_map/ppermute | solution.py:213
  54.5 3.0 %collective-permute-start.6 = (f32[64,128]{1,0:T(8,128)S(1)}, f32[64,128]{1,0:T(8,128)S(1)}, u32[]{:S(2)}, u32[]{:S(2)}) collective-permute-start(f32[64,128]{1,0:T(8,128)S(1)} %add.14), channel_id=1, source_target_pairs={{0,16},{2,18},{4,20},{6,22},{8,24},{10,26},{12,28},{14,30},{16,0},... | collective-permute-start | bytes 98312 | tf_op jit(solution)/shard_map/ppermute | solution.py:213
  57.6 1.9 %collective-permute-done.6 = f32[64,128]{1,0:T(8,128)S(1)} collective-permute-done((f32[64,128]{1,0:T(8,128)S(1)}, f32[64,128]{1,0:T(8,128)S(1)}, u32[]{:S(2)}, u32[]{:S(2)}) %collective-permute-start.6) | collective-permute-done | bytes 32800 | tf_op jit(solution)/shard_map/ppermute | solution.py:213
  59.5 0.6 %multiply_bitcast_fusion = f32[128,64]{0,1:T(8,128)} fusion(f32[64,128]{1,0:T(8,128)S(1)} %add.14, f32[64,128]{1,0:T(8,128)S(1)} %collective-permute-done.6), kind=kLoop, calls=%fused_computation.3 | loop fusion | flops 16384 | bytes 98304 | tf_op jit(solution)/shard_map/transpose | solution.py:249
  (3 shorter events, 0.0 us)
Async XLA Ops:
  0.6 39.3 %collective-permute-start.2 = (bf16[3,64,2048]{2,1,0:T(8,128)(2,1)}, bf16[3,64,2048]{2,1,0:T(8,128)(2,1)S(1)}, u32[]{:S(2)}, u32[]{:S(2)}) collective-permute-start(bf16[3,64,2048]{2,1,0:T(8,128)(2,1)} %bitcast.20), channel_id=1, source_target_pairs={{0,1},{1,0},{2,3},{3,2},{4,5},{5,4},{6,7},{7,6},{8,9},{9,8},{10,11... | collective-permute-start | bytes 2359304 | tf_op jit(solution)/shard_map/ppermute | solution.py:231
  4.4 1.1 %copy-start = (bf16[64,3,2048]{2,0,1:T(8,128)(2,1)S(1)}, bf16[64,3,2048]{2,0,1:T(8,128)(2,1)}, u32[]{:S(2)}) copy-start(bf16[64,3,2048]{2,0,1:T(8,128)(2,1)} %param.6) | copy-start | bytes 2359300
  5.5 7.9 %copy-start.4 = (s32[15,2048]{1,0:T(8,128)S(1)}, s32[15,2048]{1,0:T(8,128)}, u32[]{:S(2)}) copy-start(s32[15,2048]{1,0:T(8,128)} %slot_hbm.1) | copy-start | bytes 368644
  7.6 5.8 %collective-permute-start = (bf16[512,2,128]{2,1,0:T(2,128)(2,1)S(1)}, bf16[512,2,128]{2,1,0:T(2,128)(2,1)S(1)}, u32[]{:S(2)}, u32[]{:S(2)}) collective-permute-start(bf16[512,2,128]{2,1,0:T(2,128)(2,1)S(1)} %get-tuple-element.8), channel_id=1, source_target_pairs={{0,2},{4,6},{8,10},{12,14},{16,18},{20,22},{24,26},{28,30},{2,0},{... | collective-permute-start | bytes 786440 | tf_op jit(solution)/shard_map/ppermute | solution.py:22
  7.6 5.7 %collective-permute-start.1 = (bf16[512,2,128]{2,1,0:T(2,128)(2,1)S(1)}, bf16[512,2,128]{2,1,0:T(2,128)(2,1)S(1)}, u32[]{:S(2)}, u32[]{:S(2)}) collective-permute-start(bf16[512,2,128]{2,1,0:T(2,128)(2,1)S(1)} %get-tuple-element.9), channel_id=1, source_target_pairs={{2,4},{6,8},{10,12},{14,16},{18,20},{22,24},{26,28},{4,2},{8,6},{1... | collective-permute-start | bytes 786440 | tf_op jit(solution)/shard_map/ppermute | solution.py:22
  8.3 1.1 %copy-start.2 = (bf16[16,3,3,2048]{3,0,2,1:T(8,128)(2,1)S(1)}, bf16[16,3,3,2048]{3,0,2,1:T(8,128)(2,1)}, u32[]{:S(2)}) copy-start(bf16[16,3,3,2048]{3,0,2,1:T(8,128)(2,1)} %param.7) | copy-start | bytes 1769476
  9.4 1.0 %copy-start.3 = (bf16[144,1536]{1,0:T(8,128)(2,1)S(1)}, bf16[144,1536]{1,0:T(8,128)(2,1)}, u32[]{:S(2)}) copy-start(bf16[144,1536]{1,0:T(8,128)(2,1)} %constant.19.clone.spread_ref) | copy-start | bytes 1327108
  13.3 26.9 %copy-start.1 = (bf16[64,3,2048]{2,0,1:T(8,128)(2,1)S(1)}, bf16[64,3,2048]{2,0,1:T(8,128)(2,1)}, u32[]{:S(2)}) copy-start(bf16[64,3,2048]{2,0,1:T(8,128)(2,1)} %param.6) | copy-start | bytes 2359300
  40.7 4.7 %collective-permute-start.3 = (f32[64,128]{1,0:T(8,128)S(1)}, f32[64,128]{1,0:T(8,128)S(1)}, u32[]{:S(2)}, u32[]{:S(2)}) collective-permute-start(f32[64,128]{1,0:T(8,128)S(1)} %pad_maximum_fusion), channel_id=1, source_target_pairs={{0,2},{2,0},{4,6},{6,4},{8,10},{10,8},{12,14},{14,12},{16,18},{18,... | collective-permute-start | bytes 98312 | tf_op jit(solution)/shard_map/ppermute | solution.py:213
  45.5 4.6 %collective-permute-start.4 = (f32[64,128]{1,0:T(8,128)S(1)}, f32[64,128]{1,0:T(8,128)S(1)}, u32[]{:S(2)}, u32[]{:S(2)}) collective-permute-start(f32[64,128]{1,0:T(8,128)S(1)} %fusion.4), channel_id=1, source_target_pairs={{0,4},{2,6},{4,0},{6,2},{8,12},{10,14},{12,8},{14,10},{16,20},{18,... | collective-permute-start | bytes 98312 | tf_op jit(solution)/shard_map/ppermute | solution.py:213
  50.1 4.4 %collective-permute-start.5 = (f32[64,128]{1,0:T(8,128)S(1)}, f32[64,128]{1,0:T(8,128)S(1)}, u32[]{:S(2)}, u32[]{:S(2)}) collective-permute-start(f32[64,128]{1,0:T(8,128)S(1)} %add.13), channel_id=1, source_target_pairs={{0,8},{2,10},{4,12},{6,14},{8,0},{10,2},{12,4},{14,6},{16,24},{18,... | collective-permute-start | bytes 98312 | tf_op jit(solution)/shard_map/ppermute | solution.py:213
  54.5 4.9 %collective-permute-start.6 = (f32[64,128]{1,0:T(8,128)S(1)}, f32[64,128]{1,0:T(8,128)S(1)}, u32[]{:S(2)}, u32[]{:S(2)}) collective-permute-start(f32[64,128]{1,0:T(8,128)S(1)} %add.14), channel_id=1, source_target_pairs={{0,16},{2,18},{4,20},{6,22},{8,24},{10,26},{12,28},{14,30},{16,0},... | collective-permute-start | bytes 98312 | tf_op jit(solution)/shard_map/ppermute | solution.py:213

commit v5 on v4

v5 whole, which is shorter than its diff:
```python
import functools

import jax
import jax.numpy as jnp
from jax import lax
from jax.experimental import pallas as pl
from jax.experimental.pallas import tpu as pltpu
from jax.sharding import PartitionSpec as P

LANES = 128
HALF = LANES // 2
GROUP = 8
VMEM_BYTES = 20 * 2**20
BF16 = jnp.bfloat16
F32 = jnp.float32


def swap(value, axis, first):
    count = lax.axis_size(axis)
    pairs = [(low, low + 1) for low in range(first, count - 1, 2)]
    return lax.ppermute(value, axis, pairs + [(high, low) for low, high in pairs])


def nt_dot(left, right):
    return lax.dot_general(left, right, (((1,), (1,)), ((), ())), preferred_element_type=F32)


def table_kernel(snap_hbm, up_ref, down_ref, table_ref, to_near_ref, to_far_ref, snap_ref, sem):
    chunks = snap_ref.shape[0]
    width = snap_ref.shape[3]
    copies = [
        pltpu.make_async_copy(snap_hbm.at[:, :, pl.ds(chunk * width, width)], snap_ref.at[chunk], sem.at[chunk])
        for chunk in range(chunks)
    ]
    for copy in copies:
        copy.start()
    row = lax.broadcasted_iota(jnp.int32, (2 * LANES, 2 * LANES), 0)
    col = lax.broadcasted_iota(jnp.int32, (2 * LANES, 2 * LANES), 1)
    pick = jnp.where(col == (row // 2) + LANES * (row % 2), 1.0, 0.0).astype(BF16)
    empty = jnp.zeros((HALF, LANES), BF16)
    for chunk in range(chunks):
        copies[chunk].wait()
        for start in range(0, width, LANES):
            comps = [snap_ref[chunk, comp, :, start : start + LANES] for comp in range(3)]
            first = jnp.concatenate([comps[0], comps[2]], axis=0)
            second = jnp.concatenate([comps[1], empty], axis=0)
            rows = nt_dot(pick, jnp.concatenate([first, second], axis=1)).astype(BF16)
            table_ref[chunk * width + start : chunk * width + start + LANES] = rows.reshape(LANES, 2, LANES)

    def fill(near_list, far_list):
        for out_ref, list_ref in ((to_near_ref, near_list), (to_far_ref, far_list)):
            for entry in range(out_ref.shape[0]):
                out_ref[entry] = table_ref[list_ref[entry]]

    odd = lax.rem(lax.axis_index("dom"), 2)

    @pl.when(odd == 0)
    def _():
        fill(up_ref, down_ref)

    @pl.when(odd == 1)
    def _():
        fill(down_ref, up_ref)


def node_table(snap, send_up, send_down):
    node_count = snap.shape[2]
    halo = send_up.shape[0]
    smem = pl.BlockSpec(memory_space=pltpu.SMEM)
    vmem = pl.BlockSpec(memory_space=pltpu.VMEM)
    chunks = 4 if node_count % (4 * LANES) == 0 else 1
    return pl.pallas_call(
        table_kernel,
        in_specs=[pl.BlockSpec(memory_space=pltpu.HBM), smem, smem],
        out_specs=[vmem] * 3,
        out_shape=[
            jax.ShapeDtypeStruct((node_count, 2, LANES), BF16),
            jax.ShapeDtypeStruct((halo, 2, LANES), BF16),
            jax.ShapeDtypeStruct((halo, 2, LANES), BF16),
        ],
        scratch_shapes=[pltpu.VMEM((chunks, 3, HALF, node_count // chunks), BF16), pltpu.SemaphoreType.DMA((chunks,))],
        compiler_params=pltpu.CompilerParams(vmem_limit_bytes=VMEM_BYTES),
        name="node_table",
    )(*(pltpu.with_memory_space_constraint(operand, pltpu.HBM) for operand in (snap, send_up, send_down)))


def spread_kernel(tile_hbm, out_ref, tile_ref, sem):
    sides = out_ref.shape[0]
    depth = sides * LANES
    groups = LANES // GROUP
    chunks, height, width = tile_ref.shape
    tiles = height // 9
    copies = [
        pltpu.make_async_copy(tile_hbm.at[:, pl.ds(chunk * width, width)], tile_ref.at[chunk], sem.at[chunk])
        for chunk in range(chunks)
    ]
    for copy in copies:
        copy.start()
    row = lax.broadcasted_iota(jnp.int32, (height, depth), 0)
    col = lax.broadcasted_iota(jnp.int32, (height, depth), 1)
    same_tile = row % tiles == col // (2 * GROUP)
    spreads = []
    for half in range(2):
        in_comp = col % 2 if half == 0 else jnp.where(col % 2 == 0, 2, -1)
        for comp in range(3):
            kept = same_tile & (row // tiles == 3 * comp + in_comp) & (in_comp >= 0)
            spreads.append(jnp.where(kept, 1.0, 0.0).astype(BF16))
    node = lax.broadcasted_iota(jnp.int32, (GROUP, depth), 0)
    slot = (lax.broadcasted_iota(jnp.int32, (GROUP, depth), 1) // 2) % GROUP
    own = node == slot
    for chunk in range(chunks):
        copies[chunk].wait()
        for block in range(width // LANES):
            turned = tile_ref[chunk, :, block * LANES : (block + 1) * LANES].T
            first = (chunk * width // LANES + block) * groups
            for pair in range(3):
                both = [jnp.dot(turned, spreads[2 * pair + one], preferred_element_type=F32) for one in range(2)]
                for group in range(groups):
                    kept = [jnp.where(own, part[group * GROUP : (group + 1) * GROUP], 0.0) for part in both]
                    rows = jnp.concatenate(kept, axis=0).astype(BF16)
                    for side in range(sides):
                        out_ref[side, first + group, 16 * pair : 16 * (pair + 1), :] = rows[:, side * LANES : (side + 1) * LANES]


def spread_tiles(mass_tiles):
    tiles, _, _, node_count = mass_tiles.shape
    sides = tiles * GROUP * 2 // LANES
    chunks = 4 if node_count % (4 * LANES) == 0 else 1
    return pl.pallas_call(
        spread_kernel,
        in_specs=[pl.BlockSpec(memory_space=pltpu.HBM)],
        out_specs=pl.BlockSpec(memory_space=pltpu.VMEM),
        out_shape=jax.ShapeDtypeStruct((sides, node_count // GROUP, 48, LANES), BF16),
        scratch_shapes=[pltpu.VMEM((chunks, tiles * 9, node_count // chunks), BF16), pltpu.SemaphoreType.DMA((chunks,))],
        compiler_params=pltpu.CompilerParams(vmem_limit_bytes=VMEM_BYTES),
        cost_estimate=pl.CostEstimate(flops=2 * node_count * tiles * 9 * 6 * sides * LANES, bytes_accessed=node_count * 6 * sides * LANES * 2, transcendentals=0),
        name="spread_tiles",
    )(pltpu.with_memory_space_constraint(jnp.transpose(mass_tiles, (1, 2, 0, 3)).reshape(tiles * 9, node_count), pltpu.HBM))


def mass_kernel(parts, slot_hbm, table_hbm, near_in, far_in, left_ref, own_ref, out_ref, again_ref, *scratch):
    slot_refs = scratch[:parts]
    table_ref, turn_ref, sem, fill_sem = scratch[parts:]
    step, steps = pl.program_id(0), pl.num_programs(0)
    others = slot_hbm.shape[0]
    sides = left_ref.shape[0]
    nodes, halo = table_hbm.shape[0], near_in.shape[0]
    groups = LANES // GROUP
    low_half = lax.broadcasted_iota(jnp.int32, (GROUP, LANES), 1) < HALF

    def fetch(block, part):
        source = slot_hbm.at[:, pl.ds(pl.multiple_of(block * LANES, LANES), LANES)]
        return pltpu.make_async_copy(source, slot_refs[part], sem.at[part])

    @pl.when(step == 0)
    def _():
        odd = lax.rem(lax.axis_index("dom"), 2)
        fills = [
            pltpu.make_async_copy(table_hbm, table_ref.at[pl.ds(0, nodes)], fill_sem.at[0]),
            pltpu.make_async_copy(near_in, table_ref.at[pl.ds(nodes + (1 - odd) * halo, halo)], fill_sem.at[1]),
            pltpu.make_async_copy(far_in, table_ref.at[pl.ds(nodes + odd * halo, halo)], fill_sem.at[2]),
        ]
        for copy in (fetch(0, 0), *fills, *(fetch(part, part) for part in range(1, parts))):
            copy.start()
        for fill in fills:
            fill.wait()

    for part in range(parts):
        block = parts * step + part
        fetch(block, part).wait()
        for group in range(groups):
            rows = [own_ref[pl.ds(pl.multiple_of((block * groups + group) * 2 * GROUP, 2 * GROUP), 2 * GROUP), :]]
            for tile in range(others):
                found = [table_ref[slot_refs[part][tile, group * GROUP + node]] for node in range(GROUP)]
                rows.append(jnp.stack(found).reshape(2 * GROUP, LANES))
            left = jnp.concatenate([left_ref[side, block * groups + group] for side in range(sides)], axis=1)
            sums = jnp.dot(left, jnp.concatenate(rows, axis=0), preferred_element_type=F32)
            for comp in range(3):
                low = sums[comp * GROUP : (comp + 1) * GROUP]
                high = sums[(3 + comp) * GROUP : (4 + comp) * GROUP]
                turn_ref[comp, group * GROUP : (group + 1) * GROUP, :] = jnp.where(low_half, low, high)

        @pl.when(step < steps - 1)
        def _():
            fetch(block + parts, part).start()

        for comp in range(3):
            turned = turn_ref[comp].T
            rounded = (turned[:HALF] + turned[HALF:]).astype(BF16)
            out_ref[comp, :, part * LANES : (part + 1) * LANES] = rounded
            again_ref[comp, :, part * LANES : (part + 1) * LANES] = rounded


def apply_mass(table, from_near, from_far, left, tile_slot):
    nodes, halo = table.shape[0], from_near.shape[0]
    others = tile_slot.shape[0]
    sides = left.shape[0]
    blocks = nodes // LANES
    parts = next(count for count in (4, 2, 1) if blocks % count == 0)
    any_space = pl.BlockSpec(memory_space=pl.ANY)
    return pl.pallas_call(
        functools.partial(mass_kernel, parts),
        grid=(blocks // parts,),
        in_specs=[any_space] * 2 + [pl.BlockSpec(memory_space=pltpu.VMEM)] * 4,
        out_specs=[pl.BlockSpec((3, HALF, parts * LANES), lambda i: (0, 0, i))] * 2,
        out_shape=[jax.ShapeDtypeStruct((3, HALF, nodes), BF16)] * 2,
        scratch_shapes=[pltpu.SMEM((others, LANES), jnp.int32)] * parts
        + [
            pltpu.VMEM((nodes + 2 * halo, 2, LANES), BF16),
            pltpu.VMEM((3, LANES, LANES), F32),
            pltpu.SemaphoreType.DMA((parts,)),
            pltpu.SemaphoreType.DMA((3,)),
        ],
        cost_estimate=pl.CostEstimate(flops=2 * nodes * 6 * sides * LANES * LANES, bytes_accessed=left.size * 2, transcendentals=0),
        compiler_params=pltpu.CompilerParams(vmem_limit_bytes=VMEM_BYTES),
        name="mass_rows",
    )(tile_slot, table, from_near, from_far, left, table.reshape(2 * nodes, LANES))


def summed(value, axis):
    count = lax.axis_size(axis)
    if count & (count - 1):
        return lax.psum(value, axis)
    step = 1
    while step < count:
        value = value + lax.ppermute(value, axis, [(source, source ^ step) for source in range(count)])
        step *= 2
    return value


def in_order(blocks):
    cols, here = len(blocks), lax.axis_index("col")
    if cols == 2:
        first = here == 0
        return jnp.concatenate([jnp.where(first, *blocks), jnp.where(first, *blocks[::-1])], axis=1)
    return jnp.concatenate([lax.dynamic_index_in_dim(jnp.stack(blocks), lax.rem(here - col + cols, cols), 0, False) for col in range(cols)], axis=1)


def body(snapshots, mass_tiles, tile_slot, send_up, send_down):
    snap_count, _, node_count = snapshots.shape
    cols = lax.axis_size("col")
    by_comp = jnp.transpose(snapshots, (1, 0, 2))
    parts = [by_comp] + [
        lax.ppermute(by_comp, "col", [(source, (source + shift) % cols) for source in range(cols)])
        for shift in range(1, cols)
    ]
    left = spread_tiles(mass_tiles)
    pieces = []
    for start in range(0, snap_count, HALF):
        piece = by_comp[:, start : start + HALF]
        size = piece.shape[1]
        if size < HALF:
            piece = jnp.pad(piece, ((0, 0), (0, HALF - size), (0, 0)))
        table, to_near, to_far = node_table(piece, send_up, send_down)
        both = apply_mass(table, swap(to_near, "dom", 0), swap(to_far, "dom", 1), left, tile_slot)
        pieces.append([rows[:, :size] for rows in both])
    mass_rows, again = pieces[0] if len(pieces) == 1 else [jnp.concatenate(rows, axis=1) for rows in zip(*pieces)]
    blocks = [lax.dot_general(again, part, (((0, 2), (0, 2)), ((), ())), preferred_element_type=F32) for part in parts]
    total = summed(in_order(blocks), "dom") / (3.0 * node_count * lax.axis_size("dom"))
    return jnp.transpose(mass_rows, (1, 0, 2)), total.T


def solution(mesh):
    placed = (P("col", None, "dom"), P(None, None, None, "dom"), P(None, "dom"), P("dom"), P("dom"))
    return jax.shard_map(
        body,
        mesh=mesh,
        in_specs=placed,
        out_specs=(P("col", None, "dom"), P(None, "col")),
        check_vma=False,
    )
```

time: 60.4 us -> 57.1 us (0.945)
  local copies, waits for them, and re-layouts: 3.21 us -> 0.01 us
  starting transfers between devices: 15.9 us -> 17.5 us
  Pallas kernels: 31.4 us -> 30.6 us
  other arithmetic: 1.49 us -> 0.79 us
    unnamed x10 -> x4, local copies, waits for them, and re-layouts: 3.21 us -> 0.01 us
    pallas_call x1, Pallas kernels: 26.5 us -> 23.6 us  [apply_mass(): pl.pallas_call(functools.partial(mass_kernel, parts), grid=(blocks // par...]
    pallas_call x2, Pallas kernels: 4.95 us -> 6.94 us  [the longest x1 3.54 us: node_table(): pl.pallas_call(table_kernel, in_specs=[pl.BlockSpec(memory_space=pltpu.HB...]
    ppermute x4, starting transfers between devices: 12.1 us -> 13.7 us  [summed(): lax.ppermute(value, axis, [(source, source ^ step) for source in range(co...]
    select_n x1 -> x0, other arithmetic: 0.7 us -> none  [body(): jnp.where(even, send_down, send_up)]
  transfers between devices with their start and end apart: 7 -> 7, of which waited for: 4 -> 4; matrix products, arithmetic and copies ran while one was open for 1% -> 0% of each run, Pallas kernels for 52% -> 54%
where the time goes in v5:
time: 57.1 us; the launch traced here: 56.9 us
  Pallas kernels  30.6 us (54%)
  starting transfers between devices  17.5 us (31%)
  waiting for transfers between devices  6.55 us (11%)
  other arithmetic  0.79 us (1%)
  between operations  0.75 us (1%)
  matrix products  0.7 us (1%)
    pallas_call x1, Pallas kernels, apply_mass(): pl.pallas_call(functools.partial(mass_kernel, parts), grid=(blocks // par...  23.6 us
    ppermute x4, starting transfers between devices, summed(): lax.ppermute(value, axis, [(source, source ^ step) for source in range(co...  13.7 us
    ppermute x4, waiting for transfers between devices, summed(): lax.ppermute(value, axis, [(source, source ^ step) for source in range(co...  6.54 us
    pallas_call x1, Pallas kernels, node_table(): pl.pallas_call(table_kernel, in_specs=[pl.BlockSpec(memory_space=pltpu.HB...  3.54 us
    pallas_call x1, Pallas kernels, spread_tiles(): pl.pallas_call(spread_kernel, in_specs=[pl.BlockSpec(memory_space=pltpu.H...  3.41 us
    ppermute x1, starting transfers between devices, body(): lax.ppermute(by_comp, 'col', [(source, (source + shift) % cols) for sourc...  3.06 us
  transfers between devices with their start and end apart: 7, of which 4 were waited for; matrix products, arithmetic and copies ran while one was open for 0% of the time, Pallas kernels for 54%

profile of v5, /device:TPU:0, one launch (start us, length us, event | category | flops | bytes accessed | tf_op | source)
XLA Modules:
  0.0 56.9 jit_solution(8301939545785608132)
XLA Ops:
  0.6 0.0 copy-start
  0.6 3.1 %collective-permute-start.2 = (bf16[3,64,2048]{2,1,0:T(8,128)(2,1)}, bf16[3,64,2048]{2,1,0:T(8,128)(2,1)S(1)}, u32[]{:S(2)}, u32[]{:S(2)}) collective-permute-start(bf16[3,64,2048]{2,1,0:T(8,128)(2,1)} %bitcast.20), channel_id=1, source_target_pairs={{0,1},{1,0},{2,3},{3,2},{4,5},{5,4},{6,7},{7,6},{8,9},{9,8},{10,11... | collective-permute-start | bytes 2359304 | tf_op jit(solution)/shard_map/ppermute | solution.py:244
  3.7 3.5 %node_table.1 = (bf16[2048,2,128]{2,1,0:T(2,128)(2,1)S(1)}, bf16[512,2,128]{2,1,0:T(2,128)(2,1)S(1)}, bf16[512,2,128]{2,1,0:T(2,128)(2,1)S(1)}) custom-call(bf16[3,64,2048]{2,1,0:T(8,128)(2,1)} %bitcast.21, s32[512]{0:T(512)} %up_ref.1, s32[512]{0:T(512)} %down_ref.1), custom_call_target="tpu_custom_call" | custom-call | tf_op jit(solution)/shard_map/node_table/pallas_call | solution.py:72
  7.2 0.1 collective-permute-start
  7.3 0.7 %collective-permute-start.1 = (bf16[512,2,128]{2,1,0:T(2,128)(2,1)S(1)}, bf16[512,2,128]{2,1,0:T(2,128)(2,1)S(1)}, u32[]{:S(2)}, u32[]{:S(2)}) collective-permute-start(bf16[512,2,128]{2,1,0:T(2,128)(2,1)S(1)} %get-tuple-element.9), channel_id=1, source_target_pairs={{2,4},{6,8},{10,12},{14,16},{18,20},{22,24},{26,28},{4,2},{8,6},{1... | collective-permute-start | bytes 786440 | tf_op jit(solution)/shard_map/ppermute | solution.py:21
  8.0 3.4 %spread_tiles.1.left_ref = bf16[2,256,48,128]{3,2,1,0:T(8,128)(2,1)S(1)} custom-call(bf16[144,2048]{1,0:T(8,128)(2,1)} %bitcast.22), custom_call_target="tpu_custom_call" | custom-call | flops 905969664 | bytes 6291456 | tf_op jit(solution)/shard_map/spread_tiles/pallas_call | solution.py:129
  11.4 0.0 copy-start.1
  11.4 0.0 collective-permute-done.near_in
  11.5 0.0 collective-permute-done.1.far_in
  11.5 0.0 copy-done
  11.5 23.6 %mass_rows.1 = (bf16[3,64,2048]{2,1,0:T(8,128)(2,1)}, bf16[3,64,2048]{2,1,0:T(8,128)(2,1)S(1)}) custom-call(s32[15,2048]{1,0:T(8,128)S(1)} %copy-done, bf16[2048,2,128]{2,1,0:T(2,128)(2,1)S(1)} %get-tuple-element.7.table_hbm, bf16[512,2,128]{2,1,0:T(2,128)(2,1)S(1)} %collective-permute-done.near_in, bf16[512,2,128]{2,1,0:T(2,128)(2,1)S(1)} %collective-permute-done.1.far_in, ...), custom_call_target="tpu_custom_call" | custom-call | flops 805306368 | bytes 6291456 | tf_op jit(solution)/shard_map/mass_rows/pallas_call | solution.py:201
  35.1 0.0 collective-permute-done.2
  35.1 0.4 convolution_bitcast_fusion
  35.5 0.0 copy-done.1
  35.5 0.4 broadcast_select_fusion.1
  35.9 0.1 pad_maximum_fusion
  35.9 5.4 %collective-permute-start.3 = (f32[64,128]{1,0:T(8,128)S(1)}, f32[64,128]{1,0:T(8,128)S(1)}, u32[]{:S(2)}, u32[]{:S(2)}) collective-permute-start(f32[64,128]{1,0:T(8,128)S(1)} %pad_maximum_fusion), channel_id=1, source_target_pairs={{0,2},{2,0},{4,6},{6,4},{8,10},{10,8},{12,14},{14,12},{16,18},{18,... | collective-permute-start | bytes 98312 | tf_op jit(solution)/shard_map/ppermute | solution.py:226
  41.4 0.9 %collective-permute-done.3 = f32[64,128]{1,0:T(8,128)S(1)} collective-permute-done((f32[64,128]{1,0:T(8,128)S(1)}, f32[64,128]{1,0:T(8,128)S(1)}, u32[]{:S(2)}, u32[]{:S(2)}) %collective-permute-start.3) | collective-permute-done | bytes 32800 | tf_op jit(solution)/shard_map/ppermute | solution.py:226
  42.2 0.1 fusion.4
  42.3 2.7 %collective-permute-start.4 = (f32[64,128]{1,0:T(8,128)S(1)}, f32[64,128]{1,0:T(8,128)S(1)}, u32[]{:S(2)}, u32[]{:S(2)}) collective-permute-start(f32[64,128]{1,0:T(8,128)S(1)} %fusion.4), channel_id=1, source_target_pairs={{0,4},{2,6},{4,0},{6,2},{8,12},{10,14},{12,8},{14,10},{16,20},{18,... | collective-permute-start | bytes 98312 | tf_op jit(solution)/shard_map/ppermute | solution.py:226
  45.1 1.9 %collective-permute-done.4 = f32[64,128]{1,0:T(8,128)S(1)} collective-permute-done((f32[64,128]{1,0:T(8,128)S(1)}, f32[64,128]{1,0:T(8,128)S(1)}, u32[]{:S(2)}, u32[]{:S(2)}) %collective-permute-start.4) | collective-permute-done | bytes 32800 | tf_op jit(solution)/shard_map/ppermute | solution.py:226
  47.0 2.5 %collective-permute-start.5 = (f32[64,128]{1,0:T(8,128)S(1)}, f32[64,128]{1,0:T(8,128)S(1)}, u32[]{:S(2)}, u32[]{:S(2)}) collective-permute-start(f32[64,128]{1,0:T(8,128)S(1)} %add.13), channel_id=1, source_target_pairs={{0,8},{2,10},{4,12},{6,14},{8,0},{10,2},{12,4},{14,6},{16,24},{18,... | collective-permute-start | bytes 98312 | tf_op jit(solution)/shard_map/ppermute | solution.py:226
  49.5 1.9 %collective-permute-done.5 = f32[64,128]{1,0:T(8,128)S(1)} collective-permute-done((f32[64,128]{1,0:T(8,128)S(1)}, f32[64,128]{1,0:T(8,128)S(1)}, u32[]{:S(2)}, u32[]{:S(2)}) %collective-permute-start.5) | collective-permute-done | bytes 32800 | tf_op jit(solution)/shard_map/ppermute | solution.py:226
  51.4 3.0 %collective-permute-start.6 = (f32[64,128]{1,0:T(8,128)S(1)}, f32[64,128]{1,0:T(8,128)S(1)}, u32[]{:S(2)}, u32[]{:S(2)}) collective-permute-start(f32[64,128]{1,0:T(8,128)S(1)} %add.14), channel_id=1, source_target_pairs={{0,16},{2,18},{4,20},{6,22},{8,24},{10,26},{12,28},{14,30},{16,0},... | collective-permute-start | bytes 98312 | tf_op jit(solution)/shard_map/ppermute | solution.py:226
  54.4 1.9 %collective-permute-done.6 = f32[64,128]{1,0:T(8,128)S(1)} collective-permute-done((f32[64,128]{1,0:T(8,128)S(1)}, f32[64,128]{1,0:T(8,128)S(1)}, u32[]{:S(2)}, u32[]{:S(2)}) %collective-permute-start.6) | collective-permute-done | bytes 32800 | tf_op jit(solution)/shard_map/ppermute | solution.py:226
  56.3 0.6 %multiply_bitcast_fusion = f32[128,64]{0,1:T(8,128)} fusion(f32[64,128]{1,0:T(8,128)S(1)} %add.14, f32[64,128]{1,0:T(8,128)S(1)} %collective-permute-done.6), kind=kLoop, calls=%fused_computation.3 | loop fusion | flops 16384 | bytes 98304 | tf_op jit(solution)/shard_map/transpose | solution.py:260
  (2 shorter events, 0.0 us)
Async XLA Ops:
  0.6 10.8 %copy-start = (s32[15,2048]{1,0:T(8,128)S(1)}, s32[15,2048]{1,0:T(8,128)}, u32[]{:S(2)}) copy-start(s32[15,2048]{1,0:T(8,128)} %slot_hbm.1) | copy-start | bytes 368644
  0.6 34.5 %collective-permute-start.2 = (bf16[3,64,2048]{2,1,0:T(8,128)(2,1)}, bf16[3,64,2048]{2,1,0:T(8,128)(2,1)S(1)}, u32[]{:S(2)}, u32[]{:S(2)}) collective-permute-start(bf16[3,64,2048]{2,1,0:T(8,128)(2,1)} %bitcast.20), channel_id=1, source_target_pairs={{0,1},{1,0},{2,3},{3,2},{4,5},{5,4},{6,7},{7,6},{8,9},{9,8},{10,11... | collective-permute-start | bytes 2359304 | tf_op jit(solution)/shard_map/ppermute | solution.py:244
  7.2 4.2 %collective-permute-start = (bf16[512,2,128]{2,1,0:T(2,128)(2,1)S(1)}, bf16[512,2,128]{2,1,0:T(2,128)(2,1)S(1)}, u32[]{:S(2)}, u32[]{:S(2)}) collective-permute-start(bf16[512,2,128]{2,1,0:T(2,128)(2,1)S(1)} %get-tuple-element.8), channel_id=1, source_target_pairs={{0,2},{4,6},{8,10},{12,14},{16,18},{20,22},{24,26},{28,30},{2,0},{... | collective-permute-start | bytes 786440 | tf_op jit(solution)/shard_map/ppermute | solution.py:21
  7.3 4.1 %collective-permute-start.1 = (bf16[512,2,128]{2,1,0:T(2,128)(2,1)S(1)}, bf16[512,2,128]{2,1,0:T(2,128)(2,1)S(1)}, u32[]{:S(2)}, u32[]{:S(2)}) collective-permute-start(bf16[512,2,128]{2,1,0:T(2,128)(2,1)S(1)} %get-tuple-element.9), channel_id=1, source_target_pairs={{2,4},{6,8},{10,12},{14,16},{18,20},{22,24},{26,28},{4,2},{8,6},{1... | collective-permute-start | bytes 786440 | tf_op jit(solution)/shard_map/ppermute | solution.py:21
  11.4 24.1 %copy-start.1 = (bf16[64,3,2048]{2,0,1:T(8,128)(2,1)S(1)}, bf16[64,3,2048]{2,0,1:T(8,128)(2,1)}, u32[]{:S(2)}) copy-start(bf16[64,3,2048]{2,0,1:T(8,128)(2,1)} %param.5) | copy-start | bytes 2359300
  35.9 6.3 %collective-permute-start.3 = (f32[64,128]{1,0:T(8,128)S(1)}, f32[64,128]{1,0:T(8,128)S(1)}, u32[]{:S(2)}, u32[]{:S(2)}) collective-permute-start(f32[64,128]{1,0:T(8,128)S(1)} %pad_maximum_fusion), channel_id=1, source_target_pairs={{0,2},{2,0},{4,6},{6,4},{8,10},{10,8},{12,14},{14,12},{16,18},{18,... | collective-permute-start | bytes 98312 | tf_op jit(solution)/shard_map/ppermute | solution.py:226
  42.3 4.6 %collective-permute-start.4 = (f32[64,128]{1,0:T(8,128)S(1)}, f32[64,128]{1,0:T(8,128)S(1)}, u32[]{:S(2)}, u32[]{:S(2)}) collective-permute-start(f32[64,128]{1,0:T(8,128)S(1)} %fusion.4), channel_id=1, source_target_pairs={{0,4},{2,6},{4,0},{6,2},{8,12},{10,14},{12,8},{14,10},{16,20},{18,... | collective-permute-start | bytes 98312 | tf_op jit(solution)/shard_map/ppermute | solution.py:226
  47.0 4.4 %collective-permute-start.5 = (f32[64,128]{1,0:T(8,128)S(1)}, f32[64,128]{1,0:T(8,128)S(1)}, u32[]{:S(2)}, u32[]{:S(2)}) collective-permute-start(f32[64,128]{1,0:T(8,128)S(1)} %add.13), channel_id=1, source_target_pairs={{0,8},{2,10},{4,12},{6,14},{8,0},{10,2},{12,4},{14,6},{16,24},{18,... | collective-permute-start | bytes 98312 | tf_op jit(solution)/shard_map/ppermute | solution.py:226
  51.4 4.9 %collective-permute-start.6 = (f32[64,128]{1,0:T(8,128)S(1)}, f32[64,128]{1,0:T(8,128)S(1)}, u32[]{:S(2)}, u32[]{:S(2)}) collective-permute-start(f32[64,128]{1,0:T(8,128)S(1)} %add.14), channel_id=1, source_target_pairs={{0,16},{2,18},{4,20},{6,22},{8,24},{10,26},{12,28},{14,30},{16,0},... | collective-permute-start | bytes 98312 | tf_op jit(solution)/shard_map/ppermute | solution.py:226

commit v6 on v5

--- a/solution.py
+++ b/solution.py
@@ -240,10 +240,9 @@
     snap_count, _, node_count = snapshots.shape
     cols = lax.axis_size("col")
     by_comp = jnp.transpose(snapshots, (1, 0, 2))
-    parts = [by_comp] + [
-        lax.ppermute(by_comp, "col", [(source, (source + shift) % cols) for source in range(cols)])
-        for shift in range(1, cols)
-    ]
+    parts = [by_comp]
+    for shift in range(1, cols):
+        parts.append(lax.ppermute(by_comp, "col", [(source, (source + shift) % cols) for source in range(cols)]))
     left = spread_tiles(mass_tiles)
     pieces = []
     for start in range(0, snap_count, HALF):
@@ -252,7 +251,9 @@
         if size < HALF:
             piece = jnp.pad(piece, ((0, 0), (0, HALF - size), (0, 0)))
         table, to_near, to_far = node_table(piece, send_up, send_down)
-        both = apply_mass(table, swap(to_near, "dom", 0), swap(to_far, "dom", 1), left, tile_slot)
+        from_far = swap(to_far, "dom", 1)
+        from_near = swap(to_near, "dom", 0)
+        both = apply_mass(table, from_near, from_far, left, tile_slot)
         pieces.append([rows[:, :size] for rows in both])
     mass_rows, again = pieces[0] if len(pieces) == 1 else [jnp.concatenate(rows, axis=1) for rows in zip(*pieces)]
     blocks = [lax.dot_general(again, part, (((0, 2), (0, 2)), ((), ())), preferred_element_type=F32) for part in parts]

time: 57.1 us -> 57.1 us (level)
  no operation moved by 1% of the time
where the time goes in v6:
time: 57.1 us; the launch traced here: 56.9 us
  Pallas kernels  30.6 us (54%)
  starting transfers between devices  17.6 us (31%)
  waiting for transfers between devices  6.55 us (11%)
  other arithmetic  0.79 us (1%)
  between operations  0.75 us (1%)
  matrix products  0.7 us (1%)
    pallas_call x1, Pallas kernels, apply_mass(): pl.pallas_call(functools.partial(mass_kernel, parts), grid=(blocks // par...  23.6 us
    ppermute x4, starting transfers between devices, summed(): lax.ppermute(value, axis, [(source, source ^ step) for source in range(co...  13.8 us
    ppermute x4, waiting for transfers between devices, summed(): lax.ppermute(value, axis, [(source, source ^ step) for source in range(co...  6.54 us
    pallas_call x1, Pallas kernels, node_table(): pl.pallas_call(table_kernel, in_specs=[pl.BlockSpec(memory_space=pltpu.HB...  3.54 us
    pallas_call x1, Pallas kernels, spread_tiles(): pl.pallas_call(spread_kernel, in_specs=[pl.BlockSpec(memory_space=pltpu.H...  3.41 us
    ppermute x1, starting transfers between devices, body(): lax.ppermute(by_comp, 'col', [(source, (source + shift) % cols) for sourc...  3.06 us
  transfers between devices with their start and end apart: 7, of which 4 were waited for; matrix products, arithmetic and copies ran while one was open for 0% of the time, Pallas kernels for 54%

profile of v6, /device:TPU:0, one launch (start us, length us, event | category | flops | bytes accessed | tf_op | source)
XLA Modules:
  0.0 56.9 jit_solution(8301939545785608132)
XLA Ops:
  0.6 0.0 copy-start
  0.6 3.1 %collective-permute-start.2 = (bf16[3,64,2048]{2,1,0:T(8,128)(2,1)}, bf16[3,64,2048]{2,1,0:T(8,128)(2,1)S(1)}, u32[]{:S(2)}, u32[]{:S(2)}) collective-permute-start(bf16[3,64,2048]{2,1,0:T(8,128)(2,1)} %bitcast.20), channel_id=1, source_target_pairs={{0,1},{1,0},{2,3},{3,2},{4,5},{5,4},{6,7},{7,6},{8,9},{9,8},{10,11... | collective-permute-start | bytes 2359304 | tf_op jit(solution)/shard_map/ppermute | solution.py:245
  3.7 3.5 %node_table.1 = (bf16[2048,2,128]{2,1,0:T(2,128)(2,1)S(1)}, bf16[512,2,128]{2,1,0:T(2,128)(2,1)S(1)}, bf16[512,2,128]{2,1,0:T(2,128)(2,1)S(1)}) custom-call(bf16[3,64,2048]{2,1,0:T(8,128)(2,1)} %bitcast.21, s32[512]{0:T(512)} %up_ref.1, s32[512]{0:T(512)} %down_ref.1), custom_call_target="tpu_custom_call" | custom-call | tf_op jit(solution)/shard_map/node_table/pallas_call | solution.py:72
  7.2 0.1 collective-permute-start
  7.3 0.7 %collective-permute-start.1 = (bf16[512,2,128]{2,1,0:T(2,128)(2,1)S(1)}, bf16[512,2,128]{2,1,0:T(2,128)(2,1)S(1)}, u32[]{:S(2)}, u32[]{:S(2)}) collective-permute-start(bf16[512,2,128]{2,1,0:T(2,128)(2,1)S(1)} %get-tuple-element.9), channel_id=1, source_target_pairs={{2,4},{6,8},{10,12},{14,16},{18,20},{22,24},{26,28},{4,2},{8,6},{1... | collective-permute-start | bytes 786440 | tf_op jit(solution)/shard_map/ppermute | solution.py:21
  8.0 3.4 %spread_tiles.1.left_ref = bf16[2,256,48,128]{3,2,1,0:T(8,128)(2,1)S(1)} custom-call(bf16[144,2048]{1,0:T(8,128)(2,1)} %bitcast.22), custom_call_target="tpu_custom_call" | custom-call | flops 905969664 | bytes 6291456 | tf_op jit(solution)/shard_map/spread_tiles/pallas_call | solution.py:129
  11.4 0.0 copy-start.1
  11.4 0.0 collective-permute-done.near_in
  11.5 0.0 collective-permute-done.1.far_in
  11.5 0.0 copy-done
  11.5 23.6 %mass_rows.1 = (bf16[3,64,2048]{2,1,0:T(8,128)(2,1)}, bf16[3,64,2048]{2,1,0:T(8,128)(2,1)S(1)}) custom-call(s32[15,2048]{1,0:T(8,128)S(1)} %copy-done, bf16[2048,2,128]{2,1,0:T(2,128)(2,1)S(1)} %get-tuple-element.7.table_hbm, bf16[512,2,128]{2,1,0:T(2,128)(2,1)S(1)} %collective-permute-done.near_in, bf16[512,2,128]{2,1,0:T(2,128)(2,1)S(1)} %collective-permute-done.1.far_in, ...), custom_call_target="tpu_custom_call" | custom-call | flops 805306368 | bytes 6291456 | tf_op jit(solution)/shard_map/mass_rows/pallas_call | solution.py:201
  35.1 0.0 collective-permute-done.2
  35.1 0.3 convolution_bitcast_fusion
  35.5 0.0 copy-done.1
  35.5 0.4 broadcast_select_fusion.1
  35.8 0.1 pad_maximum_fusion
  35.9 5.5 %collective-permute-start.3 = (f32[64,128]{1,0:T(8,128)S(1)}, f32[64,128]{1,0:T(8,128)S(1)}, u32[]{:S(2)}, u32[]{:S(2)}) collective-permute-start(f32[64,128]{1,0:T(8,128)S(1)} %pad_maximum_fusion), channel_id=1, source_target_pairs={{0,2},{2,0},{4,6},{6,4},{8,10},{10,8},{12,14},{14,12},{16,18},{18,... | collective-permute-start | bytes 98312 | tf_op jit(solution)/shard_map/ppermute | solution.py:226
  41.4 0.9 %collective-permute-done.3 = f32[64,128]{1,0:T(8,128)S(1)} collective-permute-done((f32[64,128]{1,0:T(8,128)S(1)}, f32[64,128]{1,0:T(8,128)S(1)}, u32[]{:S(2)}, u32[]{:S(2)}) %collective-permute-start.3) | collective-permute-done | bytes 32800 | tf_op jit(solution)/shard_map/ppermute | solution.py:226
  42.2 0.1 fusion.4
  42.3 2.7 %collective-permute-start.4 = (f32[64,128]{1,0:T(8,128)S(1)}, f32[64,128]{1,0:T(8,128)S(1)}, u32[]{:S(2)}, u32[]{:S(2)}) collective-permute-start(f32[64,128]{1,0:T(8,128)S(1)} %fusion.4), channel_id=1, source_target_pairs={{0,4},{2,6},{4,0},{6,2},{8,12},{10,14},{12,8},{14,10},{16,20},{18,... | collective-permute-start | bytes 98312 | tf_op jit(solution)/shard_map/ppermute | solution.py:226
  45.0 1.9 %collective-permute-done.4 = f32[64,128]{1,0:T(8,128)S(1)} collective-permute-done((f32[64,128]{1,0:T(8,128)S(1)}, f32[64,128]{1,0:T(8,128)S(1)}, u32[]{:S(2)}, u32[]{:S(2)}) %collective-permute-start.4) | collective-permute-done | bytes 32800 | tf_op jit(solution)/shard_map/ppermute | solution.py:226
  46.9 2.5 %collective-permute-start.5 = (f32[64,128]{1,0:T(8,128)S(1)}, f32[64,128]{1,0:T(8,128)S(1)}, u32[]{:S(2)}, u32[]{:S(2)}) collective-permute-start(f32[64,128]{1,0:T(8,128)S(1)} %add.13), channel_id=1, source_target_pairs={{0,8},{2,10},{4,12},{6,14},{8,0},{10,2},{12,4},{14,6},{16,24},{18,... | collective-permute-start | bytes 98312 | tf_op jit(solution)/shard_map/ppermute | solution.py:226
  49.5 1.9 %collective-permute-done.5 = f32[64,128]{1,0:T(8,128)S(1)} collective-permute-done((f32[64,128]{1,0:T(8,128)S(1)}, f32[64,128]{1,0:T(8,128)S(1)}, u32[]{:S(2)}, u32[]{:S(2)}) %collective-permute-start.5) | collective-permute-done | bytes 32800 | tf_op jit(solution)/shard_map/ppermute | solution.py:226
  51.4 3.1 %collective-permute-start.6 = (f32[64,128]{1,0:T(8,128)S(1)}, f32[64,128]{1,0:T(8,128)S(1)}, u32[]{:S(2)}, u32[]{:S(2)}) collective-permute-start(f32[64,128]{1,0:T(8,128)S(1)} %add.14), channel_id=1, source_target_pairs={{0,16},{2,18},{4,20},{6,22},{8,24},{10,26},{12,28},{14,30},{16,0},... | collective-permute-start | bytes 98312 | tf_op jit(solution)/shard_map/ppermute | solution.py:226
  54.4 1.9 %collective-permute-done.6 = f32[64,128]{1,0:T(8,128)S(1)} collective-permute-done((f32[64,128]{1,0:T(8,128)S(1)}, f32[64,128]{1,0:T(8,128)S(1)}, u32[]{:S(2)}, u32[]{:S(2)}) %collective-permute-start.6) | collective-permute-done | bytes 32800 | tf_op jit(solution)/shard_map/ppermute | solution.py:226
  56.3 0.6 %multiply_bitcast_fusion = f32[128,64]{0,1:T(8,128)} fusion(f32[64,128]{1,0:T(8,128)S(1)} %add.14, f32[64,128]{1,0:T(8,128)S(1)} %collective-permute-done.6), kind=kLoop, calls=%fused_computation.3 | loop fusion | flops 16384 | bytes 98304 | tf_op jit(solution)/shard_map/transpose | solution.py:261
  (2 shorter events, 0.0 us)
Async XLA Ops:
  0.6 10.8 %copy-start = (s32[15,2048]{1,0:T(8,128)S(1)}, s32[15,2048]{1,0:T(8,128)}, u32[]{:S(2)}) copy-start(s32[15,2048]{1,0:T(8,128)} %slot_hbm.1) | copy-start | bytes 368644
  0.6 34.5 %collective-permute-start.2 = (bf16[3,64,2048]{2,1,0:T(8,128)(2,1)}, bf16[3,64,2048]{2,1,0:T(8,128)(2,1)S(1)}, u32[]{:S(2)}, u32[]{:S(2)}) collective-permute-start(bf16[3,64,2048]{2,1,0:T(8,128)(2,1)} %bitcast.20), channel_id=1, source_target_pairs={{0,1},{1,0},{2,3},{3,2},{4,5},{5,4},{6,7},{7,6},{8,9},{9,8},{10,11... | collective-permute-start | bytes 2359304 | tf_op jit(solution)/shard_map/ppermute | solution.py:245
  7.2 4.2 %collective-permute-start = (bf16[512,2,128]{2,1,0:T(2,128)(2,1)S(1)}, bf16[512,2,128]{2,1,0:T(2,128)(2,1)S(1)}, u32[]{:S(2)}, u32[]{:S(2)}) collective-permute-start(bf16[512,2,128]{2,1,0:T(2,128)(2,1)S(1)} %get-tuple-element.8), channel_id=1, source_target_pairs={{0,2},{4,6},{8,10},{12,14},{16,18},{20,22},{24,26},{28,30},{2,0},{... | collective-permute-start | bytes 786440 | tf_op jit(solution)/shard_map/ppermute | solution.py:21
  7.3 4.1 %collective-permute-start.1 = (bf16[512,2,128]{2,1,0:T(2,128)(2,1)S(1)}, bf16[512,2,128]{2,1,0:T(2,128)(2,1)S(1)}, u32[]{:S(2)}, u32[]{:S(2)}) collective-permute-start(bf16[512,2,128]{2,1,0:T(2,128)(2,1)S(1)} %get-tuple-element.9), channel_id=1, source_target_pairs={{2,4},{6,8},{10,12},{14,16},{18,20},{22,24},{26,28},{4,2},{8,6},{1... | collective-permute-start | bytes 786440 | tf_op jit(solution)/shard_map/ppermute | solution.py:21
  11.4 24.0 %copy-start.1 = (bf16[64,3,2048]{2,0,1:T(8,128)(2,1)S(1)}, bf16[64,3,2048]{2,0,1:T(8,128)(2,1)}, u32[]{:S(2)}) copy-start(bf16[64,3,2048]{2,0,1:T(8,128)(2,1)} %param.5) | copy-start | bytes 2359300
  35.9 6.3 %collective-permute-start.3 = (f32[64,128]{1,0:T(8,128)S(1)}, f32[64,128]{1,0:T(8,128)S(1)}, u32[]{:S(2)}, u32[]{:S(2)}) collective-permute-start(f32[64,128]{1,0:T(8,128)S(1)} %pad_maximum_fusion), channel_id=1, source_target_pairs={{0,2},{2,0},{4,6},{6,4},{8,10},{10,8},{12,14},{14,12},{16,18},{18,... | collective-permute-start | bytes 98312 | tf_op jit(solution)/shard_map/ppermute | solution.py:226
  42.3 4.6 %collective-permute-start.4 = (f32[64,128]{1,0:T(8,128)S(1)}, f32[64,128]{1,0:T(8,128)S(1)}, u32[]{:S(2)}, u32[]{:S(2)}) collective-permute-start(f32[64,128]{1,0:T(8,128)S(1)} %fusion.4), channel_id=1, source_target_pairs={{0,4},{2,6},{4,0},{6,2},{8,12},{10,14},{12,8},{14,10},{16,20},{18,... | collective-permute-start | bytes 98312 | tf_op jit(solution)/shard_map/ppermute | solution.py:226
  46.9 4.4 %collective-permute-start.5 = (f32[64,128]{1,0:T(8,128)S(1)}, f32[64,128]{1,0:T(8,128)S(1)}, u32[]{:S(2)}, u32[]{:S(2)}) collective-permute-start(f32[64,128]{1,0:T(8,128)S(1)} %add.13), channel_id=1, source_target_pairs={{0,8},{2,10},{4,12},{6,14},{8,0},{10,2},{12,4},{14,6},{16,24},{18,... | collective-permute-start | bytes 98312 | tf_op jit(solution)/shard_map/ppermute | solution.py:226
  51.4 4.9 %collective-permute-start.6 = (f32[64,128]{1,0:T(8,128)S(1)}, f32[64,128]{1,0:T(8,128)S(1)}, u32[]{:S(2)}, u32[]{:S(2)}) collective-permute-start(f32[64,128]{1,0:T(8,128)S(1)} %add.14), channel_id=1, source_target_pairs={{0,16},{2,18},{4,20},{6,22},{8,24},{10,26},{12,28},{14,30},{16,0},... | collective-permute-start | bytes 98312 | tf_op jit(solution)/shard_map/ppermute | solution.py:226

commit v7 on v6

--- a/solution.py
+++ b/solution.py
@@ -165,9 +165,18 @@
         for fill in fills:
             fill.wait()
 
+    def flush(part):
+        for comp in range(3):
+            turned = turn_ref[part % 2, comp].T
+            rounded = (turned[:HALF] + turned[HALF:]).astype(BF16)
+            out_ref[comp, :, part * LANES : (part + 1) * LANES] = rounded
+            again_ref[comp, :, part * LANES : (part + 1) * LANES] = rounded
+
     for part in range(parts):
         block = parts * step + part
         fetch(block, part).wait()
+        if part:
+            flush(part - 1)
         for group in range(groups):
             rows = [own_ref[pl.ds(pl.multiple_of((block * groups + group) * 2 * GROUP, 2 * GROUP), 2 * GROUP), :]]
             for tile in range(others):
@@ -178,17 +187,13 @@
             for comp in range(3):
                 low = sums[comp * GROUP : (comp + 1) * GROUP]
                 high = sums[(3 + comp) * GROUP : (4 + comp) * GROUP]
-                turn_ref[comp, group * GROUP : (group + 1) * GROUP, :] = jnp.where(low_half, low, high)
+                turn_ref[part % 2, comp, group * GROUP : (group + 1) * GROUP, :] = jnp.where(low_half, low, high)
 
         @pl.when(step < steps - 1)
         def _():
             fetch(block + parts, part).start()
 
-        for comp in range(3):
-            turned = turn_ref[comp].T
-            rounded = (turned[:HALF] + turned[HALF:]).astype(BF16)
-            out_ref[comp, :, part * LANES : (part + 1) * LANES] = rounded
-            again_ref[comp, :, part * LANES : (part + 1) * LANES] = rounded
+    flush(parts - 1)
 
 
 def apply_mass(table, from_near, from_far, left, tile_slot):
@@ -196,7 +201,7 @@
     others = tile_slot.shape[0]
     sides = left.shape[0]
     blocks = nodes // LANES
-    parts = next(count for count in (4, 2, 1) if blocks % count == 0)
+    parts = next(count for count in (8, 4, 2, 1) if blocks % count == 0)
     any_space = pl.BlockSpec(memory_space=pl.ANY)
     return pl.pallas_call(
         functools.partial(mass_kernel, parts),
@@ -207,7 +212,7 @@
         scratch_shapes=[pltpu.SMEM((others, LANES), jnp.int32)] * parts
         + [
             pltpu.VMEM((nodes + 2 * halo, 2, LANES), BF16),
-            pltpu.VMEM((3, LANES, LANES), F32),
+            pltpu.VMEM((2, 3, LANES, LANES), F32),
             pltpu.SemaphoreType.DMA((parts,)),
             pltpu.SemaphoreType.DMA((3,)),
         ],

time: 57.1 us -> 55.9 us (0.979)
  Pallas kernels: 30.6 us -> 29.5 us
    pallas_call x1, Pallas kernels: 23.6 us -> 22.5 us  [apply_mass(): pl.pallas_call(functools.partial(mass_kernel, parts), grid=(blocks // par...]
  transfers between devices with their start and end apart: 7 -> 7, of which waited for: 4 -> 4; matrix products, arithmetic and copies ran while one was open for 0% -> 0% of each run, Pallas kernels for 54% -> 53%
where the time goes in v7:
time: 55.9 us; the launch traced here: 55.7 us
  Pallas kernels  29.5 us (53%)
  starting transfers between devices  17.4 us (31%)
  waiting for transfers between devices  6.55 us (12%)
  other arithmetic  0.79 us (1%)
  between operations  0.75 us (1%)
  matrix products  0.7 us (1%)
    pallas_call x1, Pallas kernels, apply_mass(): pl.pallas_call(functools.partial(mass_kernel, parts), grid=(blocks // par...  22.5 us
    ppermute x4, starting transfers between devices, summed(): lax.ppermute(value, axis, [(source, source ^ step) for source in range(co...  13.6 us
    ppermute x4, waiting for transfers between devices, summed(): lax.ppermute(value, axis, [(source, source ^ step) for source in range(co...  6.54 us
    pallas_call x1, Pallas kernels, node_table(): pl.pallas_call(table_kernel, in_specs=[pl.BlockSpec(memory_space=pltpu.HB...  3.53 us
    pallas_call x1, Pallas kernels, spread_tiles(): pl.pallas_call(spread_kernel, in_specs=[pl.BlockSpec(memory_space=pltpu.H...  3.41 us
    ppermute x1, starting transfers between devices, body(): lax.ppermute(by_comp, 'col', [(source, (source + shift) % cols) for sourc...  3.06 us
  transfers between devices with their start and end apart: 7, of which 4 were waited for; matrix products, arithmetic and copies ran while one was open for 0% of the time, Pallas kernels for 53%

profile of v7, /device:TPU:0, one launch (start us, length us, event | category | flops | bytes accessed | tf_op | source)
XLA Modules:
  0.0 55.7 jit_solution(9585400809216532048)
XLA Ops:
  0.6 0.0 copy-start
  0.6 3.1 %collective-permute-start.2 = (bf16[3,64,2048]{2,1,0:T(8,128)(2,1)}, bf16[3,64,2048]{2,1,0:T(8,128)(2,1)S(1)}, u32[]{:S(2)}, u32[]{:S(2)}) collective-permute-start(bf16[3,64,2048]{2,1,0:T(8,128)(2,1)} %bitcast.20), channel_id=1, source_target_pairs={{0,1},{1,0},{2,3},{3,2},{4,5},{5,4},{6,7},{7,6},{8,9},{9,8},{10,11... | collective-permute-start | bytes 2359304 | tf_op jit(solution)/shard_map/ppermute | solution.py:250
  3.7 3.5 %node_table.1 = (bf16[2048,2,128]{2,1,0:T(2,128)(2,1)S(1)}, bf16[512,2,128]{2,1,0:T(2,128)(2,1)S(1)}, bf16[512,2,128]{2,1,0:T(2,128)(2,1)S(1)}) custom-call(bf16[3,64,2048]{2,1,0:T(8,128)(2,1)} %bitcast.21, s32[512]{0:T(512)} %up_ref.1, s32[512]{0:T(512)} %down_ref.1), custom_call_target="tpu_custom_call" | custom-call | tf_op jit(solution)/shard_map/node_table/pallas_call | solution.py:72
  7.2 0.1 collective-permute-start
  7.3 0.7 %collective-permute-start.1 = (bf16[512,2,128]{2,1,0:T(2,128)(2,1)S(1)}, bf16[512,2,128]{2,1,0:T(2,128)(2,1)S(1)}, u32[]{:S(2)}, u32[]{:S(2)}) collective-permute-start(bf16[512,2,128]{2,1,0:T(2,128)(2,1)S(1)} %get-tuple-element.9), channel_id=1, source_target_pairs={{2,4},{6,8},{10,12},{14,16},{18,20},{22,24},{26,28},{4,2},{8,6},{1... | collective-permute-start | bytes 786440 | tf_op jit(solution)/shard_map/ppermute | solution.py:21
  8.0 3.4 %spread_tiles.1.left_ref = bf16[2,256,48,128]{3,2,1,0:T(8,128)(2,1)S(1)} custom-call(bf16[144,2048]{1,0:T(8,128)(2,1)} %bitcast.22), custom_call_target="tpu_custom_call" | custom-call | flops 905969664 | bytes 6291456 | tf_op jit(solution)/shard_map/spread_tiles/pallas_call | solution.py:129
  11.4 0.0 copy-start.1
  11.4 0.0 collective-permute-done.near_in
  11.5 0.0 collective-permute-done.1.far_in
  11.5 0.0 copy-done
  11.5 22.5 %mass_rows.1 = (bf16[3,64,2048]{2,1,0:T(8,128)(2,1)}, bf16[3,64,2048]{2,1,0:T(8,128)(2,1)S(1)}) custom-call(s32[15,2048]{1,0:T(8,128)S(1)} %copy-done, bf16[2048,2,128]{2,1,0:T(2,128)(2,1)S(1)} %get-tuple-element.7.table_hbm, bf16[512,2,128]{2,1,0:T(2,128)(2,1)S(1)} %collective-permute-done.near_in, bf16[512,2,128]{2,1,0:T(2,128)(2,1)S(1)} %collective-permute-done.1.far_in, ...), custom_call_target="tpu_custom_call" | custom-call | flops 805306368 | bytes 6291456 | tf_op jit(solution)/shard_map/mass_rows/pallas_call | solution.py:206
  34.0 0.0 collective-permute-done.2
  34.0 0.4 convolution_bitcast_fusion
  34.4 0.0 copy-done.1
  34.4 0.4 broadcast_select_fusion.1
  34.7 0.1 pad_maximum_fusion
  34.8 5.3 %collective-permute-start.3 = (f32[64,128]{1,0:T(8,128)S(1)}, f32[64,128]{1,0:T(8,128)S(1)}, u32[]{:S(2)}, u32[]{:S(2)}) collective-permute-start(f32[64,128]{1,0:T(8,128)S(1)} %pad_maximum_fusion), channel_id=1, source_target_pairs={{0,2},{2,0},{4,6},{6,4},{8,10},{10,8},{12,14},{14,12},{16,18},{18,... | collective-permute-start | bytes 98312 | tf_op jit(solution)/shard_map/ppermute | solution.py:231
  40.1 0.9 %collective-permute-done.3 = f32[64,128]{1,0:T(8,128)S(1)} collective-permute-done((f32[64,128]{1,0:T(8,128)S(1)}, f32[64,128]{1,0:T(8,128)S(1)}, u32[]{:S(2)}, u32[]{:S(2)}) %collective-permute-start.3) | collective-permute-done | bytes 32800 | tf_op jit(solution)/shard_map/ppermute | solution.py:231
  41.0 0.1 fusion.4
  41.0 2.7 %collective-permute-start.4 = (f32[64,128]{1,0:T(8,128)S(1)}, f32[64,128]{1,0:T(8,128)S(1)}, u32[]{:S(2)}, u32[]{:S(2)}) collective-permute-start(f32[64,128]{1,0:T(8,128)S(1)} %fusion.4), channel_id=1, source_target_pairs={{0,4},{2,6},{4,0},{6,2},{8,12},{10,14},{12,8},{14,10},{16,20},{18,... | collective-permute-start | bytes 98312 | tf_op jit(solution)/shard_map/ppermute | solution.py:231
  43.8 1.9 %collective-permute-done.4 = f32[64,128]{1,0:T(8,128)S(1)} collective-permute-done((f32[64,128]{1,0:T(8,128)S(1)}, f32[64,128]{1,0:T(8,128)S(1)}, u32[]{:S(2)}, u32[]{:S(2)}) %collective-permute-start.4) | collective-permute-done | bytes 32800 | tf_op jit(solution)/shard_map/ppermute | solution.py:231
  45.7 2.5 %collective-permute-start.5 = (f32[64,128]{1,0:T(8,128)S(1)}, f32[64,128]{1,0:T(8,128)S(1)}, u32[]{:S(2)}, u32[]{:S(2)}) collective-permute-start(f32[64,128]{1,0:T(8,128)S(1)} %add.13), channel_id=1, source_target_pairs={{0,8},{2,10},{4,12},{6,14},{8,0},{10,2},{12,4},{14,6},{16,24},{18,... | collective-permute-start | bytes 98312 | tf_op jit(solution)/shard_map/ppermute | solution.py:231
  48.2 1.9 %collective-permute-done.5 = f32[64,128]{1,0:T(8,128)S(1)} collective-permute-done((f32[64,128]{1,0:T(8,128)S(1)}, f32[64,128]{1,0:T(8,128)S(1)}, u32[]{:S(2)}, u32[]{:S(2)}) %collective-permute-start.5) | collective-permute-done | bytes 32800 | tf_op jit(solution)/shard_map/ppermute | solution.py:231
  50.1 3.1 %collective-permute-start.6 = (f32[64,128]{1,0:T(8,128)S(1)}, f32[64,128]{1,0:T(8,128)S(1)}, u32[]{:S(2)}, u32[]{:S(2)}) collective-permute-start(f32[64,128]{1,0:T(8,128)S(1)} %add.14), channel_id=1, source_target_pairs={{0,16},{2,18},{4,20},{6,22},{8,24},{10,26},{12,28},{14,30},{16,0},... | collective-permute-start | bytes 98312 | tf_op jit(solution)/shard_map/ppermute | solution.py:231
  53.2 1.9 %collective-permute-done.6 = f32[64,128]{1,0:T(8,128)S(1)} collective-permute-done((f32[64,128]{1,0:T(8,128)S(1)}, f32[64,128]{1,0:T(8,128)S(1)}, u32[]{:S(2)}, u32[]{:S(2)}) %collective-permute-start.6) | collective-permute-done | bytes 32800 | tf_op jit(solution)/shard_map/ppermute | solution.py:231
  55.0 0.6 %multiply_bitcast_fusion = f32[128,64]{0,1:T(8,128)} fusion(f32[64,128]{1,0:T(8,128)S(1)} %add.14, f32[64,128]{1,0:T(8,128)S(1)} %collective-permute-done.6), kind=kLoop, calls=%fused_computation.3 | loop fusion | flops 16384 | bytes 98304 | tf_op jit(solution)/shard_map/transpose | solution.py:266
  (2 shorter events, 0.0 us)
Async XLA Ops:
  0.6 10.8 %copy-start = (s32[15,2048]{1,0:T(8,128)S(1)}, s32[15,2048]{1,0:T(8,128)}, u32[]{:S(2)}) copy-start(s32[15,2048]{1,0:T(8,128)} %slot_hbm.1) | copy-start | bytes 368644
  0.6 33.4 %collective-permute-start.2 = (bf16[3,64,2048]{2,1,0:T(8,128)(2,1)}, bf16[3,64,2048]{2,1,0:T(8,128)(2,1)S(1)}, u32[]{:S(2)}, u32[]{:S(2)}) collective-permute-start(bf16[3,64,2048]{2,1,0:T(8,128)(2,1)} %bitcast.20), channel_id=1, source_target_pairs={{0,1},{1,0},{2,3},{3,2},{4,5},{5,4},{6,7},{7,6},{8,9},{9,8},{10,11... | collective-permute-start | bytes 2359304 | tf_op jit(solution)/shard_map/ppermute | solution.py:250
  7.2 4.2 %collective-permute-start = (bf16[512,2,128]{2,1,0:T(2,128)(2,1)S(1)}, bf16[512,2,128]{2,1,0:T(2,128)(2,1)S(1)}, u32[]{:S(2)}, u32[]{:S(2)}) collective-permute-start(bf16[512,2,128]{2,1,0:T(2,128)(2,1)S(1)} %get-tuple-element.8), channel_id=1, source_target_pairs={{0,2},{4,6},{8,10},{12,14},{16,18},{20,22},{24,26},{28,30},{2,0},{... | collective-permute-start | bytes 786440 | tf_op jit(solution)/shard_map/ppermute | solution.py:21
  7.3 4.1 %collective-permute-start.1 = (bf16[512,2,128]{2,1,0:T(2,128)(2,1)S(1)}, bf16[512,2,128]{2,1,0:T(2,128)(2,1)S(1)}, u32[]{:S(2)}, u32[]{:S(2)}) collective-permute-start(bf16[512,2,128]{2,1,0:T(2,128)(2,1)S(1)} %get-tuple-element.9), channel_id=1, source_target_pairs={{2,4},{6,8},{10,12},{14,16},{18,20},{22,24},{26,28},{4,2},{8,6},{1... | collective-permute-start | bytes 786440 | tf_op jit(solution)/shard_map/ppermute | solution.py:21
  11.4 22.9 %copy-start.1 = (bf16[64,3,2048]{2,0,1:T(8,128)(2,1)S(1)}, bf16[64,3,2048]{2,0,1:T(8,128)(2,1)}, u32[]{:S(2)}) copy-start(bf16[64,3,2048]{2,0,1:T(8,128)(2,1)} %param.5) | copy-start | bytes 2359300
  34.8 6.1 %collective-permute-start.3 = (f32[64,128]{1,0:T(8,128)S(1)}, f32[64,128]{1,0:T(8,128)S(1)}, u32[]{:S(2)}, u32[]{:S(2)}) collective-permute-start(f32[64,128]{1,0:T(8,128)S(1)} %pad_maximum_fusion), channel_id=1, source_target_pairs={{0,2},{2,0},{4,6},{6,4},{8,10},{10,8},{12,14},{14,12},{16,18},{18,... | collective-permute-start | bytes 98312 | tf_op jit(solution)/shard_map/ppermute | solution.py:231
  41.0 4.6 %collective-permute-start.4 = (f32[64,128]{1,0:T(8,128)S(1)}, f32[64,128]{1,0:T(8,128)S(1)}, u32[]{:S(2)}, u32[]{:S(2)}) collective-permute-start(f32[64,128]{1,0:T(8,128)S(1)} %fusion.4), channel_id=1, source_target_pairs={{0,4},{2,6},{4,0},{6,2},{8,12},{10,14},{12,8},{14,10},{16,20},{18,... | collective-permute-start | bytes 98312 | tf_op jit(solution)/shard_map/ppermute | solution.py:231
  45.7 4.4 %collective-permute-start.5 = (f32[64,128]{1,0:T(8,128)S(1)}, f32[64,128]{1,0:T(8,128)S(1)}, u32[]{:S(2)}, u32[]{:S(2)}) collective-permute-start(f32[64,128]{1,0:T(8,128)S(1)} %add.13), channel_id=1, source_target_pairs={{0,8},{2,10},{4,12},{6,14},{8,0},{10,2},{12,4},{14,6},{16,24},{18,... | collective-permute-start | bytes 98312 | tf_op jit(solution)/shard_map/ppermute | solution.py:231
  50.1 5.0 %collective-permute-start.6 = (f32[64,128]{1,0:T(8,128)S(1)}, f32[64,128]{1,0:T(8,128)S(1)}, u32[]{:S(2)}, u32[]{:S(2)}) collective-permute-start(f32[64,128]{1,0:T(8,128)S(1)} %add.14), channel_id=1, source_target_pairs={{0,16},{2,18},{4,20},{6,22},{8,24},{10,26},{12,28},{14,30},{16,0},... | collective-permute-start | bytes 98312 | tf_op jit(solution)/shard_map/ppermute | solution.py:231

commit v8 on v7

--- a/solution.py
+++ b/solution.py
@@ -25,14 +25,15 @@
     return lax.dot_general(left, right, (((1,), (1,)), ((), ())), preferred_element_type=F32)
 
 
-def table_kernel(snap_hbm, up_ref, down_ref, table_ref, to_near_ref, to_far_ref, snap_ref, sem):
+def table_kernel(snap_hbm, up_hbm, down_hbm, table_ref, to_near_ref, to_far_ref, snap_ref, up_ref, down_ref, sem, list_sem):
     chunks = snap_ref.shape[0]
     width = snap_ref.shape[3]
     copies = [
         pltpu.make_async_copy(snap_hbm.at[:, :, pl.ds(chunk * width, width)], snap_ref.at[chunk], sem.at[chunk])
         for chunk in range(chunks)
     ]
-    for copy in copies:
+    lists = [pltpu.make_async_copy(up_hbm, up_ref, list_sem.at[0]), pltpu.make_async_copy(down_hbm, down_ref, list_sem.at[1])]
+    for copy in copies + lists:
         copy.start()
     row = lax.broadcasted_iota(jnp.int32, (2 * LANES, 2 * LANES), 0)
     col = lax.broadcasted_iota(jnp.int32, (2 * LANES, 2 * LANES), 1)
@@ -47,6 +48,9 @@
             rows = nt_dot(pick, jnp.concatenate([first, second], axis=1)).astype(BF16)
             table_ref[chunk * width + start : chunk * width + start + LANES] = rows.reshape(LANES, 2, LANES)
 
+    for copy in lists:
+        copy.wait()
+
     def fill(near_list, far_list):
         for out_ref, list_ref in ((to_near_ref, near_list), (to_far_ref, far_list)):
             for entry in range(out_ref.shape[0]):
@@ -66,19 +70,25 @@
 def node_table(snap, send_up, send_down):
     node_count = snap.shape[2]
     halo = send_up.shape[0]
-    smem = pl.BlockSpec(memory_space=pltpu.SMEM)
+    hbm = pl.BlockSpec(memory_space=pltpu.HBM)
     vmem = pl.BlockSpec(memory_space=pltpu.VMEM)
     chunks = 4 if node_count % (4 * LANES) == 0 else 1
     return pl.pallas_call(
         table_kernel,
-        in_specs=[pl.BlockSpec(memory_space=pltpu.HBM), smem, smem],
+        in_specs=[hbm] * 3,
         out_specs=[vmem] * 3,
         out_shape=[
             jax.ShapeDtypeStruct((node_count, 2, LANES), BF16),
             jax.ShapeDtypeStruct((halo, 2, LANES), BF16),
             jax.ShapeDtypeStruct((halo, 2, LANES), BF16),
         ],
-        scratch_shapes=[pltpu.VMEM((chunks, 3, HALF, node_count // chunks), BF16), pltpu.SemaphoreType.DMA((chunks,))],
+        scratch_shapes=[
+            pltpu.VMEM((chunks, 3, HALF, node_count // chunks), BF16),
+            pltpu.SMEM((halo,), jnp.int32),
+            pltpu.SMEM((halo,), jnp.int32),
+            pltpu.SemaphoreType.DMA((chunks,)),
+            pltpu.SemaphoreType.DMA((2,)),
+        ],
         compiler_params=pltpu.CompilerParams(vmem_limit_bytes=VMEM_BYTES),
         name="node_table",
     )(*(pltpu.with_memory_space_constraint(operand, pltpu.HBM) for operand in (snap, send_up, send_down)))

time: 55.9 us -> 55.2 us (0.987)
  Pallas kernels: 29.5 us -> 28.8 us
    pallas_call x1, Pallas kernels: 3.53 us -> 2.89 us  [node_table(): pl.pallas_call(table_kernel, in_specs=[hbm] * 3, out_specs=[vmem] * 3, ou...]
  transfers between devices with their start and end apart: 7 -> 7, of which waited for: 4 -> 4; matrix products, arithmetic and copies ran while one was open for 0% -> 0% of each run, Pallas kernels for 53% -> 52%
where the time goes in v8:
time: 55.2 us; the launch traced here: 55 us
  Pallas kernels  28.8 us (52%)
  starting transfers between devices  17.4 us (32%)
  waiting for transfers between devices  6.55 us (12%)
  other arithmetic  0.79 us (1%)
  between operations  0.75 us (1%)
  matrix products  0.7 us (1%)
    pallas_call x1, Pallas kernels, apply_mass(): pl.pallas_call(functools.partial(mass_kernel, parts), grid=(blocks // par...  22.5 us
    ppermute x4, starting transfers between devices, summed(): lax.ppermute(value, axis, [(source, source ^ step) for source in range(co...  13.6 us
    ppermute x4, waiting for transfers between devices, summed(): lax.ppermute(value, axis, [(source, source ^ step) for source in range(co...  6.54 us
    pallas_call x1, Pallas kernels, spread_tiles(): pl.pallas_call(spread_kernel, in_specs=[pl.BlockSpec(memory_space=pltpu.H...  3.41 us
    ppermute x1, starting transfers between devices, body(): lax.ppermute(by_comp, 'col', [(source, (source + shift) % cols) for sourc...  3.06 us
    pallas_call x1, Pallas kernels, node_table(): pl.pallas_call(table_kernel, in_specs=[hbm] * 3, out_specs=[vmem] * 3, ou...  2.89 us
  transfers between devices with their start and end apart: 7, of which 4 were waited for; matrix products, arithmetic and copies ran while one was open for 0% of the time, Pallas kernels for 52%

profile of v8, /device:TPU:0, one launch (start us, length us, event | category | flops | bytes accessed | tf_op | source)
XLA Modules:
  0.0 55.0 jit_solution(869620969496936669)
XLA Ops:
  0.6 0.0 copy-start
  0.6 3.1 %collective-permute-start.2 = (bf16[3,64,2048]{2,1,0:T(8,128)(2,1)}, bf16[3,64,2048]{2,1,0:T(8,128)(2,1)S(1)}, u32[]{:S(2)}, u32[]{:S(2)}) collective-permute-start(bf16[3,64,2048]{2,1,0:T(8,128)(2,1)} %bitcast.20), channel_id=1, source_target_pairs={{0,1},{1,0},{2,3},{3,2},{4,5},{5,4},{6,7},{7,6},{8,9},{9,8},{10,11... | collective-permute-start | bytes 2359304 | tf_op jit(solution)/shard_map/ppermute | solution.py:260
  3.7 2.9 %node_table.1 = (bf16[2048,2,128]{2,1,0:T(2,128)(2,1)S(1)}, bf16[512,2,128]{2,1,0:T(2,128)(2,1)S(1)}, bf16[512,2,128]{2,1,0:T(2,128)(2,1)S(1)}) custom-call(bf16[3,64,2048]{2,1,0:T(8,128)(2,1)} %bitcast.21, s32[512]{0:T(512)} %up_hbm.1, s32[512]{0:T(512)} %down_hbm.1), custom_call_target="tpu_custom_call" | custom-call | tf_op jit(solution)/shard_map/node_table/pallas_call | solution.py:76
  6.6 0.1 collective-permute-start
  6.7 0.7 %collective-permute-start.1 = (bf16[512,2,128]{2,1,0:T(2,128)(2,1)S(1)}, bf16[512,2,128]{2,1,0:T(2,128)(2,1)S(1)}, u32[]{:S(2)}, u32[]{:S(2)}) collective-permute-start(bf16[512,2,128]{2,1,0:T(2,128)(2,1)S(1)} %get-tuple-element.9), channel_id=1, source_target_pairs={{2,4},{6,8},{10,12},{14,16},{18,20},{22,24},{26,28},{4,2},{8,6},{1... | collective-permute-start | bytes 786440 | tf_op jit(solution)/shard_map/ppermute | solution.py:21
  7.4 3.4 %spread_tiles.1.left_ref = bf16[2,256,48,128]{3,2,1,0:T(8,128)(2,1)S(1)} custom-call(bf16[144,2048]{1,0:T(8,128)(2,1)} %bitcast.22), custom_call_target="tpu_custom_call" | custom-call | flops 905969664 | bytes 6291456 | tf_op jit(solution)/shard_map/spread_tiles/pallas_call | solution.py:139
  10.8 0.0 copy-start.1
  10.8 0.0 collective-permute-done.near_in
  10.8 0.0 collective-permute-done.1.far_in
  10.8 0.0 copy-done
  10.8 22.5 %mass_rows.1 = (bf16[3,64,2048]{2,1,0:T(8,128)(2,1)}, bf16[3,64,2048]{2,1,0:T(8,128)(2,1)S(1)}) custom-call(s32[15,2048]{1,0:T(8,128)S(1)} %copy-done, bf16[2048,2,128]{2,1,0:T(2,128)(2,1)S(1)} %get-tuple-element.7.table_hbm, bf16[512,2,128]{2,1,0:T(2,128)(2,1)S(1)} %collective-permute-done.near_in, bf16[512,2,128]{2,1,0:T(2,128)(2,1)S(1)} %collective-permute-done.1.far_in, ...), custom_call_target="tpu_custom_call" | custom-call | flops 805306368 | bytes 6291456 | tf_op jit(solution)/shard_map/mass_rows/pallas_call | solution.py:216
  33.4 0.0 collective-permute-done.2
  33.4 0.4 convolution_bitcast_fusion
  33.7 0.0 copy-done.1
  33.7 0.4 broadcast_select_fusion.1
  34.1 0.1 pad_maximum_fusion
  34.2 5.3 %collective-permute-start.3 = (f32[64,128]{1,0:T(8,128)S(1)}, f32[64,128]{1,0:T(8,128)S(1)}, u32[]{:S(2)}, u32[]{:S(2)}) collective-permute-start(f32[64,128]{1,0:T(8,128)S(1)} %pad_maximum_fusion), channel_id=1, source_target_pairs={{0,2},{2,0},{4,6},{6,4},{8,10},{10,8},{12,14},{14,12},{16,18},{18,... | collective-permute-start | bytes 98312 | tf_op jit(solution)/shard_map/ppermute | solution.py:241
  39.5 0.9 %collective-permute-done.3 = f32[64,128]{1,0:T(8,128)S(1)} collective-permute-done((f32[64,128]{1,0:T(8,128)S(1)}, f32[64,128]{1,0:T(8,128)S(1)}, u32[]{:S(2)}, u32[]{:S(2)}) %collective-permute-start.3) | collective-permute-done | bytes 32800 | tf_op jit(solution)/shard_map/ppermute | solution.py:241
  40.3 0.1 fusion.4
  40.4 2.7 %collective-permute-start.4 = (f32[64,128]{1,0:T(8,128)S(1)}, f32[64,128]{1,0:T(8,128)S(1)}, u32[]{:S(2)}, u32[]{:S(2)}) collective-permute-start(f32[64,128]{1,0:T(8,128)S(1)} %fusion.4), channel_id=1, source_target_pairs={{0,4},{2,6},{4,0},{6,2},{8,12},{10,14},{12,8},{14,10},{16,20},{18,... | collective-permute-start | bytes 98312 | tf_op jit(solution)/shard_map/ppermute | solution.py:241
  43.2 1.9 %collective-permute-done.4 = f32[64,128]{1,0:T(8,128)S(1)} collective-permute-done((f32[64,128]{1,0:T(8,128)S(1)}, f32[64,128]{1,0:T(8,128)S(1)}, u32[]{:S(2)}, u32[]{:S(2)}) %collective-permute-start.4) | collective-permute-done | bytes 32800 | tf_op jit(solution)/shard_map/ppermute | solution.py:241
  45.1 2.5 %collective-permute-start.5 = (f32[64,128]{1,0:T(8,128)S(1)}, f32[64,128]{1,0:T(8,128)S(1)}, u32[]{:S(2)}, u32[]{:S(2)}) collective-permute-start(f32[64,128]{1,0:T(8,128)S(1)} %add.13), channel_id=1, source_target_pairs={{0,8},{2,10},{4,12},{6,14},{8,0},{10,2},{12,4},{14,6},{16,24},{18,... | collective-permute-start | bytes 98312 | tf_op jit(solution)/shard_map/ppermute | solution.py:241
  47.6 1.9 %collective-permute-done.5 = f32[64,128]{1,0:T(8,128)S(1)} collective-permute-done((f32[64,128]{1,0:T(8,128)S(1)}, f32[64,128]{1,0:T(8,128)S(1)}, u32[]{:S(2)}, u32[]{:S(2)}) %collective-permute-start.5) | collective-permute-done | bytes 32800 | tf_op jit(solution)/shard_map/ppermute | solution.py:241
  49.5 3.1 %collective-permute-start.6 = (f32[64,128]{1,0:T(8,128)S(1)}, f32[64,128]{1,0:T(8,128)S(1)}, u32[]{:S(2)}, u32[]{:S(2)}) collective-permute-start(f32[64,128]{1,0:T(8,128)S(1)} %add.14), channel_id=1, source_target_pairs={{0,16},{2,18},{4,20},{6,22},{8,24},{10,26},{12,28},{14,30},{16,0},... | collective-permute-start | bytes 98312 | tf_op jit(solution)/shard_map/ppermute | solution.py:241
  52.5 1.9 %collective-permute-done.6 = f32[64,128]{1,0:T(8,128)S(1)} collective-permute-done((f32[64,128]{1,0:T(8,128)S(1)}, f32[64,128]{1,0:T(8,128)S(1)}, u32[]{:S(2)}, u32[]{:S(2)}) %collective-permute-start.6) | collective-permute-done | bytes 32800 | tf_op jit(solution)/shard_map/ppermute | solution.py:241
  54.4 0.6 %multiply_bitcast_fusion = f32[128,64]{0,1:T(8,128)} fusion(f32[64,128]{1,0:T(8,128)S(1)} %add.14, f32[64,128]{1,0:T(8,128)S(1)} %collective-permute-done.6), kind=kLoop, calls=%fused_computation.3 | loop fusion | flops 16384 | bytes 98304 | tf_op jit(solution)/shard_map/transpose | solution.py:276
  (2 shorter events, 0.0 us)
Async XLA Ops:
  0.6 10.2 %copy-start = (s32[15,2048]{1,0:T(8,128)S(1)}, s32[15,2048]{1,0:T(8,128)}, u32[]{:S(2)}) copy-start(s32[15,2048]{1,0:T(8,128)} %slot_hbm.1) | copy-start | bytes 368644
  0.6 32.7 %collective-permute-start.2 = (bf16[3,64,2048]{2,1,0:T(8,128)(2,1)}, bf16[3,64,2048]{2,1,0:T(8,128)(2,1)S(1)}, u32[]{:S(2)}, u32[]{:S(2)}) collective-permute-start(bf16[3,64,2048]{2,1,0:T(8,128)(2,1)} %bitcast.20), channel_id=1, source_target_pairs={{0,1},{1,0},{2,3},{3,2},{4,5},{5,4},{6,7},{7,6},{8,9},{9,8},{10,11... | collective-permute-start | bytes 2359304 | tf_op jit(solution)/shard_map/ppermute | solution.py:260
  6.6 4.2 %collective-permute-start = (bf16[512,2,128]{2,1,0:T(2,128)(2,1)S(1)}, bf16[512,2,128]{2,1,0:T(2,128)(2,1)S(1)}, u32[]{:S(2)}, u32[]{:S(2)}) collective-permute-start(bf16[512,2,128]{2,1,0:T(2,128)(2,1)S(1)} %get-tuple-element.8), channel_id=1, source_target_pairs={{0,2},{4,6},{8,10},{12,14},{16,18},{20,22},{24,26},{28,30},{2,0},{... | collective-permute-start | bytes 786440 | tf_op jit(solution)/shard_map/ppermute | solution.py:21
  6.7 4.1 %collective-permute-start.1 = (bf16[512,2,128]{2,1,0:T(2,128)(2,1)S(1)}, bf16[512,2,128]{2,1,0:T(2,128)(2,1)S(1)}, u32[]{:S(2)}, u32[]{:S(2)}) collective-permute-start(bf16[512,2,128]{2,1,0:T(2,128)(2,1)S(1)} %get-tuple-element.9), channel_id=1, source_target_pairs={{2,4},{6,8},{10,12},{14,16},{18,20},{22,24},{26,28},{4,2},{8,6},{1... | collective-permute-start | bytes 786440 | tf_op jit(solution)/shard_map/ppermute | solution.py:21
  10.8 23.0 %copy-start.1 = (bf16[64,3,2048]{2,0,1:T(8,128)(2,1)S(1)}, bf16[64,3,2048]{2,0,1:T(8,128)(2,1)}, u32[]{:S(2)}) copy-start(bf16[64,3,2048]{2,0,1:T(8,128)(2,1)} %param.5) | copy-start | bytes 2359300
  34.2 6.2 %collective-permute-start.3 = (f32[64,128]{1,0:T(8,128)S(1)}, f32[64,128]{1,0:T(8,128)S(1)}, u32[]{:S(2)}, u32[]{:S(2)}) collective-permute-start(f32[64,128]{1,0:T(8,128)S(1)} %pad_maximum_fusion), channel_id=1, source_target_pairs={{0,2},{2,0},{4,6},{6,4},{8,10},{10,8},{12,14},{14,12},{16,18},{18,... | collective-permute-start | bytes 98312 | tf_op jit(solution)/shard_map/ppermute | solution.py:241
  40.4 4.6 %collective-permute-start.4 = (f32[64,128]{1,0:T(8,128)S(1)}, f32[64,128]{1,0:T(8,128)S(1)}, u32[]{:S(2)}, u32[]{:S(2)}) collective-permute-start(f32[64,128]{1,0:T(8,128)S(1)} %fusion.4), channel_id=1, source_target_pairs={{0,4},{2,6},{4,0},{6,2},{8,12},{10,14},{12,8},{14,10},{16,20},{18,... | collective-permute-start | bytes 98312 | tf_op jit(solution)/shard_map/ppermute | solution.py:241
  45.1 4.4 %collective-permute-start.5 = (f32[64,128]{1,0:T(8,128)S(1)}, f32[64,128]{1,0:T(8,128)S(1)}, u32[]{:S(2)}, u32[]{:S(2)}) collective-permute-start(f32[64,128]{1,0:T(8,128)S(1)} %add.13), channel_id=1, source_target_pairs={{0,8},{2,10},{4,12},{6,14},{8,0},{10,2},{12,4},{14,6},{16,24},{18,... | collective-permute-start | bytes 98312 | tf_op jit(solution)/shard_map/ppermute | solution.py:241
  49.5 5.0 %collective-permute-start.6 = (f32[64,128]{1,0:T(8,128)S(1)}, f32[64,128]{1,0:T(8,128)S(1)}, u32[]{:S(2)}, u32[]{:S(2)}) collective-permute-start(f32[64,128]{1,0:T(8,128)S(1)} %add.14), channel_id=1, source_target_pairs={{0,16},{2,18},{4,20},{6,22},{8,24},{10,26},{12,28},{14,30},{16,0},... | collective-permute-start | bytes 98312 | tf_op jit(solution)/shard_map/ppermute | solution.py:241
